TPU v7x, 512 devices: a whole 4x4x16 slice. The times are simulated.
512 devices in a mesh: db: 64 (over z, x), seq: 8 (over y, core).
Axes of the slice: x: 4, y: 4, z: 16, core: 2. Of those that a mesh axis runs over, the one named last changes fastest.
Arguments:
- reader: bfloat16 [64, 1024, 2048], P('db', 'seq'), may hold values from -6 to 6
- reader_gain: float32 [2048], replicated, may hold values from 0.1 to 1.9
- database: bfloat16 [8192, 2, 896], P('db')
- encoder_gain: float32 [896], replicated, may hold values from 0.1 to 1.9
- w_expand: bfloat16 [896, 1792], P('db', 'seq'), may hold values from -0.1875 to 0.1875
- w_reduce: bfloat16 [1792, 896], P('seq', 'db'), may hold values from -0.125 to 0.125
- w_query: bfloat16 [2048, 2048], P('db', 'seq'), may hold values from -0.125 to 0.125
- w_key: bfloat16 [896, 2048], P('db', 'seq'), may hold values from -0.1875 to 0.1875
- w_value: bfloat16 [896, 2048], P('db', 'seq'), may hold values from -0.1875 to 0.1875
- w_output: bfloat16 [2048, 2048], P('db', 'seq'), may hold values from -0.125 to 0.125
- neighbour_ids: int32 [64, 8, 4], replicated, may hold values from 0 to 127
- lengths: int32 [64, 8, 4], P('db'), may hold values from 1 to 128, 320 in all within a row
- owners: int32 [64, 8, 4], P('db'), may hold values from 0 to 63
Outputs:
- updated: bfloat16 [64, 1024, 2048], P('db', None, 'seq')
Inputs may be any that keep to these rules, and one draw needn't show every extreme that they name: For every sequence b and every q, the lengths[b, q, :] of its 4 neighbours sum to exactly 320, and the longest of them is 128.
All inputs are finite; a program needn't handle non-finite values.
Results may differ from a plain program's by a relative error of at most 0.0065.
The roundings to bfloat16 on the way count: a program that leaves them out, or rounds other values in their place, can miss the bound.
Values may be sent and summed in bfloat16 or wider, within the bound.
No kernel may reach another device: no remote copies, remote signals or barrier semaphores. Data moves between devices by JAX's collectives and lax.ppermute only.
A program may use at most 64 MiB of HBM per device.

v0:
```python
import jax
import jax.numpy as jnp
from jax import lax
from jax.sharding import PartitionSpec as P

HD = 128
SPAN = 64
KNN = 2


epsilon = 1e-06


def rms_scale(values, scales):
    widened = values.astype(jnp.float32)
    mean_square = jnp.mean(widened * widened, axis=-1, keepdims=True)
    return widened * lax.rsqrt(mean_square + epsilon) * scales


def body(
    reader,
    reader_gain,
    database,
    encoder_gain,
    w_expand,
    w_reduce,
    w_query,
    w_key,
    w_value,
    w_output,
    neighbour_ids,
    lengths,
    owners,
):
    shards = lax.axis_size("db")
    seq_index = lax.axis_index("seq")
    entries, stripe, features = database.shape
    query_part = lax.all_gather(w_query, "db", axis=0, tiled=True)
    reader_output_part = lax.all_gather(w_output, "db", axis=0, tiled=True)
    rows = lax.all_gather(reader[0], "seq", axis=0, tiled=True)
    normed_tokens = rms_scale(rows, reader_gain).astype(jnp.bfloat16)
    queries = jnp.dot(normed_tokens, query_part, preferred_element_type=jnp.float32).astype(
        jnp.bfloat16
    )
    rows, queries, output_part = (rows, queries, reader_output_part)
    expand_part = lax.all_gather(w_expand, "db", axis=0, tiled=True)
    reduce_part = lax.all_gather(w_reduce, "db", axis=1, tiled=True)
    key_part = lax.all_gather(w_key, "db", axis=0, tiled=True)
    value_part = lax.all_gather(w_value, "db", axis=0, tiled=True)
    stored = database.reshape(entries * stripe, features)
    normed_rows = rms_scale(stored, encoder_gain).astype(jnp.bfloat16)
    hidden = jax.nn.gelu(
        jnp.dot(normed_rows, expand_part, preferred_element_type=jnp.float32), approximate=False
    ).astype(jnp.bfloat16)
    partial_sum = jnp.dot(hidden, reduce_part, preferred_element_type=jnp.float32)
    total = lax.psum(partial_sum, "seq")
    encoded = (stored.astype(jnp.float32) + total).astype(jnp.bfloat16)
    w_pairs = jnp.concatenate([key_part, value_part], axis=1)
    table = jnp.dot(encoded, w_pairs, preferred_element_type=jnp.float32).astype(jnp.bfloat16)
    table = table.reshape(entries, stripe, w_pairs.shape[1])
    requests = neighbour_ids.reshape(shards, -1)
    outgoing = table[requests]
    arrived = lax.all_to_all(outgoing, "db", split_axis=0, concat_axis=0, tiled=True)
    seq_len = rows.shape[0]
    per_seq = neighbour_ids.shape[1] * neighbour_ids.shape[2]
    width = arrived.shape[-1]
    local_heads = width // (2 * HD)
    positions = jnp.arange(stripe * shards, dtype=jnp.int32)
    owner_flat = owners[0].reshape(-1)
    length_flat = lengths[0].reshape(-1)
    source = (owner_flat[:, None] + positions[None, :] // stripe) % shards
    neighbour_index = jnp.arange(per_seq, dtype=jnp.int32)[:, None]
    flat_index = (source * per_seq + neighbour_index) * stripe + (positions % stripe)[None, :]
    key_value = arrived.reshape(-1, width)[flat_index]
    live = positions[None, :] < length_flat[:, None]
    spans = per_seq // KNN
    window = KNN * positions.shape[0]
    span_pairs = key_value.reshape(spans, window, width)
    span_live = live.reshape(spans, window)
    prior_pairs = jnp.concatenate(
        [jnp.zeros((1, window, width), jnp.bfloat16), span_pairs[:-1]], axis=0
    )
    prior_live = jnp.concatenate([jnp.zeros((1, window), bool), span_live[:-1]], axis=0)
    query_spans = queries.reshape(spans, SPAN, local_heads, HD)
    key_heads = prior_pairs[:, :, : local_heads * HD].reshape(spans, window, local_heads, HD)
    value_heads = prior_pairs[:, :, local_heads * HD :].reshape(spans, window, local_heads, HD)
    scores = jnp.einsum(
        "cqhd,ckhd->chqk", query_spans, key_heads, preferred_element_type=jnp.float32
    ) * HD ** (-0.5)
    masked = jnp.where(prior_live[:, None, None, :], scores, -jnp.inf)
    largest = jnp.max(masked, axis=-1, keepdims=True)
    largest = jnp.where(jnp.isfinite(largest), largest, 0.0)
    powers = jnp.exp(masked - largest)
    totals = jnp.sum(powers, axis=-1, keepdims=True)
    weights = (powers / jnp.where(totals > 0, totals, 1.0)).astype(jnp.bfloat16)
    attended = jnp.einsum(
        "chqk,ckhd->cqhd", weights, value_heads, preferred_element_type=jnp.float32
    )
    attended = attended.reshape(seq_len, local_heads * HD).astype(jnp.bfloat16)
    model_cols = output_part.shape[1]
    update = jnp.dot(
        lax.all_gather(attended, "seq", axis=1, tiled=True),
        output_part,
        preferred_element_type=jnp.float32,
    )
    residual = lax.dynamic_slice_in_dim(rows, seq_index * model_cols, model_cols, 1)
    result = (residual.astype(jnp.float32) + update).astype(jnp.bfloat16)
    return result[None]


def solution(mesh):
    in_specs = (
        P("db", "seq", None),
        P(),
        P("db", None, None),
        P(),
        P("db", "seq"),
        P("seq", "db"),
        P("db", "seq"),
        P("db", "seq"),
        P("db", "seq"),
        P("db", "seq"),
        P(),
        P("db", None, None),
        P("db", None, None),
    )
    out_specs = P("db", None, "seq")
    return jax.shard_map(body, mesh=mesh, in_specs=in_specs, out_specs=out_specs, check_vma=False)
```

profile of v0, /device:TPU:1, one launch (start us, length us, event | category | flops | bytes accessed | tf_op | source)
XLA Modules:
  0.0 866.0 jit_solution(5057858195962454341)
XLA Ops:
  6.5 0.0 all-reduce.4.cloned.1.call-start
  6.5 1.2 reshape.275
  7.7 0.0 copy-start.7
  7.7 1.6 multiply_reduce_fusion
  9.3 81.7 %all-gather.2 = bf16[64,14,224]{2,1,0:T(8,128)(2,1)S(1)} all-gather(bf16[1,14,224]{2,1,0:T(8,128)(2,1)} %bitcast.53), channel_id=1, replica_groups=mesh['db'=64,'seq'=8] {'db'}, dimensions={0}, use_global_device_ids=true | all-gather | bytes 407680 | tf_op jit(solution)/shard_map/all_gather | solution.py:47
  90.9 0.2 reshape.303
  91.2 0.0 copy-done.1
  91.2 73.5 %all-gather.1 = bf16[64,14,224]{2,1,0:T(8,128)(2,1)S(1)} all-gather(bf16[1,14,224]{2,1,0:T(8,128)(2,1)S(1)} %bitcast.54), channel_id=1, replica_groups=mesh['db'=64,'seq'=8] {'db'}, dimensions={0}, use_global_device_ids=true | all-gather | bytes 407680 | tf_op jit(solution)/shard_map/all_gather | solution.py:46
  164.7 0.2 reshape.301
  165.0 0.1 rsqrt.20
  165.1 0.0 copy-done.7
  165.1 0.0 copy-start.2
  165.1 0.0 copy-start.3
  165.1 2.4 fusion.38
  167.5 0.0 all-reduce.4.cloned.1.call-update
  167.5 0.0 copy-done.2
  167.5 73.3 %all-gather.4 = bf16[64,14,256]{2,1,0:T(8,128)(2,1)S(1)} all-gather(bf16[1,14,256]{2,1,0:T(8,128)(2,1)S(1)} %bitcast.55), channel_id=1, replica_groups=mesh['db'=64,'seq'=8] {'db'}, dimensions={0}, use_global_device_ids=true | all-gather | bytes 465920 | tf_op jit(solution)/shard_map/all_gather | solution.py:49
  240.8 0.0 copy-done.3
  240.8 75.0 %all-gather.3 = bf16[64,14,256]{2,1,0:T(8,128)(2,1)S(1)} all-gather(bf16[1,14,256]{2,1,0:T(8,128)(2,1)S(1)} %bitcast.56), channel_id=1, replica_groups=mesh['db'=64,'seq'=8] {'db'}, dimensions={0}, use_global_device_ids=true | all-gather | bytes 465920 | tf_op jit(solution)/shard_map/all_gather | solution.py:48
  315.8 0.1 reshape.307
  316.0 0.1 reshape.305
  316.1 0.0 copy-done
  316.1 0.1 copy.27
  316.2 0.1 reshape.278
  316.3 0.0 all-reduce.4.cloned.1.call-done
  316.3 1.6 convolution_convert_fusion.1
  317.9 0.1 reshape.269
  318.1 21.4 %gather_fusion = bf16[2048,2,512]{2,1,0:T(2,128)(2,1)} fusion(bf16[128,2,512]{2,1,0:T(2,128)(2,1)S(1)} %reshape.269, s32[2048]{0:T(1024)S(1)} %broadcast_clamp_fusion), kind=kCustom, calls=%fused_computation | custom fusion | bytes 8396800 | tf_op jit(solution)/shard_map/gather | solution.py:62
  339.5 10.5 %all-to-all-start = ((bf16[64,32,2,512]{3,2,1,0:T(2,128)(2,1)}), bf16[64,32,2,512]{3,2,1,0:T(2,128)(2,1)}, u32[]{:S(2)}, u32[]{:S(2)}) async-start(bf16[64,32,2,512]{3,2,1,0:T(2,128)(2,1)} %bitcast.46), calls=%async_computation | async-start | bytes 8388608 | tf_op jit(solution)/shard_map/all_to_all | solution.py:63
  349.9 0.0 all-gather.16.cloned.1.call-start
  350.0 0.7 all-gather.16.cloned.1.call-update
  350.7 0.0 all-gather.10.cloned.1.call-start
  350.7 0.7 all-gather.10.cloned.1.call-update
  351.4 0.0 all-gather.14.cloned.1.call-start
  351.5 0.5 all-gather.14.cloned.1.call-update
  352.0 0.2 all-gather.12.cloned.1.call-start
  352.2 0.0 copy-done.4
  352.2 0.1 copy.30
  352.3 0.1 add.149
  352.4 0.1 copy.32
  352.5 0.1 lt.61
  352.6 0.1 iota_compare_fusion
  352.7 0.1 fusion.75
  352.8 0.0 copy-start.6
  352.8 173.5 %all-gather.16.cloned.1.call-done = bf16[1,1024,2048]{2,1,0:T(8,128)(2,1)} async-done(((bf16[1,128,2048]{2,1,0:T(8,128)(2,1)}), bf16[1,1024,2048]{2,1,0:T(8,128)(2,1)}) %all-gather.16.cloned.1.call-update) | async-done | bytes 4194320 | tf_op jit(solution)/shard_map/all_gather | solution.py:40
  526.3 3.1 fusion
  529.4 134.8 %all-gather.10.cloned.1.call-done = bf16[2048,256]{1,0:T(8,128)(2,1)} async-done(((bf16[32,256]{1,0:T(8,128)(2,1)}), bf16[2048,256]{1,0:T(8,128)(2,1)}) %all-gather.10.cloned.1.call-update) | async-done | bytes 1048592 | tf_op jit(solution)/shard_map/all_gather | solution.py:38
  664.1 3.8 fusion.11
  667.9 0.1 reshape.273
  668.1 0.0 all-to-all-done
  668.1 7.2 reshape.271
  675.3 20.1 %gather_fusion.1 = bf16[4096,512]{1,0:T(8,128)(2,1)} fusion(bf16[4096,512]{1,0:T(8,128)(2,1)} %reshape.271, s32[4096]{0:T(1024)S(1)} %fusion.75), kind=kCustom, calls=%fused_computation.1 | custom fusion | bytes 8404992 | tf_op jit(solution)/shard_map/gather | solution.py:74
  695.4 4.2 slice.29
  699.6 6.3 copy.31
  705.9 2.6 pad_slice_fusion
  708.5 0.6 fusion.8
  709.1 0.9 fusion.9
  710.1 1.0 fusion.14
  711.1 0.5 copy.36
  711.6 0.9 copy.45
  712.5 0.0 all-gather.12.cloned.1.call-update
  712.5 90.4 %all-gather.14.cloned.1.call-done = bf16[2048,256]{1,0:T(8,128)(2,1)} async-done(((bf16[32,256]{1,0:T(8,128)(2,1)}), bf16[2048,256]{1,0:T(8,128)(2,1)}) %all-gather.14.cloned.1.call-update) | async-done | bytes 1048592 | tf_op jit(solution)/shard_map/all_gather | solution.py:39
  802.9 51.9 %all-gather.12.cloned.1.call-done = bf16[1024,2048]{1,0:T(8,128)(2,1)} async-done(((bf16[1024,256]{1,0:T(8,128)(2,1)}), bf16[1024,2048]{1,0:T(8,128)(2,1)}) %all-gather.12.cloned.1.call-update) | async-done | bytes 4194320 | tf_op jit(solution)/shard_map/all_gather | solution.py:102
  854.8 4.6 fusion.15
  (15 shorter events, 0.1 us)
Async XLA Ops:
  6.5 84.7 %copy-start.1 = (bf16[14,224]{1,0:T(8,128)(2,1)S(1)}, bf16[14,224]{1,0:T(8,128)(2,1)}, u32[]{:S(2)}) copy-start(bf16[14,224]{1,0:T(8,128)(2,1)} %param.17) | copy-start | bytes 18820
  6.5 309.8 %all-reduce.4.cloned.1.call-start = ((), (), s32[]{:S(2)}) async-start(), calls=%async_computation.1 | async-start | bytes 1835008 | tf_op jit(solution)/shard_map/psum | solution.py:56
  7.7 157.4 %copy-start.7 = (f32[896]{0:T(1024)S(1)}, f32[896]{0:T(1024)}, u32[]{:S(2)}) copy-start(f32[896]{0:T(1024)} %param.16) | copy-start | bytes 10756
  165.1 2.4 copy-start.2
  165.1 75.7 %copy-start.3 = (bf16[14,256]{1,0:T(8,128)(2,1)S(1)}, bf16[14,256]{1,0:T(8,128)(2,1)}, u32[]{:S(2)}) copy-start(bf16[14,256]{1,0:T(8,128)(2,1)} %param.20) | copy-start | bytes 21508
  167.5 148.6 %copy-start = (s32[64,8,4]{0,2,1:T(4,128)S(1)}, s32[64,8,4]{0,2,1:T(4,128)}, u32[]{:S(2)}) copy-start(s32[64,8,4]{0,2,1:T(4,128)} %param.23) | copy-start | bytes 24580
  339.5 12.8 %copy-start.4 = (s32[1,8,4]{1,2,0:T(4,128)S(1)}, s32[1,8,4]{1,2,0:T(4,128)}, u32[]{:S(2)}) copy-start(s32[1,8,4]{1,2,0:T(4,128)} %param.25) | copy-start | bytes 388
  339.5 12.9 %copy-start.5 = (s32[1,8,4]{1,2,0:T(4,128)S(1)}, s32[1,8,4]{1,2,0:T(4,128)}, u32[]{:S(2)}) copy-start(s32[1,8,4]{1,2,0:T(4,128)} %param.24) | copy-start | bytes 388
  339.5 328.6 %all-to-all-start = ((bf16[64,32,2,512]{3,2,1,0:T(2,128)(2,1)}), bf16[64,32,2,512]{3,2,1,0:T(2,128)(2,1)}, u32[]{:S(2)}, u32[]{:S(2)}) async-start(bf16[64,32,2,512]{3,2,1,0:T(2,128)(2,1)} %bitcast.46), calls=%async_computation | async-start | bytes 8388608 | tf_op jit(solution)/shard_map/all_to_all | solution.py:63
  349.9 176.3 %all-gather.16.cloned.1.call-start = ((), (), s32[]{:S(2)}) async-start(), calls=%async_computation.5 | async-start | bytes 4718592 | tf_op jit(solution)/shard_map/all_gather | solution.py:40
  350.7 313.4 %all-gather.10.cloned.1.call-start = ((), (), s32[]{:S(2)}) async-start(), calls=%async_computation.2 | async-start | bytes 1064960 | tf_op jit(solution)/shard_map/all_gather | solution.py:38
  351.4 451.5 %all-gather.14.cloned.1.call-start = ((), (), s32[]{:S(2)}) async-start(), calls=%async_computation.4 | async-start | bytes 1064960 | tf_op jit(solution)/shard_map/all_gather | solution.py:39
  352.0 502.8 %all-gather.12.cloned.1.call-start = ((), (), s32[]{:S(2)}) async-start(), calls=%async_computation.3 | async-start | bytes 4718592 | tf_op jit(solution)/shard_map/all_gather | solution.py:102
  352.8 311.3 %copy-start.6 = (f32[2048]{0:T(1024)S(1)}, f32[2048]{0:T(1024)}, u32[]{:S(2)}) copy-start(f32[2048]{0:T(1024)} %param.14) | copy-start | bytes 24580
Sparse Core Ops, SparseCore 0:
  167.7 123.3 all-reduce.3
  352.9 173.3 all-gather.15
  529.2 134.8 all-gather.9
  666.9 135.9 all-gather.13
  804.9 49.8 all-gather.11
where the time goes:
time: 867 us; the launch traced here: 866 us
  waiting for transfers between devices  452 us (52%)
  blocking collectives  303 us (35%)
  local copies, waits for them, and re-layouts  66 us (8%)
  matrix products  14 us (2%)
  between operations  13.4 us (2%)
  starting transfers between devices  10.8 us (1%)
    all_gather x1, waiting for transfers between devices, body(): rows = lax.all_gather(reader[0], 'seq', axis=0, tiled=True)  173 us
    all_gather x1, waiting for transfers between devices, body(): query_part = lax.all_gather(w_query, 'db', axis=0, tiled=True)  135 us
    all_gather x1, waiting for transfers between devices, body(): reader_output_part = lax.all_gather(w_output, 'db', axis=0, tiled=True)  90.4 us
    all_gather x1, blocking collectives, body(): reduce_part = lax.all_gather(w_reduce, 'db', axis=1, tiled=True)  81.7 us
    all_gather x1, blocking collectives, body(): key_part = lax.all_gather(w_key, 'db', axis=0, tiled=True)  75 us
    all_gather x1, blocking collectives, body(): expand_part = lax.all_gather(w_expand, 'db', axis=0, tiled=True)  73.5 us
    all_gather x1, blocking collectives, body(): value_part = lax.all_gather(w_value, 'db', axis=0, tiled=True)  73.3 us
    all_gather x1, waiting for transfers between devices, body(): lax.all_gather(attended, 'seq', axis=1, tiled=True)  51.9 us
  transfers between devices with their start and end apart: 6, of which 4 were waited for; matrix products, arithmetic and copies ran while one was open for 6% of the time, Pallas kernels for 0%

commit v1 on v0

v1 whole, which is shorter than its diff:
```python
import jax
import jax.numpy as jnp
from jax import lax
from jax.sharding import Mesh, PartitionSpec as P

HD = 128
SPAN = 64
KNN = 2
NZ = 16
NX = 4
NY = 4
NC = 2
PACK = 320
DB = ("z", "x")
SEQ = ("y", "c")


epsilon = 1e-06


def rms_scale(values, scales):
    widened = values.astype(jnp.float32)
    mean_square = jnp.mean(widened * widened, axis=-1, keepdims=True)
    return widened * lax.rsqrt(mean_square + epsilon) * scales


def dot(a, b):
    return jnp.dot(a, b, preferred_element_type=jnp.float32)


def spread(part, axis, size):
    copies = jnp.broadcast_to(part[None], (size,) + part.shape)
    return lax.all_to_all(copies, axis, split_axis=0, concat_axis=0, tiled=True)


def ring(step):
    return [(i, (i + step) % NY) for i in range(NY)]


def gather_seq(part):
    half = part.shape[0] // 2
    left = lax.ppermute(part, "y", ring(-1))
    right = lax.ppermute(part, "y", ring(1))
    far_left = lax.ppermute(left[half:], "y", ring(-1))
    far_right = lax.ppermute(right[:half], "y", ring(1))
    far = jnp.concatenate([far_right, far_left], axis=0)
    mine = jnp.stack([part, left, far, right])
    other = lax.ppermute(mine, "c", [(0, 1), (1, 0)])
    return mine, other


def to_natural(mine, other):
    y = lax.axis_index("y")
    c = lax.axis_index("c")
    both = jnp.stack([mine, other], axis=1)
    both = jnp.where(c == 1, both[:, ::-1], both)
    both = jnp.where(y % 2 == 1, jnp.roll(both, 1, axis=0), both)
    both = jnp.where(y // 2 == 1, jnp.roll(both, 2, axis=0), both)
    return both.reshape((NY * NC,) + mine.shape[1:])


def to_relative(blocks):
    y = lax.axis_index("y")
    c = lax.axis_index("c")
    both = blocks.reshape((NY, NC) + blocks.shape[1:])
    both = jnp.where(c == 1, both[:, ::-1], both)
    both = jnp.where(y % 2 == 1, jnp.roll(both, -1, axis=0), both)
    both = jnp.where(y // 2 == 1, jnp.roll(both, -2, axis=0), both)
    return jnp.swapaxes(both, 0, 1).reshape(blocks.shape)


def pad_rows(a, rows):
    return jnp.pad(a, ((0, rows - a.shape[0]), (0, 0)))


def body(
    reader,
    reader_gain,
    database,
    encoder_gain,
    w_expand,
    w_reduce,
    w_query,
    w_key,
    w_value,
    w_output,
    neighbour_ids,
    lengths,
    owners,
):
    bf16 = jnp.bfloat16
    shards = NZ * NX
    seq_index = lax.axis_index("y") * NC + lax.axis_index("c")
    entries, stripe, features = database.shape
    per_row = neighbour_ids.shape[2]

    ids = lax.dynamic_index_in_dim(neighbour_ids, seq_index, 1, keepdims=False)
    token_row = (ids[:, :, None] * stripe + jnp.arange(stripe, dtype=jnp.int32)).reshape(-1)
    stored = database.reshape(entries * stripe, features)
    pick = (token_row[:, None] == jnp.arange(entries * stripe, dtype=jnp.int32)[None]).astype(bf16)
    outgoing = dot(pick, stored).astype(bf16).reshape(shards, per_row * stripe, features)
    arrived = lax.all_to_all(outgoing, DB, split_axis=0, concat_axis=0, tiled=True)
    arrived = arrived.reshape(shards * per_row * stripe, features)

    rows_each = w_expand.shape[0]
    padded = 16
    ff_part = pad_rows(jnp.concatenate([w_expand, w_reduce.T], axis=1), padded)
    ff_cols = spread(spread(ff_part, "z", NZ), "x", NX).reshape(shards * padded, -1)
    slot = jnp.arange(shards * padded, dtype=jnp.int32)
    slot_shard = (slot // padded) % NZ * NX + slot // (padded * NZ)
    slot_feature = jnp.where(slot % padded < rows_each, slot_shard * rows_each + slot % padded, -1)
    place = (slot_feature[:, None] == jnp.arange(features, dtype=jnp.int32)[None]).astype(bf16)
    ff_t = lax.dot_general(
        ff_cols, place, (((0,), (0,)), ((), ())), preferred_element_type=jnp.float32
    ).astype(bf16)
    ff_mine, ff_other = gather_seq(ff_t)
    ff_all = jnp.concatenate([ff_mine, ff_other], axis=0)
    hidden_each = w_expand.shape[1]
    expand_t = ff_all[:, :hidden_each].reshape(-1, features)
    reduce_all = ff_all[:, hidden_each:].reshape(-1, features)

    head_part = jnp.concatenate(
        [
            jnp.concatenate([w_query, w_output], axis=1),
            pad_rows(jnp.concatenate([w_key, w_value], axis=1), padded),
        ],
        axis=0,
    )
    heads = spread(spread(head_part, "z", NZ), "x", NX).reshape((NX, NZ) + head_part.shape)
    model_each = w_query.shape[0]
    width = w_query.shape[1]
    q_o = jnp.swapaxes(heads[:, :, :model_each], 0, 1).reshape(-1, 2 * width)
    w_q = q_o[:, :width]
    w_o = to_relative(q_o[:, width:].reshape(NY * NC, -1, width)).reshape(-1, width)
    pairs = heads[:, :, model_each:].reshape(shards * padded, 2 * width)
    w_pairs = lax.dot_general(
        place, pairs, (((0,), (0,)), ((), ())), preferred_element_type=jnp.float32
    ).astype(bf16)

    own_rows, other_rows = gather_seq(reader[0])
    rows = jnp.concatenate([own_rows, other_rows], axis=0)
    tokens = rows.shape[1]
    normed = rms_scale(rows, reader_gain).astype(bf16).reshape(-1, rows.shape[2])
    queries = dot(normed, w_q).astype(bf16).reshape(2, NY, tokens, width)
    queries = to_natural(queries[0], queries[1]).reshape(-1, width)
    queries = jnp.concatenate([queries[SPAN:], queries[:SPAN]], axis=0)
    queries = to_relative(queries.reshape(NY * NC, tokens, width))
    residual = lax.dynamic_slice_in_dim(rows, seq_index * width, width, 2)
    residual = to_natural(residual[:NY], residual[NY:]).reshape(-1, width)

    own_len = lax.dynamic_index_in_dim(lengths[0], seq_index, 0, keepdims=False)
    own_owner = lax.dynamic_index_in_dim(owners[0], seq_index, 0, keepdims=False)
    position = jnp.arange(PACK, dtype=jnp.int32)
    start = jnp.int32(0)
    source_row = jnp.zeros((PACK,), jnp.int32)
    for j in range(per_row):
        token = position - start
        inside = (token >= 0) & (token < own_len[j])
        shard = (own_owner[j] + token // stripe) % shards
        source = (shard * per_row + j) * stripe + token % stripe
        source_row = jnp.where(inside, source, source_row)
        start = start + own_len[j]
    slots = jnp.arange(arrived.shape[0], dtype=jnp.int32)
    packing = (source_row[:, None] == slots[None]).astype(bf16)
    live_rows = dot(packing, arrived).astype(bf16)

    normed_rows = rms_scale(live_rows, encoder_gain).astype(bf16)
    hidden = lax.dot_general(
        normed_rows, expand_t, (((1,), (1,)), ((), ())), preferred_element_type=jnp.float32
    )
    hidden = jax.nn.gelu(hidden, approximate=False).astype(bf16)
    encoded = (live_rows.astype(jnp.float32) + dot(hidden, reduce_all)).astype(bf16)

    enc_mine, enc_other = gather_seq(encoded)
    enc_all = jnp.concatenate([enc_mine, enc_other], axis=0).reshape(-1, features)
    key_value = dot(enc_all, w_pairs).astype(bf16).reshape(NY * NC, PACK, 2 * width)

    local_heads = width // HD
    keys = key_value[:, :, :width].reshape(NY * NC, PACK, local_heads, HD)
    values = key_value[:, :, width:].reshape(NY * NC, PACK, local_heads, HD)
    first_live = to_relative(lengths[0, :, 0] + lengths[0, :, 1])
    in_first = position[None, :] < first_live[:, None]
    upper = jnp.arange(tokens, dtype=jnp.int32) < SPAN
    allowed = in_first[:, None, :] == upper[None, :, None]
    query_heads = queries.reshape(NY * NC, tokens, local_heads, HD)
    scores = jnp.einsum(
        "cqhd,ckhd->chqk", query_heads, keys, preferred_element_type=jnp.float32
    ) * HD ** (-0.5)
    masked = jnp.where(allowed[:, None], scores, -jnp.inf)
    largest = jnp.max(masked, axis=-1, keepdims=True)
    largest = jnp.where(jnp.isfinite(largest), largest, 0.0)
    powers = jnp.exp(masked - largest)
    totals = jnp.sum(powers, axis=-1, keepdims=True)
    weights = (powers / jnp.where(totals > 0, totals, 1.0)).astype(bf16)
    attended = jnp.einsum("chqk,ckhd->cqhd", weights, values, preferred_element_type=jnp.float32)
    attended = attended.astype(bf16).reshape(NC, NY, tokens, width)
    attended = to_natural(attended[0], attended[1]).reshape(-1, width)
    attended = jnp.concatenate(
        [jnp.zeros((SPAN, width), bf16), attended[: attended.shape[0] - SPAN]], axis=0
    )

    att_mine, att_other = gather_seq(attended)
    att = jnp.concatenate([att_mine, att_other], axis=0)
    att = jnp.swapaxes(att, 0, 1).reshape(att.shape[1], -1)
    update = dot(att, w_o)
    return (residual.astype(jnp.float32) + update).astype(bf16)[None]


def solution(mesh):
    fine = Mesh(mesh.devices.reshape(NZ, NX, NY, NC), ("z", "x", "y", "c"))
    in_specs = (
        P(DB, SEQ, None),
        P(),
        P(DB, None, None),
        P(),
        P(DB, SEQ),
        P(SEQ, DB),
        P(DB, SEQ),
        P(DB, SEQ),
        P(DB, SEQ),
        P(DB, SEQ),
        P(),
        P(DB, None, None),
        P(DB, None, None),
    )
    out_specs = P(DB, None, SEQ)
    return jax.shard_map(body, mesh=fine, in_specs=in_specs, out_specs=out_specs, check_vma=False)
```

time: 867 us -> 352 us (0.41)
  waiting for transfers between devices: 452 us -> 93.5 us
  blocking collectives: 303 us -> 29.3 us
  starting transfers between devices: 10.8 us -> 110 us
  matrix products: 14 us -> 36 us
  other arithmetic: 5.79 us -> 27.2 us
  local copies, waits for them, and re-layouts: 66 us -> 51.4 us
  between operations: 13.4 us -> 2.93 us
    all_gather x4 -> x0, waiting for transfers between devices: 450 us -> none  [the longest x1 173 us: body(): rows = lax.all_gather(reader[0], 'seq', axis=0, tiled=True)]
    all_gather x4 -> x0, blocking collectives: 303 us -> none  [the longest x1 81.7 us: body(): reduce_part = lax.all_gather(w_reduce, 'db', axis=1, tiled=True)]
    ppermute x0 -> x20, starting transfers between devices: none -> 74 us  [the longest x4 18.9 us: gather_seq(): other = lax.ppermute(mine, 'c', [(0, 1), (1, 0)])]
    all_to_all x1 -> x4, waiting for transfers between devices: 0.01 us -> 52.7 us  [the longest x3 52.7 us: spread(): return lax.all_to_all(copies, axis, split_axis=0, concat_axis=0, tiled=True)]
    gather x2 -> x0, local copies, waits for them, and re-layouts: 41.5 us -> none  [the longest x1 21.4 us: body(): outgoing = table[requests]]
    ppermute x0 -> x20, waiting for transfers between devices: none -> 40.8 us  [the longest x4 14.5 us: gather_seq(): right = lax.ppermute(part, 'y', ring(1))]
    all_to_all x0 -> x1, blocking collectives: none -> 29.3 us  [spread(): return lax.all_to_all(copies, axis, split_axis=0, concat_axis=0, tiled=True)]
    all_to_all x1 -> x4, starting transfers between devices: 10.5 us -> 36.1 us  [the longest x3 22.8 us: spread(): return lax.all_to_all(copies, axis, split_axis=0, concat_axis=0, tiled=True)]
  transfers between devices with their start and end apart: 6 -> 24, of which waited for: 4 -> 13; matrix products, arithmetic and copies ran while one was open for 6% -> 16% of each run, Pallas kernels for 0% -> 0%
where the time goes in v1:
time: 352 us; the launch traced here: 350 us
  starting transfers between devices  110 us (31%)
  waiting for transfers between devices  93.5 us (27%)
  local copies, waits for them, and re-layouts  51.4 us (15%)
  matrix products  36 us (10%)
  blocking collectives  29.3 us (8%)
  other arithmetic  27.2 us (8%)
    all_to_all x3, waiting for transfers between devices, spread(): return lax.all_to_all(copies, axis, split_axis=0, concat_axis=0, tiled=True)  52.7 us
    dot_general x6, matrix products, dot(): return jnp.dot(a, b, preferred_element_type=jnp.float32)  30.8 us
    all_to_all x1, blocking collectives, spread(): return lax.all_to_all(copies, axis, split_axis=0, concat_axis=0, tiled=True)  29.3 us
    all_to_all x3, starting transfers between devices, spread(): return lax.all_to_all(copies, axis, split_axis=0, concat_axis=0, tiled=True)  22.8 us
    ppermute x4, starting transfers between devices, gather_seq(): other = lax.ppermute(mine, 'c', [(0, 1), (1, 0)])  18.9 us
    ppermute x4, starting transfers between devices, gather_seq(): far_left = lax.ppermute(left[half:], 'y', ring(-1))  17.9 us
    ppermute x4, starting transfers between devices, gather_seq(): left = lax.ppermute(part, 'y', ring(-1))  17.2 us
    ppermute x4, waiting for transfers between devices, gather_seq(): right = lax.ppermute(part, 'y', ring(1))  14.5 us
  transfers between devices with their start and end apart: 24, of which 13 were waited for; matrix products, arithmetic and copies ran while one was open for 16% of the time, Pallas kernels for 0%

profile of v1, /device:TPU:1, one launch (start us, length us, event | category | flops | bytes accessed | tf_op | source)
XLA Modules:
  0.0 350.5 jit_solution(14118781625080874942)
XLA Ops:
  0.9 29.3 %all_to_all.25 = bf16[16,16,448]{2,1,0:T(8,128)(2,1)S(1)} all-to-all(bf16[16,16,448]{2,1,0:T(8,128)(2,1)S(1)} %broadcast_in_dim.26), channel_id=1, replica_groups=mesh['z'=16,'x'=4,'y'=4,'c'=2] {'z'}, dimensions={0} | all-to-all | bytes 458752 | tf_op jit(solution)/shard_map/all_to_all | solution.py:33
  30.2 1.1 broadcast_in_dim.27
  31.3 4.1 %all-to-all-start.2 = ((bf16[4,16,16,448]{3,2,1,0:T(8,128)(2,1)}), bf16[4,16,16,448]{3,2,1,0:T(8,128)(2,1)S(1)}, u32[]{:S(2)}, u32[]{:S(2)}) async-start(bf16[4,16,16,448]{3,2,1,0:T(8,128)(2,1)} %broadcast_in_dim.27), calls=%async_computation.2 | async-start | bytes 2097152 | tf_op jit(solution)/shard_map/all_to_all | solution.py:33
  35.5 9.7 %all-to-all-done.2 = bf16[4,16,16,448]{3,2,1,0:T(8,128)(2,1)S(1)} async-done(((bf16[4,16,16,448]{3,2,1,0:T(8,128)(2,1)}), bf16[4,16,16,448]{3,2,1,0:T(8,128)(2,1)S(1)}, u32[]{:S(2)}, u32[]{:S(2)}) %all-to-all-start.2) | async-done | bytes 917536 | tf_op jit(solution)/shard_map/all_to_all | solution.py:33
  45.2 1.1 broadcast_in_dim.28
  46.3 14.7 %all-to-all-start.3 = ((bf16[16,48,512]{2,1,0:T(8,128)(2,1)}), bf16[16,48,512]{2,1,0:T(8,128)(2,1)S(1)}, u32[]{:S(2)}, u32[]{:S(2)}) async-start(bf16[16,48,512]{2,1,0:T(8,128)(2,1)} %broadcast_in_dim.28), calls=%async_computation.3 | async-start | bytes 1572864 | tf_op jit(solution)/shard_map/all_to_all | solution.py:33
  61.1 3.2 collective-permute-start.1
  64.3 3.4 collective-permute-start
  72.7 1.4 fusion.20
  74.1 21.8 %all-to-all-done.3 = bf16[16,48,512]{2,1,0:T(8,128)(2,1)S(1)} async-done(((bf16[16,48,512]{2,1,0:T(8,128)(2,1)}), bf16[16,48,512]{2,1,0:T(8,128)(2,1)S(1)}, u32[]{:S(2)}, u32[]{:S(2)}) %all-to-all-start.3) | async-done | bytes 786464 | tf_op jit(solution)/shard_map/all_to_all | solution.py:33
  95.9 13.3 %all-to-all-start = ((bf16[64,8,896]{2,1,0:T(8,128)(2,1)}), bf16[64,8,896]{2,1,0:T(8,128)(2,1)}, u32[]{:S(2)}, u32[]{:S(2)}) async-start(bf16[64,8,896]{2,1,0:T(8,128)(2,1)} %fusion.20), calls=%async_computation | async-start | bytes 1835008 | tf_op jit(solution)/shard_map/all_to_all | solution.py:102
  109.9 3.2 collective-permute-start.2
  113.8 3.3 collective-permute-start.3
  117.2 5.0 %fusion.117 = s32[320]{0:T(512)S(1)} fusion(s32[]{:T(128)} %bitcast.15, s32[]{:T(128)} %bitcast.14, s32[]{:T(128)} %bitcast.9, s32[]{:T(128)} %bitcast.8, s32[]{:T(128)} %bitcast.13, s32[]{:T(128)} %bitcast.10, s32[]{:T(128)S(6)} %add.326, s32[]{:T(128)} %bitcast.12, s32[]{:T(128)} %bitcast.11, s32[]{:T(128)S(6)} %add.327), kind=kLoop, calls=%fused_computation.232 | loop fusion | flops 47360 | bytes 1320 | tf_op jit(solution)/shard_map/jit(_where)/select_n | solution.py:161
  122.5 3.4 constant_dynamic-update-slice_fusion.9
  125.9 3.2 collective-permute-start.6
  129.1 3.4 collective-permute-start.5
  132.4 1.6 pad_maximum_fusion.2
  134.1 4.6 %collective-permute-start.4 = (bf16[4,128,2048]{2,1,0:T(8,128)(2,1)}, bf16[4,128,2048]{2,1,0:T(8,128)(2,1)}, u32[]{:S(2)}, u32[]{:S(2)}) collective-permute-start(bf16[4,128,2048]{2,1,0:T(8,128)(2,1)} %pad_maximum_fusion.2), channel_id=1, source_target_pairs={{0,1},{1,0},{2,3},{3,2},{4,5},{5,4},{6,7},{7,6},{8,9},{9,8},{10,11... | collective-permute-start | bytes 6291464 | tf_op jit(solution)/shard_map/ppermute | solution.py:48
  138.8 7.7 %collective-permute-done.6 = bf16[448,896]{1,0:T(8,128)(2,1)S(1)} collective-permute-done((bf16[448,896]{1,0:T(8,128)(2,1)S(1)}, bf16[448,896]{1,0:T(8,128)(2,1)S(1)}, u32[]{:S(2)}, u32[]{:S(2)}) %collective-permute-start.6) | collective-permute-done | bytes 802848 | tf_op jit(solution)/shard_map/ppermute | solution.py:43
  146.5 1.9 collective-permute-start.7
  148.5 4.6 %collective-permute-start.8 = (bf16[224,896]{1,0:T(8,128)(2,1)S(1)}, bf16[224,896]{1,0:T(8,128)(2,1)S(1)}, u32[]{:S(2)}, u32[]{:S(2)}) collective-permute-start(bf16[224,896]{1,0:T(8,128)(2,1)S(1)} %slice.274), channel_id=1, source_target_pairs={{0,6},{2,0},{4,2},{6,4},{1,7},{3,1},{5,3},{7,5},{8,14},{10,8},{12,... | collective-permute-start | bytes 1204232 | tf_op jit(solution)/shard_map/ppermute | solution.py:44
  153.1 4.6 %collective-permute-done.7 = bf16[224,896]{1,0:T(8,128)(2,1)S(1)} collective-permute-done((bf16[224,896]{1,0:T(8,128)(2,1)S(1)}, bf16[224,896]{1,0:T(8,128)(2,1)S(1)}, u32[]{:S(2)}, u32[]{:S(2)}) %collective-permute-start.7) | collective-permute-done | bytes 401440 | tf_op jit(solution)/shard_map/ppermute | solution.py:45
  158.6 1.9 pad_maximum_fusion
  160.5 5.9 %collective-permute-start.9 = (bf16[4,448,896]{2,1,0:T(8,128)(2,1)}, bf16[4,448,896]{2,1,0:T(8,128)(2,1)}, u32[]{:S(2)}, u32[]{:S(2)}) collective-permute-start(bf16[4,448,896]{2,1,0:T(8,128)(2,1)} %pad_maximum_fusion), channel_id=1, source_target_pairs={{0,1},{1,0},{2,3},{3,2},{4,5},{5,4},{6,7},{7,6},{8,9},{9,8},{10,11... | collective-permute-start | bytes 9633800 | tf_op jit(solution)/shard_map/ppermute | solution.py:48
  168.4 2.0 broadcast_in_dim.29
  170.4 3.9 %all-to-all-start.4 = ((bf16[4,16,48,512]{3,2,1,0:T(8,128)(2,1)}), bf16[4,16,48,512]{3,2,1,0:T(8,128)(2,1)S(1)}, u32[]{:S(2)}, u32[]{:S(2)}) async-start(bf16[4,16,48,512]{3,2,1,0:T(8,128)(2,1)} %broadcast_in_dim.29), calls=%async_computation.4 | async-start | bytes 6291456 | tf_op jit(solution)/shard_map/all_to_all | solution.py:33
  174.3 2.1 constant_dynamic-update-slice_fusion.6
  176.4 3.2 constant_dynamic-update-slice_fusion
  179.5 1.1 dynamic-slice_bitcast_fusion.1
  181.4 3.2 multiply_reduce_fusion
  184.9 3.1 fusion.1
  188.0 2.6 fusion.37
  190.5 21.2 %all-to-all-done.4 = bf16[4,16,48,512]{3,2,1,0:T(8,128)(2,1)S(1)} async-done(((bf16[4,16,48,512]{3,2,1,0:T(8,128)(2,1)}), bf16[4,16,48,512]{3,2,1,0:T(8,128)(2,1)S(1)}, u32[]{:S(2)}, u32[]{:S(2)}) %all-to-all-start.4) | async-done | bytes 3145760 | tf_op jit(solution)/shard_map/all_to_all | solution.py:33
  211.9 1.9 copy.35
  213.8 3.9 %constant_dynamic-update-slice_fusion.5 = bf16[8,448,896]{2,1,0:T(8,128)(2,1)} fusion(bf16[8,448,896]{2,1,0:T(8,128)(2,1)} %constant_dynamic-update-slice_fusion.6, bf16[4,448,896]{2,1,0:T(8,128)(2,1)} %collective-permute-done.9), kind=kLoop, calls=%fused_computation.138 | loop fusion | bytes 6422528 | tf_op jit(solution)/shard_map/concatenate | solution.py:117
  217.7 6.1 %fusion.188 = (bf16[8,224,896]{2,1,0:T(8,128)(2,1)}, bf16[8,224,896]{2,1,0:T(8,128)(2,1)}) fusion(bf16[8,448,896]{2,1,0:T(8,128)(2,1)} %constant_dynamic-update-slice_fusion.5), kind=kLoop, calls=%fused_computation.320 | loop fusion | bytes 12845056 | tf_op jit(solution)/shard_map/slice | solution.py:119
  223.8 10.9 %constant_dynamic-update-slice_fusion.14 = (bf16[8,320,896]{2,1,0:T(8,128)(2,1)}, bf16[320,896]{1,0:T(8,128)(2,1)}) fusion(bf16[1792,896]{1,0:T(8,128)(2,1)} %bitcast.149, bf16[1792,896]{1,0:T(8,128)(2,1)} %bitcast.148, bf16[320,896]{1,0:T(8,128)(2,1)} %get-tuple-element.40, f32[896]{0:T(1024)S(1)} %copy-done.28, f32[320]{0:T(512)S(1)} %add_rsqrt_fusion), kind=kOutput, calls=%fused_computation.147 | convolution fusion | flops 2094489600 | bytes 8721152 | tf_op jit(solution)/shard_map/dot_general | solution.py:28
  234.7 2.4 collective-permute-start.11
  237.1 5.1 %collective-permute-start.10 = (bf16[320,896]{1,0:T(8,128)(2,1)}, bf16[320,896]{1,0:T(8,128)(2,1)S(1)}, u32[]{:S(2)}, u32[]{:S(2)}) collective-permute-start(bf16[320,896]{1,0:T(8,128)(2,1)} %get-tuple-element.42), channel_id=1, source_target_pairs={{0,6},{2,0},{4,2},{6,4},{1,7},{3,1},{5,3},{7,5},{8,14},{10,8},{12,... | collective-permute-start | bytes 1720328 | tf_op jit(solution)/shard_map/ppermute | solution.py:42
  242.2 3.7 %convolution_convert_fusion.3 = bf16[1024,256]{1,0:T(8,128)(2,1)S(1)} fusion(bf16[1024,2048]{1,0:T(8,128)(2,1)} %fusion.1, bf16[2048,512]{1,0:T(8,128)(2,1)} %bitcast.138), kind=kOutput, calls=%fused_computation.61 | convolution fusion | flops 1074003968 | bytes 5767168 | tf_op jit(solution)/shard_map/dot_general | solution.py:28
  246.0 6.7 %collective-permute-done.11 = bf16[320,896]{1,0:T(8,128)(2,1)S(1)} collective-permute-done((bf16[320,896]{1,0:T(8,128)(2,1)}, bf16[320,896]{1,0:T(8,128)(2,1)S(1)}, u32[]{:S(2)}, u32[]{:S(2)}) %collective-permute-start.11) | collective-permute-done | bytes 573472 | tf_op jit(solution)/shard_map/ppermute | solution.py:43
  252.7 1.9 collective-permute-start.12
  254.7 4.7 %collective-permute-start.13 = (bf16[160,896]{1,0:T(8,128)(2,1)S(1)}, bf16[160,896]{1,0:T(8,128)(2,1)S(1)}, u32[]{:S(2)}, u32[]{:S(2)}) collective-permute-start(bf16[160,896]{1,0:T(8,128)(2,1)S(1)} %slice.278), channel_id=1, source_target_pairs={{0,6},{2,0},{4,2},{6,4},{1,7},{3,1},{5,3},{7,5},{8,14},{10,8},{12,... | collective-permute-start | bytes 860168 | tf_op jit(solution)/shard_map/ppermute | solution.py:44
  259.7 3.1 collective-permute-done.12
  262.8 1.1 collective-permute-done.13
  264.6 1.8 pad_maximum_fusion.1
  266.4 4.5 %collective-permute-start.14 = (bf16[4,320,896]{2,1,0:T(8,128)(2,1)}, bf16[4,320,896]{2,1,0:T(8,128)(2,1)}, u32[]{:S(2)}, u32[]{:S(2)}) collective-permute-start(bf16[4,320,896]{2,1,0:T(8,128)(2,1)} %pad_maximum_fusion.1), channel_id=1, source_target_pairs={{0,1},{1,0},{2,3},{3,2},{4,5},{5,4},{6,7},{7,6},{8,9},{9,8},{10,11... | collective-permute-start | bytes 6881288 | tf_op jit(solution)/shard_map/ppermute | solution.py:48
  274.2 2.0 copy.38
  279.9 3.4 constant_dynamic-update-slice_fusion.10
  283.3 7.8 %convolution_convert_fusion = bf16[2560,512]{1,0:T(8,128)(2,1)} fusion(bf16[2560,896]{1,0:T(8,128)(2,1)} %bitcast.168, bf16[1024,512]{1,0:T(8,128)(2,1)S(1)} %bitcast.135, s32[1024]{0:T(1024)S(1)} %fusion.102), kind=kOutput, calls=%fused_computation.4 | convolution fusion | flops 3291021312 | bytes 8261632 | tf_op jit(solution)/shard_map/dot_general | solution.py:28
  291.1 2.2 slice_bitcast_fusion.2
  294.5 1.3 fusion.34
  296.8 5.5 %collective-permute-start.15 = (bf16[1024,256]{1,0:T(8,128)(2,1)S(1)}, bf16[1024,256]{1,0:T(8,128)(2,1)S(1)}, u32[]{:S(2)}, u32[]{:S(2)}) collective-permute-start(bf16[1024,256]{1,0:T(8,128)(2,1)S(1)} %get-tuple-element.26), channel_id=1, source_target_pairs={{0,6},{2,0},{4,2},{6,4},{1,7},{3,1},{5,3},{7,5},{8,14},{10,8},{12,... | collective-permute-start | bytes 1572872 | tf_op jit(solution)/shard_map/ppermute | solution.py:42
  302.3 1.9 collective-permute-start.16
  304.5 9.1 %collective-permute-done.15 = bf16[1024,256]{1,0:T(8,128)(2,1)S(1)} collective-permute-done((bf16[1024,256]{1,0:T(8,128)(2,1)S(1)}, bf16[1024,256]{1,0:T(8,128)(2,1)S(1)}, u32[]{:S(2)}, u32[]{:S(2)}) %collective-permute-start.15) | collective-permute-done | bytes 524320 | tf_op jit(solution)/shard_map/ppermute | solution.py:42
  313.6 5.3 %collective-permute-start.18 = (bf16[512,256]{1,0:T(8,128)(2,1)S(1)}, bf16[512,256]{1,0:T(8,128)(2,1)S(1)}, u32[]{:S(2)}, u32[]{:S(2)}) collective-permute-start(bf16[512,256]{1,0:T(8,128)(2,1)S(1)} %slice.304), channel_id=1, source_target_pairs={{0,6},{2,0},{4,2},{6,4},{1,7},{3,1},{5,3},{7,5},{8,14},{10,8},{12,... | collective-permute-start | bytes 786440 | tf_op jit(solution)/shard_map/ppermute | solution.py:44
  318.9 2.2 collective-permute-start.17
  321.4 2.3 collective-permute-done.18
  323.7 5.1 %collective-permute-done.17 = bf16[512,256]{1,0:T(8,128)(2,1)S(1)} collective-permute-done((bf16[512,256]{1,0:T(8,128)(2,1)S(1)}, bf16[512,256]{1,0:T(8,128)(2,1)S(1)}, u32[]{:S(2)}, u32[]{:S(2)}) %collective-permute-start.17) | collective-permute-done | bytes 262176 | tf_op jit(solution)/shard_map/ppermute | solution.py:45
  329.1 3.9 %collective-permute-start.19 = (bf16[4,1024,256]{2,1,0:T(8,128)(2,1)S(1)}, bf16[4,1024,256]{2,1,0:T(8,128)(2,1)S(1)}, u32[]{:S(2)}, u32[]{:S(2)}) collective-permute-start(bf16[4,1024,256]{2,1,0:T(8,128)(2,1)S(1)} %pad_maximum_fusion.3), channel_id=1, source_target_pairs={{0,1},{1,0},{2,3},{3,2},{4,5},{5,4},{6,7},{7,6},{8,9},{9,8},{10,11... | collective-permute-start | bytes 6291464 | tf_op jit(solution)/shard_map/ppermute | solution.py:48
  338.2 1.5 constant_dynamic-update-slice_fusion.15
  339.7 6.5 %copy.44 = bf16[1024,8,256]{0,2,1:T(8,128)(2,1)} copy(bf16[1024,8,256]{2,0,1:T(8,128)(2,1)} %bitcast.55) | data formatting | bytes 8388608 | tf_op jit(solution)/shard_map/transpose | solution.py:204
  346.2 4.3 %fusion.33 = bf16[1,1024,256]{2,1,0:T(8,128)(2,1)} fusion(bf16[1024,2048]{0,1:T(8,128)(2,1)} %bitcast.140, bf16[2048,256]{1,0:T(8,128)(2,1)S(1)} %bitcast.158, bf16[1024,256]{1,0:T(8,128)(2,1)S(1)} %bitcast.165), kind=kOutput, calls=%fused_computation.62 | convolution fusion | flops 1074528256 | bytes 6291456 | tf_op jit(solution)/shard_map/dot_general | solution.py:28
  (178 shorter events, 25.6 us)
Async XLA Ops:
  0.0 35.5 %copy-start.24 = (bf16[14,256]{1,0:T(8,128)(2,1)S(1)}, bf16[14,256]{1,0:T(8,128)(2,1)}, u32[]{:S(2)}) copy-start(bf16[14,256]{1,0:T(8,128)(2,1)} %param.21) | copy-start | bytes 21508
  0.0 35.5 %copy-start.25 = (bf16[14,256]{1,0:T(8,128)(2,1)S(1)}, bf16[14,256]{1,0:T(8,128)(2,1)}, u32[]{:S(2)}) copy-start(bf16[14,256]{1,0:T(8,128)(2,1)} %param.20) | copy-start | bytes 21508
  0.0 35.5 %copy-start.21 = (bf16[32,256]{1,0:T(8,128)(2,1)S(1)}, bf16[32,256]{1,0:T(8,128)(2,1)}, u32[]{:S(2)}) copy-start(bf16[32,256]{1,0:T(8,128)(2,1)} %param.22) | copy-start | bytes 49156
  0.0 35.5 %copy-start.22 = (bf16[32,256]{1,0:T(8,128)(2,1)S(1)}, bf16[32,256]{1,0:T(8,128)(2,1)}, u32[]{:S(2)}) copy-start(bf16[32,256]{1,0:T(8,128)(2,1)} %param.19) | copy-start | bytes 49156
  31.3 29.8 %copy-start.12 = (bf16[1,128,2048]{2,1,0:T(8,128)(2,1)S(1)}, bf16[1,128,2048]{2,1,0:T(8,128)(2,1)}, u32[]{:S(2)}) copy-start(bf16[1,128,2048]{2,1,0:T(8,128)(2,1)} %param.13) | copy-start | bytes 1572868
  31.3 36.4 %copy-start.26 = (s32[1,8,4]{1,2,0:T(4,128)S(1)}, s32[1,8,4]{1,2,0:T(4,128)}, u32[]{:S(2)}) copy-start(s32[1,8,4]{1,2,0:T(4,128)} %param.24) | copy-start | bytes 388
  31.3 37.9 %copy-start.20 = (bf16[128,2,896]{2,1,0:T(2,128)(2,1)S(1)}, bf16[128,2,896]{2,1,0:T(2,128)(2,1)}, u32[]{:S(2)}) copy-start(bf16[128,2,896]{2,1,0:T(2,128)(2,1)} %param.15) | copy-start | bytes 1376260
  31.3 13.9 %all-to-all-start.2 = ((bf16[4,16,16,448]{3,2,1,0:T(8,128)(2,1)}), bf16[4,16,16,448]{3,2,1,0:T(8,128)(2,1)S(1)}, u32[]{:S(2)}, u32[]{:S(2)}) async-start(bf16[4,16,16,448]{3,2,1,0:T(8,128)(2,1)} %broadcast_in_dim.27), calls=%async_computation.2 | async-start | bytes 2097152 | tf_op jit(solution)/shard_map/all_to_all | solution.py:33
  35.5 34.0 %copy-start.27 = (s32[1,8,4]{1,2,0:T(4,128)S(1)}, s32[1,8,4]{1,2,0:T(4,128)}, u32[]{:S(2)}) copy-start(s32[1,8,4]{1,2,0:T(4,128)} %param.25) | copy-start | bytes 388
  45.2 15.9 %copy-start.17 = (bf16[4,16,16,448]{3,2,1,0:T(8,128)(2,1)}, bf16[4,16,16,448]{3,2,1,0:T(8,128)(2,1)S(1)}, u32[]{:S(2)}) copy-start(bf16[4,16,16,448]{3,2,1,0:T(8,128)(2,1)S(1)} %all-to-all-done.2) | copy-start | bytes 2752516
  46.3 49.6 %all-to-all-start.3 = ((bf16[16,48,512]{2,1,0:T(8,128)(2,1)}), bf16[16,48,512]{2,1,0:T(8,128)(2,1)S(1)}, u32[]{:S(2)}, u32[]{:S(2)}) async-start(bf16[16,48,512]{2,1,0:T(8,128)(2,1)} %broadcast_in_dim.28), calls=%async_computation.3 | async-start | bytes 1572864 | tf_op jit(solution)/shard_map/all_to_all | solution.py:33
  61.1 48.7 %collective-permute-start.1 = (bf16[128,2048]{1,0:T(8,128)(2,1)S(1)}, bf16[128,2048]{1,0:T(8,128)(2,1)S(1)}, u32[]{:S(2)}, u32[]{:S(2)}) collective-permute-start(bf16[128,2048]{1,0:T(8,128)(2,1)S(1)} %bitcast.154), channel_id=1, source_target_pairs={{0,2},{2,4},{4,6},{6,0},{1,3},{3,5},{5,7},{7,1},{8,10},{10,12},{12... | collective-permute-start | bytes 1572872 | tf_op jit(solution)/shard_map/ppermute | solution.py:43
  64.3 48.8 %collective-permute-start = (bf16[128,2048]{1,0:T(8,128)(2,1)S(1)}, bf16[128,2048]{1,0:T(8,128)(2,1)S(1)}, u32[]{:S(2)}, u32[]{:S(2)}) collective-permute-start(bf16[128,2048]{1,0:T(8,128)(2,1)S(1)} %bitcast.155), channel_id=1, source_target_pairs={{0,6},{2,0},{4,2},{6,4},{1,7},{3,1},{5,3},{7,5},{8,14},{10,8},{12,... | collective-permute-start | bytes 1572872 | tf_op jit(solution)/shard_map/ppermute | solution.py:42
  95.9 72.5 %all-to-all-start = ((bf16[64,8,896]{2,1,0:T(8,128)(2,1)}), bf16[64,8,896]{2,1,0:T(8,128)(2,1)}, u32[]{:S(2)}, u32[]{:S(2)}) async-start(bf16[64,8,896]{2,1,0:T(8,128)(2,1)} %fusion.20), calls=%async_computation | async-start | bytes 1835008 | tf_op jit(solution)/shard_map/all_to_all | solution.py:102
  109.9 12.3 %collective-permute-start.2 = (bf16[64,2048]{1,0:T(8,128)(2,1)S(1)}, bf16[64,2048]{1,0:T(8,128)(2,1)S(1)}, u32[]{:S(2)}, u32[]{:S(2)}) collective-permute-start(bf16[64,2048]{1,0:T(8,128)(2,1)S(1)} %slice.267), channel_id=1, source_target_pairs={{0,2},{2,4},{4,6},{6,0},{1,3},{3,5},{5,7},{7,1},{8,10},{10,12},{12... | collective-permute-start | bytes 786440 | tf_op jit(solution)/shard_map/ppermute | solution.py:45
  113.8 8.6 %collective-permute-start.3 = (bf16[64,2048]{1,0:T(8,128)(2,1)}, bf16[64,2048]{1,0:T(8,128)(2,1)S(1)}, u32[]{:S(2)}, u32[]{:S(2)}) collective-permute-start(bf16[64,2048]{1,0:T(8,128)(2,1)} %slice.268), channel_id=1, source_target_pairs={{0,6},{2,0},{4,2},{6,4},{1,7},{3,1},{5,3},{7,5},{8,14},{10,8},{12,... | collective-permute-start | bytes 786440 | tf_op jit(solution)/shard_map/ppermute | solution.py:44
  125.9 20.6 %collective-permute-start.6 = (bf16[448,896]{1,0:T(8,128)(2,1)S(1)}, bf16[448,896]{1,0:T(8,128)(2,1)S(1)}, u32[]{:S(2)}, u32[]{:S(2)}) collective-permute-start(bf16[448,896]{1,0:T(8,128)(2,1)S(1)} %get-tuple-element.38), channel_id=1, source_target_pairs={{0,2},{2,4},{4,6},{6,0},{1,3},{3,5},{5,7},{7,1},{8,10},{10,12},{12... | collective-permute-start | bytes 2408456 | tf_op jit(solution)/shard_map/ppermute | solution.py:43
  129.1 19.3 %collective-permute-start.5 = (bf16[448,896]{1,0:T(8,128)(2,1)S(1)}, bf16[448,896]{1,0:T(8,128)(2,1)S(1)}, u32[]{:S(2)}, u32[]{:S(2)}) collective-permute-start(bf16[448,896]{1,0:T(8,128)(2,1)S(1)} %get-tuple-element.38), channel_id=1, source_target_pairs={{0,6},{2,0},{4,2},{6,4},{1,7},{3,1},{5,3},{7,5},{8,14},{10,8},{12,... | collective-permute-start | bytes 2408456 | tf_op jit(solution)/shard_map/ppermute | solution.py:42
  134.1 42.3 %collective-permute-start.4 = (bf16[4,128,2048]{2,1,0:T(8,128)(2,1)}, bf16[4,128,2048]{2,1,0:T(8,128)(2,1)}, u32[]{:S(2)}, u32[]{:S(2)}) collective-permute-start(bf16[4,128,2048]{2,1,0:T(8,128)(2,1)} %pad_maximum_fusion.2), channel_id=1, source_target_pairs={{0,1},{1,0},{2,3},{3,2},{4,5},{5,4},{6,7},{7,6},{8,9},{9,8},{10,11... | collective-permute-start | bytes 6291464 | tf_op jit(solution)/shard_map/ppermute | solution.py:48
  146.5 14.1 %copy-start.3 = (bf16[448,896]{1,0:T(8,128)(2,1)}, bf16[448,896]{1,0:T(8,128)(2,1)S(1)}, u32[]{:S(2)}) copy-start(bf16[448,896]{1,0:T(8,128)(2,1)S(1)} %collective-permute-done.6) | copy-start | bytes 2408452
  146.5 11.2 %collective-permute-start.7 = (bf16[224,896]{1,0:T(8,128)(2,1)S(1)}, bf16[224,896]{1,0:T(8,128)(2,1)S(1)}, u32[]{:S(2)}, u32[]{:S(2)}) collective-permute-start(bf16[224,896]{1,0:T(8,128)(2,1)S(1)} %slice.273), channel_id=1, source_target_pairs={{0,2},{2,4},{4,6},{6,0},{1,3},{3,5},{5,7},{7,1},{8,10},{10,12},{12... | collective-permute-start | bytes 1204232 | tf_op jit(solution)/shard_map/ppermute | solution.py:45
  148.5 10.0 %collective-permute-start.8 = (bf16[224,896]{1,0:T(8,128)(2,1)S(1)}, bf16[224,896]{1,0:T(8,128)(2,1)S(1)}, u32[]{:S(2)}, u32[]{:S(2)}) collective-permute-start(bf16[224,896]{1,0:T(8,128)(2,1)S(1)} %slice.274), channel_id=1, source_target_pairs={{0,6},{2,0},{4,2},{6,4},{1,7},{3,1},{5,3},{7,5},{8,14},{10,8},{12,... | collective-permute-start | bytes 1204232 | tf_op jit(solution)/shard_map/ppermute | solution.py:44
  153.1 7.4 %copy-start = (bf16[8,128,2048]{2,1,0:T(8,128)(2,1)}, bf16[8,128,2048]{2,1,0:T(8,128)(2,1)S(1)}, u32[]{:S(2)}) copy-start(bf16[8,128,2048]{2,1,0:T(8,128)(2,1)S(1)} %constant_dynamic-update-slice_fusion.1) | copy-start | bytes 12582916
  160.5 53.3 %collective-permute-start.9 = (bf16[4,448,896]{2,1,0:T(8,128)(2,1)}, bf16[4,448,896]{2,1,0:T(8,128)(2,1)}, u32[]{:S(2)}, u32[]{:S(2)}) collective-permute-start(bf16[4,448,896]{2,1,0:T(8,128)(2,1)} %pad_maximum_fusion), channel_id=1, source_target_pairs={{0,1},{1,0},{2,3},{3,2},{4,5},{5,4},{6,7},{7,6},{8,9},{9,8},{10,11... | collective-permute-start | bytes 9633800 | tf_op jit(solution)/shard_map/ppermute | solution.py:48
  170.4 41.3 %all-to-all-start.4 = ((bf16[4,16,48,512]{3,2,1,0:T(8,128)(2,1)}), bf16[4,16,48,512]{3,2,1,0:T(8,128)(2,1)S(1)}, u32[]{:S(2)}, u32[]{:S(2)}) async-start(bf16[4,16,48,512]{3,2,1,0:T(8,128)(2,1)} %broadcast_in_dim.29), calls=%async_computation.4 | async-start | bytes 6291456 | tf_op jit(solution)/shard_map/all_to_all | solution.py:33
  181.4 3.4 copy-start.1
  181.4 3.4 copy-start.23
  211.7 64.5 %copy-start.2 = (bf16[4,16,48,512]{3,2,1,0:T(8,128)(2,1)}, bf16[4,16,48,512]{3,2,1,0:T(8,128)(2,1)S(1)}, u32[]{:S(2)}) copy-start(bf16[4,16,48,512]{3,2,1,0:T(8,128)(2,1)S(1)} %all-to-all-done.4) | copy-start | bytes 9437188
  217.7 6.1 %copy-start.28 = (f32[896]{0:T(1024)S(1)}, f32[896]{0:T(1024)}, u32[]{:S(2)}) copy-start(f32[896]{0:T(1024)} %param.16) | copy-start | bytes 10756
  234.7 18.0 %collective-permute-start.11 = (bf16[320,896]{1,0:T(8,128)(2,1)}, bf16[320,896]{1,0:T(8,128)(2,1)S(1)}, u32[]{:S(2)}, u32[]{:S(2)}) collective-permute-start(bf16[320,896]{1,0:T(8,128)(2,1)} %get-tuple-element.42), channel_id=1, source_target_pairs={{0,2},{2,4},{4,6},{6,0},{1,3},{3,5},{5,7},{7,1},{8,10},{10,12},{12... | collective-permute-start | bytes 1720328 | tf_op jit(solution)/shard_map/ppermute | solution.py:43
  237.1 17.6 %collective-permute-start.10 = (bf16[320,896]{1,0:T(8,128)(2,1)}, bf16[320,896]{1,0:T(8,128)(2,1)S(1)}, u32[]{:S(2)}, u32[]{:S(2)}) collective-permute-start(bf16[320,896]{1,0:T(8,128)(2,1)} %get-tuple-element.42), channel_id=1, source_target_pairs={{0,6},{2,0},{4,2},{6,4},{1,7},{3,1},{5,3},{7,5},{8,14},{10,8},{12,... | collective-permute-start | bytes 1720328 | tf_op jit(solution)/shard_map/ppermute | solution.py:42
  252.7 11.9 %copy-start.7 = (bf16[320,896]{1,0:T(8,128)(2,1)}, bf16[320,896]{1,0:T(8,128)(2,1)S(1)}, u32[]{:S(2)}) copy-start(bf16[320,896]{1,0:T(8,128)(2,1)S(1)} %collective-permute-done.11) | copy-start | bytes 1720324
  252.7 10.0 %collective-permute-start.12 = (bf16[160,896]{1,0:T(8,128)(2,1)S(1)}, bf16[160,896]{1,0:T(8,128)(2,1)S(1)}, u32[]{:S(2)}, u32[]{:S(2)}) collective-permute-start(bf16[160,896]{1,0:T(8,128)(2,1)S(1)} %slice.277), channel_id=1, source_target_pairs={{0,2},{2,4},{4,6},{6,0},{1,3},{3,5},{5,7},{7,1},{8,10},{10,12},{12... | collective-permute-start | bytes 860168 | tf_op jit(solution)/shard_map/ppermute | solution.py:45
  254.7 9.9 %copy-start.9 = (bf16[320,896]{1,0:T(8,128)(2,1)}, bf16[320,896]{1,0:T(8,128)(2,1)S(1)}, u32[]{:S(2)}) copy-start(bf16[320,896]{1,0:T(8,128)(2,1)S(1)} %collective-permute-done.10) | copy-start | bytes 1720324
  254.7 9.9 %copy-start.18 = (bf16[320,896]{1,0:T(8,128)(2,1)S(1)}, bf16[320,896]{1,0:T(8,128)(2,1)}, u32[]{:S(2)}) copy-start(bf16[320,896]{1,0:T(8,128)(2,1)} %get-tuple-element.42) | copy-start | bytes 1720324
  254.7 9.2 %collective-permute-start.13 = (bf16[160,896]{1,0:T(8,128)(2,1)S(1)}, bf16[160,896]{1,0:T(8,128)(2,1)S(1)}, u32[]{:S(2)}, u32[]{:S(2)}) collective-permute-start(bf16[160,896]{1,0:T(8,128)(2,1)S(1)} %slice.278), channel_id=1, source_target_pairs={{0,6},{2,0},{4,2},{6,4},{1,7},{3,1},{5,3},{7,5},{8,14},{10,8},{12,... | collective-permute-start | bytes 860168 | tf_op jit(solution)/shard_map/ppermute | solution.py:44
  262.8 1.1 copy-start.13
  263.9 0.7 copy-start.15
  266.4 13.5 %collective-permute-start.14 = (bf16[4,320,896]{2,1,0:T(8,128)(2,1)}, bf16[4,320,896]{2,1,0:T(8,128)(2,1)}, u32[]{:S(2)}, u32[]{:S(2)}) collective-permute-start(bf16[4,320,896]{2,1,0:T(8,128)(2,1)} %pad_maximum_fusion.1), channel_id=1, source_target_pairs={{0,1},{1,0},{2,3},{3,2},{4,5},{5,4},{6,7},{7,6},{8,9},{9,8},{10,11... | collective-permute-start | bytes 6881288 | tf_op jit(solution)/shard_map/ppermute | solution.py:48
  271.1 1.0 copy-start.11
  276.2 1.1 copy-start.10
  276.2 1.9 copy-start.14
  276.2 1.9 copy-start.16
  276.2 2.8 copy-start.8
  279.9 3.4 slice-start
  291.1 2.2 copy-start.19
  296.6 7.6 %copy-start.5 = (bf16[16,4,32,512]{3,2,1,0:T(8,128)(2,1)S(1)}, bf16[16,4,32,512]{3,2,1,0:T(8,128)(2,1)}, u32[]{:S(2)}) copy-start(bf16[16,4,32,512]{3,2,1,0:T(8,128)(2,1)} %copy.35) | copy-start | bytes 6291460
  296.7 7.6 %copy-start.4 = (bf16[4,2,128,256]{3,2,1,0:T(8,128)(2,1)S(1)}, bf16[4,2,128,256]{3,2,1,0:T(8,128)(2,1)}, u32[]{:S(2)}) copy-start(bf16[4,2,128,256]{3,2,1,0:T(8,128)(2,1)} %get-tuple-element.48) | copy-start | bytes 1572868
  296.8 16.7 %collective-permute-start.15 = (bf16[1024,256]{1,0:T(8,128)(2,1)S(1)}, bf16[1024,256]{1,0:T(8,128)(2,1)S(1)}, u32[]{:S(2)}, u32[]{:S(2)}) collective-permute-start(bf16[1024,256]{1,0:T(8,128)(2,1)S(1)} %get-tuple-element.26), channel_id=1, source_target_pairs={{0,6},{2,0},{4,2},{6,4},{1,7},{3,1},{5,3},{7,5},{8,14},{10,8},{12,... | collective-permute-start | bytes 1572872 | tf_op jit(solution)/shard_map/ppermute | solution.py:42
  302.3 16.6 %collective-permute-start.16 = (bf16[1024,256]{1,0:T(8,128)(2,1)S(1)}, bf16[1024,256]{1,0:T(8,128)(2,1)S(1)}, u32[]{:S(2)}, u32[]{:S(2)}) collective-permute-start(bf16[1024,256]{1,0:T(8,128)(2,1)S(1)} %get-tuple-element.26), channel_id=1, source_target_pairs={{0,2},{2,4},{4,6},{6,0},{1,3},{3,5},{5,7},{7,1},{8,10},{10,12},{12... | collective-permute-start | bytes 1572872 | tf_op jit(solution)/shard_map/ppermute | solution.py:43
  313.6 10.1 %collective-permute-start.18 = (bf16[512,256]{1,0:T(8,128)(2,1)S(1)}, bf16[512,256]{1,0:T(8,128)(2,1)S(1)}, u32[]{:S(2)}, u32[]{:S(2)}) collective-permute-start(bf16[512,256]{1,0:T(8,128)(2,1)S(1)} %slice.304), channel_id=1, source_target_pairs={{0,6},{2,0},{4,2},{6,4},{1,7},{3,1},{5,3},{7,5},{8,14},{10,8},{12,... | collective-permute-start | bytes 786440 | tf_op jit(solution)/shard_map/ppermute | solution.py:44
  318.9 9.8 %collective-permute-start.17 = (bf16[512,256]{1,0:T(8,128)(2,1)S(1)}, bf16[512,256]{1,0:T(8,128)(2,1)S(1)}, u32[]{:S(2)}, u32[]{:S(2)}) collective-permute-start(bf16[512,256]{1,0:T(8,128)(2,1)S(1)} %slice.303), channel_id=1, source_target_pairs={{0,2},{2,4},{4,6},{6,0},{1,3},{3,5},{5,7},{7,1},{8,10},{10,12},{12... | collective-permute-start | bytes 786440 | tf_op jit(solution)/shard_map/ppermute | solution.py:45
  321.3 11.7 %copy-start.6 = (bf16[4,2,256,256]{3,2,0,1:T(8,128)(2,1)}, bf16[4,2,256,256]{3,2,0,1:T(8,128)(2,1)S(1)}, u32[]{:S(2)}) copy-start(bf16[4,2,256,256]{3,2,0,1:T(8,128)(2,1)S(1)} %reverse_select_fusion) | copy-start | bytes 3145732
  329.1 9.1 %collective-permute-start.19 = (bf16[4,1024,256]{2,1,0:T(8,128)(2,1)S(1)}, bf16[4,1024,256]{2,1,0:T(8,128)(2,1)S(1)}, u32[]{:S(2)}, u32[]{:S(2)}) collective-permute-start(bf16[4,1024,256]{2,1,0:T(8,128)(2,1)S(1)} %pad_maximum_fusion.3), channel_id=1, source_target_pairs={{0,1},{1,0},{2,3},{3,2},{4,5},{5,4},{6,7},{7,6},{8,9},{9,8},{10,11... | collective-permute-start | bytes 6291464 | tf_op jit(solution)/shard_map/ppermute | solution.py:48
  333.1 1.0 slice-start.1
  333.1 1.2 slice-start.2

commit v2 on v1

v2 whole, which is shorter than its diff:
```python
import jax
import jax.numpy as jnp
from jax import lax
from jax.experimental import pallas as pl
from jax.experimental.pallas import tpu as pltpu
from jax.sharding import Mesh, PartitionSpec as P

HD = 128
SPAN = 64
NZ = 16
NX = 4
NY = 4
NC = 2
PACK = 320
DB = ("z", "x")
SEQ = ("y", "c")


epsilon = 1e-06


def rms_scale(values, scales):
    widened = values.astype(jnp.float32)
    mean_square = jnp.mean(widened * widened, axis=-1, keepdims=True)
    return widened * lax.rsqrt(mean_square + epsilon) * scales


def dot(a, b):
    return jnp.dot(a, b, preferred_element_type=jnp.float32)


def exchange(blocks, axis):
    return lax.all_to_all(blocks, axis, split_axis=0, concat_axis=0, tiled=True)


def spread(part, axis, size):
    return exchange(jnp.broadcast_to(part[None], (size,) + part.shape), axis)


def ring(step):
    return [(i, (i + step) % NY) for i in range(NY)]


def gather_seq(part):
    swap = [(0, 1), (1, 0)]
    near = lax.ppermute(part, "y", ring(-1))
    last = lax.ppermute(part, "y", ring(1))
    far = lax.ppermute(part, "y", ring(2))
    mine = [part, near, far, last]
    return mine + [lax.ppermute(piece, "c", swap) for piece in mine]


def gather_x(part):
    hops = (-1, 2, 1)
    return [part] + [
        lax.ppermute(part, "x", [(i, (i + step) % NX) for i in range(NX)])
        for step in hops
    ]


def natural_columns():
    return ((lax.axis_index("x") + jnp.arange(NX, dtype=jnp.int32)) % NX).astype(jnp.int32)


def natural_places():
    y = lax.axis_index("y")
    c = lax.axis_index("c")
    ahead = (y + jnp.arange(NY, dtype=jnp.int32)) % NY * NC
    return jnp.concatenate([ahead + c, ahead + 1 - c]).astype(jnp.int32)


def call(kernel, out_shape, operands, scalars, flops, scratch=()):
    size = sum(o.size * o.dtype.itemsize for o in operands)
    return pl.pallas_call(
        kernel,
        out_shape=out_shape,
        in_specs=[pl.BlockSpec(memory_space=pltpu.SMEM)] * scalars
        + [pl.BlockSpec(memory_space=pltpu.VMEM)] * (len(operands) - scalars),
        scratch_shapes=list(scratch),
        cost_estimate=pl.CostEstimate(flops=flops, bytes_accessed=size, transcendentals=0),
    )(*operands)


NT = (((1,), (1,)), ((), ()))


def feed_forward_kernel(rows_ref, gain_ref, *refs):
    pieces, out_ref = refs[:-1], refs[-1]
    each = pieces[0].shape[0] // 2
    rows = rows_ref[...]
    normed = rms_scale(rows, gain_ref[...]).astype(jnp.bfloat16)
    total = rows.astype(jnp.float32)
    for piece in pieces:
        hidden = lax.dot_general(normed, piece[:each], NT, preferred_element_type=jnp.float32)
        hidden = 0.5 * hidden * (1.0 + lax.erf(hidden * 0.5**0.5))
        total = total + dot(hidden.astype(jnp.bfloat16), piece[each:])
    out_ref[...] = total.astype(jnp.bfloat16)


def feature_slots(column, rows_each, slots, axis):
    shape = (1, slots) if axis == 1 else (slots, 1)
    slot = lax.broadcasted_iota(jnp.int32, shape, axis)
    shard = (slot >> 4) * NX + column
    return jnp.where((slot & 15) < rows_each, shard * rows_each + (slot & 15), -1)


def arrange_kernel(column_ref, *refs):
    pieces, out_ref = refs[:-1], refs[-1]
    features = out_ref.shape[1]
    slots = NZ * 16
    total = jnp.zeros(out_ref.shape, jnp.float32)
    for j, piece in enumerate(pieces):
        held = feature_slots(column_ref[j], features // (NZ * NX), slots, 0)
        place = lax.broadcasted_iota(jnp.int32, (slots, features), 1) == held
        total = total + lax.dot_general(
            piece[...].reshape(slots, -1),
            place.astype(jnp.bfloat16),
            (((0,), (0,)), ((), ())),
            preferred_element_type=jnp.float32,
        )
    out_ref[...] = total.astype(jnp.bfloat16)


def query_kernel(place_ref, column_ref, gain_ref, *refs):
    head_pieces, pieces = refs[:NX], refs[NX : NX + NY * NC]
    query_ref, residual_ref, pairs_ref, w_ref = refs[NX + NY * NC :]
    width = w_ref.shape[1]
    features = pairs_ref.shape[0]
    slots = NZ * 16
    total = jnp.zeros(pairs_ref.shape, jnp.float32)
    for j, piece in enumerate(head_pieces):
        column = column_ref[j]
        for z in range(NZ):
            at = pl.multiple_of((z * NX + column) * 32, 32)
            w_ref[pl.ds(at, 16)] = piece[z, :16, :width]
            w_ref[pl.ds(pl.multiple_of(at + 16, 16), 16)] = piece[z, :16, width:]
        held = feature_slots(column, features // (NZ * NX), slots, 1)
        place = lax.broadcasted_iota(jnp.int32, (features, slots), 0) == held
        total = total + dot(place.astype(jnp.bfloat16), piece[:, 16:].reshape(slots, -1))
    pairs_ref[...] = total.astype(jnp.bfloat16)
    count = pieces[0].shape[0]
    own = pl.multiple_of(place_ref[0] * width, width)
    for i, piece in enumerate(pieces):
        at = pl.ds(pl.multiple_of(place_ref[i] * count, count), count)
        normed = rms_scale(piece[...], gain_ref[...]).astype(jnp.bfloat16)
        query_ref[at, :] = dot(normed, w_ref[...]).astype(jnp.bfloat16)
        residual_ref[at, :] = piece[:, pl.ds(own, width)]


def attention_kernel(place_ref, live_ref, query_ref, w_ref, *refs):
    pieces, out_ref, pair_ref = refs[:-2], refs[-2], refs[-1]
    width = query_ref.shape[1]
    total_rows = query_ref.shape[0]
    for i, piece in enumerate(pieces):
        pair_ref[i] = dot(piece[...], w_ref[...]).astype(jnp.bfloat16)
    out_ref[:SPAN] = jnp.zeros((SPAN, width), jnp.bfloat16)

    def one(i, carry):
        place = place_ref[i]
        first = pl.multiple_of(place * 2 * SPAN + SPAN, SPAN)
        second = pl.multiple_of(jnp.minimum(first + SPAN, total_rows - SPAN), SPAN)
        query = jnp.concatenate([query_ref[pl.ds(first, SPAN)], query_ref[pl.ds(second, SPAN)]])
        upper = lax.broadcasted_iota(jnp.int32, (2 * SPAN, PACK), 0) < SPAN
        in_first = lax.broadcasted_iota(jnp.int32, (2 * SPAN, PACK), 1) < live_ref[place]
        allowed = (upper & in_first) | jnp.logical_not(upper | in_first)
        heads = []
        for h in range(width // HD):
            cols = slice(h * HD, (h + 1) * HD)
            keys = pair_ref[i, :, cols]
            values = pair_ref[i, :, width + h * HD : width + (h + 1) * HD]
            scores = lax.dot_general(query[:, cols], keys, NT, preferred_element_type=jnp.float32)
            scores = jnp.where(allowed, scores * HD ** (-0.5), -jnp.inf)
            largest = jnp.max(scores, axis=-1, keepdims=True)
            powers = jnp.exp(scores - largest)
            totals = jnp.sum(powers, axis=-1, keepdims=True)
            weights = (powers / totals).astype(jnp.bfloat16)
            heads.append(dot(weights, values).astype(jnp.bfloat16))
        result = jnp.concatenate(heads, axis=1)
        out_ref[pl.ds(first, SPAN)] = result[:SPAN]

        @pl.when(place < NY * NC - 1)
        def _():
            out_ref[pl.ds(second, SPAN)] = result[SPAN:]

        return carry

    lax.fori_loop(0, len(pieces), one, 0)


def output_kernel(place_ref, column_ref, residual_ref, *refs):
    head_pieces, pieces = refs[:NX], refs[NX : NX + NY * NC]
    out_ref, w_ref = refs[NX + NY * NC :]
    width = pieces[0].shape[1]
    chunk = 256
    for j, piece in enumerate(head_pieces):
        for z in range(NZ):
            at = pl.multiple_of((z * NX + column_ref[j]) * 32, 32)
            w_ref[pl.ds(at, 32)] = piece[z]

    def one(step, carry):
        at = pl.ds(pl.multiple_of(step * chunk, chunk), chunk)
        total = residual_ref[at].astype(jnp.float32)
        for i, piece in enumerate(pieces):
            depth = pl.ds(pl.multiple_of(place_ref[i] * width, width), width)
            total = total + dot(piece[at], w_ref[depth])
        out_ref[at] = total.astype(jnp.bfloat16)
        return carry

    lax.fori_loop(0, out_ref.shape[0] // chunk, one, 0)


def pad_rows(a, rows):
    return jnp.pad(a, ((0, rows - a.shape[0]), (0, 0)))


def body(
    reader,
    reader_gain,
    database,
    encoder_gain,
    w_expand,
    w_reduce,
    w_query,
    w_key,
    w_value,
    w_output,
    neighbour_ids,
    lengths,
    owners,
):
    bf16 = jnp.bfloat16
    shards = NZ * NX
    seq_index = lax.axis_index("y") * NC + lax.axis_index("c")
    entries, stripe, features = database.shape
    per_row = neighbour_ids.shape[2]

    ids = lax.dynamic_index_in_dim(neighbour_ids, seq_index, 1, keepdims=False)
    token_row = (ids[:, :, None] * stripe + jnp.arange(stripe, dtype=jnp.int32)).reshape(-1)
    stored = database.reshape(entries * stripe, features)
    pick = (token_row[:, None] == jnp.arange(entries * stripe, dtype=jnp.int32)[None]).astype(bf16)
    outgoing = dot(pick, stored).astype(bf16).reshape(shards, per_row * stripe, features)
    arrived = exchange(outgoing, DB)
    arrived = arrived.reshape(shards * per_row * stripe, features)

    padded = 16
    ff_part = pad_rows(jnp.concatenate([w_expand, w_reduce.T], axis=1), padded)
    columns = natural_columns()
    ff_x = gather_x(spread(ff_part, "z", NZ))
    hidden_each = w_expand.shape[1]
    ff_t = call(
        arrange_kernel,
        jax.ShapeDtypeStruct((2 * hidden_each, features), bf16),
        [columns] + ff_x,
        1,
        4 * shards * padded * features * hidden_each,
    )
    ff_pieces = gather_seq(ff_t)

    _, width = w_query.shape
    key_value = pad_rows(jnp.concatenate([w_key, w_value], axis=1), padded)
    halves = jnp.concatenate([w_query[:padded], w_query[padded:]], axis=1)
    head_part = jnp.concatenate([halves, key_value], axis=0)
    head_x = gather_x(spread(head_part, "z", NZ))
    out_x = gather_x(spread(w_output, "z", NZ))

    row_pieces = gather_seq(reader[0])
    places = natural_places()
    seq_len = reader.shape[1] * NY * NC
    model = reader.shape[2]
    half_shape = jax.ShapeDtypeStruct((seq_len, width), bf16)
    queries, residual, w_pairs = call(
        query_kernel,
        (half_shape, half_shape, jax.ShapeDtypeStruct((features, 2 * width), bf16)),
        [places, columns, reader_gain.reshape(1, -1)] + head_x + row_pieces,
        2,
        2 * seq_len * model * width,
        [pltpu.VMEM((model, width), bf16)],
    )

    own_len = lax.dynamic_index_in_dim(lengths[0], seq_index, 0, keepdims=False)
    own_owner = lax.dynamic_index_in_dim(owners[0], seq_index, 0, keepdims=False)
    position = jnp.arange(PACK, dtype=jnp.int32)
    start = jnp.int32(0)
    source_row = jnp.zeros((PACK,), jnp.int32)
    for j in range(per_row):
        token = position - start
        inside = (token >= 0) & (token < own_len[j])
        shard = (own_owner[j] + token // stripe) % shards
        source = (shard * per_row + j) * stripe + token % stripe
        source_row = jnp.where(inside, source, source_row)
        start = start + own_len[j]
    slots = jnp.arange(arrived.shape[0], dtype=jnp.int32)
    packing = (source_row[:, None] == slots[None]).astype(bf16)
    live_rows = dot(packing, arrived).astype(bf16)

    encoded = call(
        feed_forward_kernel,
        jax.ShapeDtypeStruct((PACK, features), bf16),
        [live_rows, encoder_gain.reshape(1, -1)] + ff_pieces,
        0,
        4 * PACK * features * hidden_each * NY * NC,
    )
    encoded_pieces = gather_seq(encoded)
    first_live = lengths[0, :, 0] + lengths[0, :, 1]
    attended = call(
        attention_kernel,
        half_shape,
        [places, first_live, queries, w_pairs] + encoded_pieces,
        2,
        2 * PACK * NY * NC * features * 2 * width,
        [pltpu.VMEM((NY * NC, PACK, 2 * width), bf16)],
    )
    attended_pieces = gather_seq(attended)
    result = call(
        output_kernel,
        half_shape,
        [places, columns, residual] + out_x + attended_pieces,
        2,
        2 * seq_len * model * width,
        [pltpu.VMEM((model, width), bf16)],
    )
    return result[None]


def solution(mesh):
    fine = Mesh(mesh.devices.reshape(NZ, NX, NY, NC), ("z", "x", "y", "c"))
    in_specs = (
        P(DB, SEQ, None),
        P(),
        P(DB, None, None),
        P(),
        P(DB, SEQ),
        P(SEQ, DB),
        P(DB, SEQ),
        P(DB, SEQ),
        P(DB, SEQ),
        P(DB, SEQ),
        P(),
        P(DB, None, None),
        P(DB, None, None),
    )
    out_specs = P(DB, None, SEQ)
    return jax.shard_map(body, mesh=fine, in_specs=in_specs, out_specs=out_specs, check_vma=False)
```

time: 352 us -> 304 us (0.86)
  starting transfers between devices: 110 us -> 168 us
  local copies, waits for them, and re-layouts: 51.4 us -> 8.41 us
  Pallas kernels: 0 us -> 35.9 us
  matrix products: 36 us -> 2.79 us
  blocking collectives: 29.3 us -> 0 us
  other arithmetic: 27.2 us -> 8.4 us
  waiting for transfers between devices: 93.5 us -> 75.7 us
    ppermute x20 -> x37, starting transfers between devices: 74 us -> 121 us  [the longest x16 53.1 us: gather_seq(): return mine + [lax.ppermute(piece, 'c', swap) for piece in mine]]
    pallas_call x0 -> x5, Pallas kernels: none -> 35.9 us  [call(): pl.pallas_call(kernel, out_shape=out_shape, in_specs=[pl.BlockSpec(memory...]
    all_to_all x4, waiting for transfers between devices: 52.7 us -> 23.2 us  [exchange(): return lax.all_to_all(blocks, axis, split_axis=0, concat_axis=0, tiled=True)]
    all_to_all x1 -> x0, blocking collectives: 29.3 us -> none  [spread(): return lax.all_to_all(copies, axis, split_axis=0, concat_axis=0, tiled=True)]
    dot_general x6 -> x2, matrix products: 30.8 us -> 2.79 us  [dot(): return jnp.dot(a, b, preferred_element_type=jnp.float32)]
    concatenate x4 -> x0, local copies, waits for them, and re-layouts: 11.9 us -> none  [the longest x1 3.87 us: body(): ff_all = jnp.concatenate([ff_mine, ff_other], axis=0)]
    ppermute x20 -> x37, waiting for transfers between devices: 40.8 us -> 52.5 us  [the longest x9 32.6 us: gather_x(): lax.ppermute(part, 'x', [(i, (i + step) % NX) for i in range(NX)])]
    transpose x5 -> x0, local copies, waits for them, and re-layouts: 10.7 us -> none  [the longest x1 6.48 us: body(): att = jnp.swapaxes(att, 0, 1).reshape(att.shape[1], -1)]
  transfers between devices with their start and end apart: 24 -> 41, of which waited for: 13 -> 10; matrix products, arithmetic and copies ran while one was open for 16% -> 5% of each run, Pallas kernels for 0% -> 10%
where the time goes in v2:
time: 304 us; the launch traced here: 302 us
  starting transfers between devices  168 us (55%)
  waiting for transfers between devices  75.7 us (25%)
  Pallas kernels  35.9 us (12%)
  local copies, waits for them, and re-layouts  8.41 us (3%)
  other arithmetic  8.4 us (3%)
    ppermute x16, starting transfers between devices, gather_seq(): return mine + [lax.ppermute(piece, 'c', swap) for piece in mine]  53.1 us
    all_to_all x4, starting transfers between devices, exchange(): return lax.all_to_all(blocks, axis, split_axis=0, concat_axis=0, tiled=True)  46.7 us
    pallas_call x5, Pallas kernels, call(): pl.pallas_call(kernel, out_shape=out_shape, in_specs=[pl.BlockSpec(memory...  35.9 us
    ppermute x9, waiting for transfers between devices, gather_x(): lax.ppermute(part, 'x', [(i, (i + step) % NX) for i in range(NX)])  32.6 us
    ppermute x9, starting transfers between devices, gather_x(): lax.ppermute(part, 'x', [(i, (i + step) % NX) for i in range(NX)])  31.2 us
    all_to_all x4, waiting for transfers between devices, exchange(): return lax.all_to_all(blocks, axis, split_axis=0, concat_axis=0, tiled=True)  23.2 us
    ppermute x4, waiting for transfers between devices, gather_seq(): last = lax.ppermute(part, 'y', ring(1))  18.2 us
    ppermute x4, starting transfers between devices, gather_seq(): far = lax.ppermute(part, 'y', ring(2))  15.9 us
  transfers between devices with their start and end apart: 41, of which 10 were waited for; matrix products, arithmetic and copies ran while one was open for 5% of the time, Pallas kernels for 10%

profile of v2, /device:TPU:1, one launch (start us, length us, event | category | flops | bytes accessed | tf_op | source)
XLA Modules:
  0.0 302.0 jit_solution(2533158622908725198)
XLA Ops:
  0.0 0.8 fusion.9
  1.6 15.7 %all-to-all-start.3 = ((bf16[16,16,448]{2,1,0:T(8,128)(2,1)}), bf16[16,16,448]{2,1,0:T(8,128)(2,1)S(1)}, u32[]{:S(2)}, u32[]{:S(2)}) async-start(bf16[16,16,448]{2,1,0:T(8,128)(2,1)} %broadcast_in_dim.10), calls=%async_computation.3 | async-start | bytes 524288 | tf_op jit(solution)/shard_map/all_to_all | solution.py:33
  18.6 1.4 fusion
  20.0 11.1 %all-to-all-done.3.refs_0_ = bf16[16,16,448]{2,1,0:T(8,128)(2,1)S(1)} async-done(((bf16[16,16,448]{2,1,0:T(8,128)(2,1)}), bf16[16,16,448]{2,1,0:T(8,128)(2,1)S(1)}, u32[]{:S(2)}, u32[]{:S(2)}) %all-to-all-start.3) | async-done | bytes 229408 | tf_op jit(solution)/shard_map/all_to_all | solution.py:33
  31.1 13.7 %all-to-all-start.2 = ((bf16[64,8,896]{2,1,0:T(8,128)(2,1)}), bf16[64,8,896]{2,1,0:T(8,128)(2,1)S(1)}, u32[]{:S(2)}, u32[]{:S(2)}) async-start(bf16[64,8,896]{2,1,0:T(8,128)(2,1)} %fusion), calls=%async_computation.2 | async-start | bytes 1835008 | tf_op jit(solution)/shard_map/all_to_all | solution.py:33
  44.8 2.9 collective-permute-start.15
  47.8 4.3 %collective-permute-start.14 = (bf16[16,16,448]{2,1,0:T(8,128)(2,1)S(1)}, bf16[16,16,448]{2,1,0:T(8,128)(2,1)S(1)}, u32[]{:S(2)}, u32[]{:S(2)}) collective-permute-start(bf16[16,16,448]{2,1,0:T(8,128)(2,1)S(1)} %all-to-all-done.3.refs_0_), channel_id=1, source_target_pairs={{0,16},{8,24},{16,0},{24,8},{1,17},{9,25},{17,1},{25,9},{2,18},{10... | collective-permute-start | bytes 688136 | tf_op jit(solution)/shard_map/ppermute | solution.py:56
  52.1 3.1 %collective-permute-start.13 = (bf16[16,16,448]{2,1,0:T(8,128)(2,1)S(1)}, bf16[16,16,448]{2,1,0:T(8,128)(2,1)S(1)}, u32[]{:S(2)}, u32[]{:S(2)}) collective-permute-start(bf16[16,16,448]{2,1,0:T(8,128)(2,1)S(1)} %all-to-all-done.3.refs_0_), channel_id=1, source_target_pairs={{0,24},{8,0},{16,8},{24,16},{1,25},{9,1},{17,9},{25,17},{2,26},{10... | collective-permute-start | bytes 688136 | tf_op jit(solution)/shard_map/ppermute | solution.py:56
  55.8 8.7 %collective-permute-done.14.refs_2_ = bf16[16,16,448]{2,1,0:T(8,128)(2,1)S(1)} collective-permute-done((bf16[16,16,448]{2,1,0:T(8,128)(2,1)S(1)}, bf16[16,16,448]{2,1,0:T(8,128)(2,1)S(1)}, u32[]{:S(2)}, u32[]{:S(2)}) %collective-permute-start.14) | collective-permute-done | bytes 229408 | tf_op jit(solution)/shard_map/ppermute | solution.py:56
  64.4 2.6 collective-permute-done.13.refs_1_
  67.7 3.3 %shard_map.128.refs_0_ = bf16[448,896]{1,0:T(8,128)(2,1)} custom-call(s32[4]{0:T(128)} %and_select_fusion.column_ref, bf16[16,16,448]{2,1,0:T(8,128)(2,1)} %copy-done.17, bf16[16,16,448]{2,1,0:T(8,128)(2,1)} %copy-done.32, bf16[16,16,448]{2,1,0:T(8,128)(2,1)} %copy-done.31, bf16[16,16,448]{2,1,0:T(8,128)(2,1)} %copy-done.30), custom_call_target="tpu_custom_call" | custom-call | flops 822083584 | bytes 917520 | tf_op jit(solution)/shard_map/pallas_call | solution.py:74
  71.0 3.3 %collective-permute-start.18 = (bf16[448,896]{1,0:T(8,128)(2,1)}, bf16[448,896]{1,0:T(8,128)(2,1)}, u32[]{:S(2)}, u32[]{:S(2)}) collective-permute-start(bf16[448,896]{1,0:T(8,128)(2,1)} %shard_map.128.refs_0_), channel_id=1, source_target_pairs={{0,2},{2,4},{4,6},{6,0},{1,3},{3,5},{5,7},{7,1},{8,10},{10,12},{12... | collective-permute-start | bytes 2408456 | tf_op jit(solution)/shard_map/ppermute | solution.py:47
  74.3 4.5 %collective-permute-start.17 = (bf16[448,896]{1,0:T(8,128)(2,1)}, bf16[448,896]{1,0:T(8,128)(2,1)}, u32[]{:S(2)}, u32[]{:S(2)}) collective-permute-start(bf16[448,896]{1,0:T(8,128)(2,1)} %shard_map.128.refs_0_), channel_id=1, source_target_pairs={{0,4},{2,6},{4,0},{6,2},{1,5},{3,7},{5,1},{7,3},{8,12},{10,14},{12... | collective-permute-start | bytes 2408456 | tf_op jit(solution)/shard_map/ppermute | solution.py:48
  78.9 12.1 %all-to-all-done.2 = bf16[64,8,896]{2,1,0:T(8,128)(2,1)S(1)} async-done(((bf16[64,8,896]{2,1,0:T(8,128)(2,1)}), bf16[64,8,896]{2,1,0:T(8,128)(2,1)S(1)}, u32[]{:S(2)}, u32[]{:S(2)}) %all-to-all-start.2) | async-done | bytes 917536 | tf_op jit(solution)/shard_map/all_to_all | solution.py:33
  91.0 0.8 broadcast_in_dim.8
  91.8 5.8 %all-to-all-start = ((bf16[16,32,512]{2,1,0:T(8,128)(2,1)}), bf16[16,32,512]{2,1,0:T(8,128)(2,1)S(1)}, u32[]{:S(2)}, u32[]{:S(2)}) async-start(bf16[16,32,512]{2,1,0:T(8,128)(2,1)} %broadcast_in_dim.8), calls=%async_computation | async-start | bytes 1048576 | tf_op jit(solution)/shard_map/all_to_all | solution.py:33
  97.6 3.2 %collective-permute-start.5 = (bf16[128,2048]{1,0:T(8,128)(2,1)S(1)}, bf16[128,2048]{1,0:T(8,128)(2,1)S(1)}, u32[]{:S(2)}, u32[]{:S(2)}) collective-permute-start(bf16[128,2048]{1,0:T(8,128)(2,1)S(1)} %bitcast.23), channel_id=1, source_target_pairs={{0,2},{2,4},{4,6},{6,0},{1,3},{3,5},{5,7},{7,1},{8,10},{10,12},{12... | collective-permute-start | bytes 1572872 | tf_op jit(solution)/shard_map/ppermute | solution.py:47
  100.8 3.4 %collective-permute-start.16 = (bf16[448,896]{1,0:T(8,128)(2,1)}, bf16[448,896]{1,0:T(8,128)(2,1)}, u32[]{:S(2)}, u32[]{:S(2)}) collective-permute-start(bf16[448,896]{1,0:T(8,128)(2,1)} %shard_map.128.refs_0_), channel_id=1, source_target_pairs={{0,6},{2,0},{4,2},{6,4},{1,7},{3,1},{5,3},{7,5},{8,14},{10,8},{12,... | collective-permute-start | bytes 2408456 | tf_op jit(solution)/shard_map/ppermute | solution.py:46
  104.2 3.5 %collective-permute-start.4 = (bf16[128,2048]{1,0:T(8,128)(2,1)S(1)}, bf16[128,2048]{1,0:T(8,128)(2,1)S(1)}, u32[]{:S(2)}, u32[]{:S(2)}) collective-permute-start(bf16[128,2048]{1,0:T(8,128)(2,1)S(1)} %bitcast.24), channel_id=1, source_target_pairs={{0,4},{2,6},{4,0},{6,2},{1,5},{3,7},{5,1},{7,3},{8,12},{10,14},{12... | collective-permute-start | bytes 1572872 | tf_op jit(solution)/shard_map/ppermute | solution.py:48
  107.8 18.2 %collective-permute-done.5.refs_7_ = bf16[128,2048]{1,0:T(8,128)(2,1)S(1)} collective-permute-done((bf16[128,2048]{1,0:T(8,128)(2,1)S(1)}, bf16[128,2048]{1,0:T(8,128)(2,1)S(1)}, u32[]{:S(2)}, u32[]{:S(2)}) %collective-permute-start.5) | collective-permute-done | bytes 524320 | tf_op jit(solution)/shard_map/ppermute | solution.py:47
  126.0 2.5 collective-permute-start.19
  128.5 1.9 collective-permute-start.22
  130.4 2.4 collective-permute-start.21
  133.0 2.1 collective-permute-start.3
  135.2 5.9 %collective-permute-start.20 = (bf16[448,896]{1,0:T(8,128)(2,1)}, bf16[448,896]{1,0:T(8,128)(2,1)}, u32[]{:S(2)}, u32[]{:S(2)}) collective-permute-start(bf16[448,896]{1,0:T(8,128)(2,1)} %collective-permute-done.16.refs_1_), channel_id=1, source_target_pairs={{0,1},{1,0},{2,3},{3,2},{4,5},{5,4},{6,7},{7,6},{8,9},{9,8},{10,11... | collective-permute-start | bytes 2408456 | tf_op jit(solution)/shard_map/ppermute | solution.py:50
  144.3 1.4 collective-permute-done.3.refs_5_
  145.8 5.4 %collective-permute-start.6 = (bf16[128,2048]{1,0:T(8,128)(2,1)S(1)}, bf16[128,2048]{1,0:T(8,128)(2,1)}, u32[]{:S(2)}, u32[]{:S(2)}) collective-permute-start(bf16[128,2048]{1,0:T(8,128)(2,1)S(1)} %bitcast.26), channel_id=1, source_target_pairs={{0,1},{1,0},{2,3},{3,2},{4,5},{5,4},{6,7},{7,6},{8,9},{9,8},{10,11... | collective-permute-start | bytes 1572872 | tf_op jit(solution)/shard_map/ppermute | solution.py:50
  151.2 1.9 collective-permute-start.9
  153.1 2.4 collective-permute-start.8
  155.5 1.9 collective-permute-start.7
  157.5 5.0 %fusion.20 = s32[320]{0:T(512)S(1)} fusion(s32[]{:T(128)} %bitcast.10, s32[]{:T(128)} %bitcast.9, s32[]{:T(128)} %bitcast.4, s32[]{:T(128)} %bitcast.3, s32[]{:T(128)} %bitcast.8, s32[]{:T(128)} %bitcast.5, s32[]{:T(128)S(6)} %add.268, s32[]{:T(128)} %bitcast.7, s32[]{:T(128)} %bitcast.6, s32[]{:T(128)S(6)} %add.269), kind=kLoop, calls=%fused_computation.63 | loop fusion | flops 47360 | bytes 1320 | tf_op jit(solution)/shard_map/jit(_where)/select_n | solution.py:290
  163.1 1.4 convolution_convert_fusion.1.rows_ref
  164.5 5.8 %collective-permute-start.2 = (bf16[16,32,512]{2,1,0:T(8,128)(2,1)S(1)}, bf16[16,32,512]{2,1,0:T(8,128)(2,1)S(1)}, u32[]{:S(2)}, u32[]{:S(2)}) collective-permute-start(bf16[16,32,512]{2,1,0:T(8,128)(2,1)S(1)} %all-to-all-done.refs_0_), channel_id=1, source_target_pairs={{0,8},{8,16},{16,24},{24,0},{1,9},{9,17},{17,25},{25,1},{2,10},{10... | collective-permute-start | bytes 1572872 | tf_op jit(solution)/shard_map/ppermute | solution.py:56
  170.3 7.3 %shard_map.129.refs_0_ = bf16[320,896]{1,0:T(8,128)(2,1)} custom-call(bf16[320,896]{1,0:T(8,128)(2,1)} %convolution_convert_fusion.1.rows_ref, f32[1,896]{1,0:T(1,128)} %reshape.248.gain_ref, bf16[448,896]{1,0:T(8,128)(2,1)} %shard_map.128.refs_0_, bf16[448,896]{1,0:T(8,128)(2,1)} %collective-permute-done.16.refs_1_, ...), custom_call_target="tpu_custom_call" | custom-call | flops 2055208960 | bytes 6999552 | tf_op jit(solution)/shard_map/pallas_call | solution.py:74
  177.6 1.9 collective-permute-start.25
  179.6 4.3 %collective-permute-start.24 = (bf16[320,896]{1,0:T(8,128)(2,1)}, bf16[320,896]{1,0:T(8,128)(2,1)}, u32[]{:S(2)}, u32[]{:S(2)}) collective-permute-start(bf16[320,896]{1,0:T(8,128)(2,1)} %shard_map.129.refs_0_), channel_id=1, source_target_pairs={{0,4},{2,6},{4,0},{6,2},{1,5},{3,7},{5,1},{7,3},{8,12},{10,14},{12... | collective-permute-start | bytes 1720328 | tf_op jit(solution)/shard_map/ppermute | solution.py:48
  183.9 2.2 collective-permute-start.23
  186.1 3.9 %collective-permute-start.1 = (bf16[16,32,512]{2,1,0:T(8,128)(2,1)S(1)}, bf16[16,32,512]{2,1,0:T(8,128)(2,1)S(1)}, u32[]{:S(2)}, u32[]{:S(2)}) collective-permute-start(bf16[16,32,512]{2,1,0:T(8,128)(2,1)S(1)} %all-to-all-done.refs_0_), channel_id=1, source_target_pairs={{0,16},{8,24},{16,0},{24,8},{1,17},{9,25},{17,1},{25,9},{2,18},{10... | collective-permute-start | bytes 1572872 | tf_op jit(solution)/shard_map/ppermute | solution.py:56
  190.1 2.3 collective-permute-start
  192.4 9.3 %collective-permute-done.1.refs_2_ = bf16[16,32,512]{2,1,0:T(8,128)(2,1)S(1)} collective-permute-done((bf16[16,32,512]{2,1,0:T(8,128)(2,1)S(1)}, bf16[16,32,512]{2,1,0:T(8,128)(2,1)S(1)}, u32[]{:S(2)}, u32[]{:S(2)}) %collective-permute-start.1) | collective-permute-done | bytes 524320 | tf_op jit(solution)/shard_map/ppermute | solution.py:56
  201.7 4.0 %collective-permute-start.26 = (bf16[320,896]{1,0:T(8,128)(2,1)}, bf16[320,896]{1,0:T(8,128)(2,1)S(1)}, u32[]{:S(2)}, u32[]{:S(2)}) collective-permute-start(bf16[320,896]{1,0:T(8,128)(2,1)} %shard_map.129.refs_0_), channel_id=1, source_target_pairs={{0,1},{1,0},{2,3},{3,2},{4,5},{5,4},{6,7},{7,6},{8,9},{9,8},{10,11... | collective-permute-start | bytes 1720328 | tf_op jit(solution)/shard_map/ppermute | solution.py:50
  205.7 4.9 %collective-permute-start.29 = (bf16[320,896]{1,0:T(8,128)(2,1)}, bf16[320,896]{1,0:T(8,128)(2,1)}, u32[]{:S(2)}, u32[]{:S(2)}) collective-permute-start(bf16[320,896]{1,0:T(8,128)(2,1)} %collective-permute-done.25.refs_3_), channel_id=1, source_target_pairs={{0,1},{1,0},{2,3},{3,2},{4,5},{5,4},{6,7},{7,6},{8,9},{9,8},{10,11... | collective-permute-start | bytes 1720328 | tf_op jit(solution)/shard_map/ppermute | solution.py:50
  210.6 1.9 collective-permute-start.28
  212.6 2.4 collective-permute-start.27
  215.0 0.7 broadcast_in_dim.9
  215.7 11.5 %all-to-all-start.1 = ((bf16[16,32,256]{2,1,0:T(8,128)(2,1)}), bf16[16,32,256]{2,1,0:T(8,128)(2,1)S(1)}, u32[]{:S(2)}, u32[]{:S(2)}) async-start(bf16[16,32,256]{2,1,0:T(8,128)(2,1)} %broadcast_in_dim.9), calls=%async_computation.1 | async-start | bytes 524288 | tf_op jit(solution)/shard_map/all_to_all | solution.py:33
  228.5 0.8 copy-done.11
  229.3 7.0 %shard_map.127 = (bf16[1024,256]{1,0:T(8,128)(2,1)}, bf16[1024,256]{1,0:T(8,128)(2,1)}, bf16[896,512]{1,0:T(8,128)(2,1)}) custom-call(s32[8]{0:T(128)} %pad_add_fusion.place_ref, s32[4]{0:T(128)} %and_select_fusion.column_ref, f32[1,2048]{1,0:T(1,128)} %bitcast.27, bf16[16,32,512]{2,1,0:T(8,128)(2,1)} %copy-done, bf16[16,32,512]{2,1,0:T(8,128)(2,1)} %copy-done.11, ...), custom_call_target="tpu_custom_call" | custom-call | flops 1073741824 | bytes 6299696 | tf_op jit(solution)/shard_map/pallas_call | solution.py:74
  236.3 0.8 copy-done.29
  237.1 13.1 %shard_map.130.refs_4_ = bf16[1024,256]{1,0:T(8,128)(2,1)} custom-call(s32[8]{0:T(128)} %pad_add_fusion.place_ref, s32[8]{0:T(128)} %add_bitcast_fusion.live_ref, bf16[1024,256]{1,0:T(8,128)(2,1)} %get-tuple-element.9.query_ref, bf16[896,512]{1,0:T(8,128)(2,1)} %get-tuple-element.10.w_ref, bf16[320,896]{1,0:T(8,128)(2,1)} %shard_map.129.refs_0_, ...), custom_call_target="tpu_custom_call" | custom-call | flops 2348810240 | bytes 6029376 | tf_op jit(solution)/shard_map/pallas_call | solution.py:74
  250.2 1.9 collective-permute-start.32
  252.2 3.5 %collective-permute-start.31 = (bf16[1024,256]{1,0:T(8,128)(2,1)}, bf16[1024,256]{1,0:T(8,128)(2,1)S(1)}, u32[]{:S(2)}, u32[]{:S(2)}) collective-permute-start(bf16[1024,256]{1,0:T(8,128)(2,1)} %shard_map.130.refs_4_), channel_id=1, source_target_pairs={{0,4},{2,6},{4,0},{6,2},{1,5},{3,7},{5,1},{7,3},{8,12},{10,14},{12... | collective-permute-start | bytes 1572872 | tf_op jit(solution)/shard_map/ppermute | solution.py:48
  255.7 3.0 collective-permute-start.30
  258.7 2.5 collective-permute-start.12
  261.2 3.7 %collective-permute-start.11 = (bf16[16,32,256]{2,1,0:T(8,128)(2,1)S(1)}, bf16[16,32,256]{2,1,0:T(8,128)(2,1)S(1)}, u32[]{:S(2)}, u32[]{:S(2)}) collective-permute-start(bf16[16,32,256]{2,1,0:T(8,128)(2,1)S(1)} %all-to-all-done.1.refs_0_), channel_id=1, source_target_pairs={{0,16},{8,24},{16,0},{24,8},{1,17},{9,25},{17,1},{25,9},{2,18},{10... | collective-permute-start | bytes 786440 | tf_op jit(solution)/shard_map/ppermute | solution.py:56
  265.0 4.8 %collective-permute-done.12.refs_3_ = bf16[16,32,256]{2,1,0:T(8,128)(2,1)S(1)} collective-permute-done((bf16[16,32,256]{2,1,0:T(8,128)(2,1)S(1)}, bf16[16,32,256]{2,1,0:T(8,128)(2,1)S(1)}, u32[]{:S(2)}, u32[]{:S(2)}) %collective-permute-start.12) | collective-permute-done | bytes 262176 | tf_op jit(solution)/shard_map/ppermute | solution.py:56
  269.8 8.2 %collective-permute-start.33 = (bf16[1024,256]{1,0:T(8,128)(2,1)}, bf16[1024,256]{1,0:T(8,128)(2,1)S(1)}, u32[]{:S(2)}, u32[]{:S(2)}) collective-permute-start(bf16[1024,256]{1,0:T(8,128)(2,1)} %shard_map.130.refs_4_), channel_id=1, source_target_pairs={{0,1},{1,0},{2,3},{3,2},{4,5},{5,4},{6,7},{7,6},{8,9},{9,8},{10,11... | collective-permute-start | bytes 1572872 | tf_op jit(solution)/shard_map/ppermute | solution.py:50
  278.1 3.0 collective-permute-start.36
  281.1 1.9 collective-permute-start.35
  283.0 2.4 collective-permute-start.34
  285.4 2.6 collective-permute-start.10
  288.0 7.2 %collective-permute-done.10.refs_1_ = bf16[16,32,256]{2,1,0:T(8,128)(2,1)S(1)} collective-permute-done((bf16[16,32,256]{2,1,0:T(8,128)(2,1)S(1)}, bf16[16,32,256]{2,1,0:T(8,128)(2,1)S(1)}, u32[]{:S(2)}, u32[]{:S(2)}) %collective-permute-start.10) | collective-permute-done | bytes 262176 | tf_op jit(solution)/shard_map/ppermute | solution.py:56
  295.9 0.8 copy-done.15
  296.7 5.3 %shard_map.131 = bf16[1024,256]{1,0:T(8,128)(2,1)} custom-call(s32[8]{0:T(128)} %pad_add_fusion.place_ref, s32[4]{0:T(128)} %and_select_fusion.column_ref, bf16[1024,256]{1,0:T(8,128)(2,1)} %get-tuple-element.8.residual_ref, bf16[16,32,256]{2,1,0:T(8,128)(2,1)} %copy-done.1, bf16[16,32,256]{2,1,0:T(8,128)(2,1)} %copy-done.20, ...), custom_call_target="tpu_custom_call" | custom-call | flops 1073741824 | bytes 5767216 | tf_op jit(solution)/shard_map/pallas_call | solution.py:74
  (112 shorter events, 7.3 us)
Async XLA Ops:
  0.0 18.4 %copy-start.16 = (bf16[128,2,896]{2,1,0:T(2,128)(2,1)S(1)}, bf16[128,2,896]{2,1,0:T(2,128)(2,1)}, u32[]{:S(2)}) copy-start(bf16[128,2,896]{2,1,0:T(2,128)(2,1)} %param.15) | copy-start | bytes 1376260
  1.6 29.5 %all-to-all-start.3 = ((bf16[16,16,448]{2,1,0:T(8,128)(2,1)}), bf16[16,16,448]{2,1,0:T(8,128)(2,1)S(1)}, u32[]{:S(2)}, u32[]{:S(2)}) async-start(bf16[16,16,448]{2,1,0:T(8,128)(2,1)} %broadcast_in_dim.10), calls=%async_computation.3 | async-start | bytes 524288 | tf_op jit(solution)/shard_map/all_to_all | solution.py:33
  20.0 24.8 %copy-start.23 = (bf16[14,256]{1,0:T(8,128)(2,1)S(1)}, bf16[14,256]{1,0:T(8,128)(2,1)}, u32[]{:S(2)}) copy-start(bf16[14,256]{1,0:T(8,128)(2,1)} %param.21) | copy-start | bytes 21508
  20.0 24.8 %copy-start.24 = (bf16[14,256]{1,0:T(8,128)(2,1)S(1)}, bf16[14,256]{1,0:T(8,128)(2,1)}, u32[]{:S(2)}) copy-start(bf16[14,256]{1,0:T(8,128)(2,1)} %param.20) | copy-start | bytes 21508
  20.0 35.7 %copy-start.22 = (bf16[32,256]{1,0:T(8,128)(2,1)S(1)}, bf16[32,256]{1,0:T(8,128)(2,1)}, u32[]{:S(2)}) copy-start(bf16[32,256]{1,0:T(8,128)(2,1)} %param.19) | copy-start | bytes 49156
  31.1 21.0 %copy-start.17 = (bf16[16,16,448]{2,1,0:T(8,128)(2,1)}, bf16[16,16,448]{2,1,0:T(8,128)(2,1)S(1)}, u32[]{:S(2)}) copy-start(bf16[16,16,448]{2,1,0:T(8,128)(2,1)S(1)} %all-to-all-done.3.refs_0_) | copy-start | bytes 688132
  31.1 59.9 %all-to-all-start.2 = ((bf16[64,8,896]{2,1,0:T(8,128)(2,1)}), bf16[64,8,896]{2,1,0:T(8,128)(2,1)S(1)}, u32[]{:S(2)}, u32[]{:S(2)}) async-start(bf16[64,8,896]{2,1,0:T(8,128)(2,1)} %fusion), calls=%async_computation.2 | async-start | bytes 1835008 | tf_op jit(solution)/shard_map/all_to_all | solution.py:33
  44.8 10.9 %collective-permute-start.15 = (bf16[16,16,448]{2,1,0:T(8,128)(2,1)S(1)}, bf16[16,16,448]{2,1,0:T(8,128)(2,1)S(1)}, u32[]{:S(2)}, u32[]{:S(2)}) collective-permute-start(bf16[16,16,448]{2,1,0:T(8,128)(2,1)S(1)} %all-to-all-done.3.refs_0_), channel_id=1, source_target_pairs={{0,8},{8,16},{16,24},{24,0},{1,9},{9,17},{17,25},{25,1},{2,10},{10... | collective-permute-start | bytes 688136 | tf_op jit(solution)/shard_map/ppermute | solution.py:56
  47.8 16.7 %collective-permute-start.14 = (bf16[16,16,448]{2,1,0:T(8,128)(2,1)S(1)}, bf16[16,16,448]{2,1,0:T(8,128)(2,1)S(1)}, u32[]{:S(2)}, u32[]{:S(2)}) collective-permute-start(bf16[16,16,448]{2,1,0:T(8,128)(2,1)S(1)} %all-to-all-done.3.refs_0_), channel_id=1, source_target_pairs={{0,16},{8,24},{16,0},{24,8},{1,17},{9,25},{17,1},{25,9},{2,18},{10... | collective-permute-start | bytes 688136 | tf_op jit(solution)/shard_map/ppermute | solution.py:56
  52.1 14.9 %collective-permute-start.13 = (bf16[16,16,448]{2,1,0:T(8,128)(2,1)S(1)}, bf16[16,16,448]{2,1,0:T(8,128)(2,1)S(1)}, u32[]{:S(2)}, u32[]{:S(2)}) collective-permute-start(bf16[16,16,448]{2,1,0:T(8,128)(2,1)S(1)} %all-to-all-done.3.refs_0_), channel_id=1, source_target_pairs={{0,24},{8,0},{16,8},{24,16},{1,25},{9,1},{17,9},{25,17},{2,26},{10... | collective-permute-start | bytes 688136 | tf_op jit(solution)/shard_map/ppermute | solution.py:56
  55.8 11.2 %copy-start.30 = (bf16[16,16,448]{2,1,0:T(8,128)(2,1)}, bf16[16,16,448]{2,1,0:T(8,128)(2,1)S(1)}, u32[]{:S(2)}) copy-start(bf16[16,16,448]{2,1,0:T(8,128)(2,1)S(1)} %collective-permute-done.15.refs_3_) | copy-start | bytes 688132
  70.9 26.7 %copy-start.2 = (bf16[1,128,2048]{2,1,0:T(8,128)(2,1)S(1)}, bf16[1,128,2048]{2,1,0:T(8,128)(2,1)}, u32[]{:S(2)}) copy-start(bf16[1,128,2048]{2,1,0:T(8,128)(2,1)} %param.13) | copy-start | bytes 1572868
  70.9 70.2 %copy-start.26 = (s32[1,8,4]{1,2,0:T(4,128)S(1)}, s32[1,8,4]{1,2,0:T(4,128)}, u32[]{:S(2)}) copy-start(s32[1,8,4]{1,2,0:T(4,128)} %param.25) | copy-start | bytes 388
  70.9 70.2 %copy-start.27 = (s32[1,8,4]{1,2,0:T(4,128)S(1)}, s32[1,8,4]{1,2,0:T(4,128)}, u32[]{:S(2)}) copy-start(s32[1,8,4]{1,2,0:T(4,128)} %param.24) | copy-start | bytes 388
  70.9 91.5 %copy-start.25 = (f32[896]{0:T(1024)S(1)}, f32[896]{0:T(1024)}, u32[]{:S(2)}) copy-start(f32[896]{0:T(1024)} %param.16) | copy-start | bytes 10756
  71.0 57.5 %collective-permute-start.18 = (bf16[448,896]{1,0:T(8,128)(2,1)}, bf16[448,896]{1,0:T(8,128)(2,1)}, u32[]{:S(2)}, u32[]{:S(2)}) collective-permute-start(bf16[448,896]{1,0:T(8,128)(2,1)} %shard_map.128.refs_0_), channel_id=1, source_target_pairs={{0,2},{2,4},{4,6},{6,0},{1,3},{3,5},{5,7},{7,1},{8,10},{10,12},{12... | collective-permute-start | bytes 2408456 | tf_op jit(solution)/shard_map/ppermute | solution.py:47
  74.3 56.1 %collective-permute-start.17 = (bf16[448,896]{1,0:T(8,128)(2,1)}, bf16[448,896]{1,0:T(8,128)(2,1)}, u32[]{:S(2)}, u32[]{:S(2)}) collective-permute-start(bf16[448,896]{1,0:T(8,128)(2,1)} %shard_map.128.refs_0_), channel_id=1, source_target_pairs={{0,4},{2,6},{4,0},{6,2},{1,5},{3,7},{5,1},{7,3},{8,12},{10,14},{12... | collective-permute-start | bytes 2408456 | tf_op jit(solution)/shard_map/ppermute | solution.py:48
  91.8 72.6 %all-to-all-start = ((bf16[16,32,512]{2,1,0:T(8,128)(2,1)}), bf16[16,32,512]{2,1,0:T(8,128)(2,1)S(1)}, u32[]{:S(2)}, u32[]{:S(2)}) async-start(bf16[16,32,512]{2,1,0:T(8,128)(2,1)} %broadcast_in_dim.8), calls=%async_computation | async-start | bytes 1048576 | tf_op jit(solution)/shard_map/all_to_all | solution.py:33
  97.6 28.4 %collective-permute-start.5 = (bf16[128,2048]{1,0:T(8,128)(2,1)S(1)}, bf16[128,2048]{1,0:T(8,128)(2,1)S(1)}, u32[]{:S(2)}, u32[]{:S(2)}) collective-permute-start(bf16[128,2048]{1,0:T(8,128)(2,1)S(1)} %bitcast.23), channel_id=1, source_target_pairs={{0,2},{2,4},{4,6},{6,0},{1,3},{3,5},{5,7},{7,1},{8,10},{10,12},{12... | collective-permute-start | bytes 1572872 | tf_op jit(solution)/shard_map/ppermute | solution.py:47
  100.8 34.3 %collective-permute-start.16 = (bf16[448,896]{1,0:T(8,128)(2,1)}, bf16[448,896]{1,0:T(8,128)(2,1)}, u32[]{:S(2)}, u32[]{:S(2)}) collective-permute-start(bf16[448,896]{1,0:T(8,128)(2,1)} %shard_map.128.refs_0_), channel_id=1, source_target_pairs={{0,6},{2,0},{4,2},{6,4},{1,7},{3,1},{5,3},{7,5},{8,14},{10,8},{12,... | collective-permute-start | bytes 2408456 | tf_op jit(solution)/shard_map/ppermute | solution.py:46
  104.2 28.8 %collective-permute-start.4 = (bf16[128,2048]{1,0:T(8,128)(2,1)S(1)}, bf16[128,2048]{1,0:T(8,128)(2,1)S(1)}, u32[]{:S(2)}, u32[]{:S(2)}) collective-permute-start(bf16[128,2048]{1,0:T(8,128)(2,1)S(1)} %bitcast.24), channel_id=1, source_target_pairs={{0,4},{2,6},{4,0},{6,2},{1,5},{3,7},{5,1},{7,3},{8,12},{10,14},{12... | collective-permute-start | bytes 1572872 | tf_op jit(solution)/shard_map/ppermute | solution.py:48
  126.0 51.6 %copy-start.3 = (bf16[128,2048]{1,0:T(8,128)(2,1)}, bf16[128,2048]{1,0:T(8,128)(2,1)S(1)}, u32[]{:S(2)}) copy-start(bf16[128,2048]{1,0:T(8,128)(2,1)S(1)} %collective-permute-done.5.refs_7_) | copy-start | bytes 1572868
  126.0 25.2 %collective-permute-start.19 = (bf16[448,896]{1,0:T(8,128)(2,1)}, bf16[448,896]{1,0:T(8,128)(2,1)}, u32[]{:S(2)}, u32[]{:S(2)}) collective-permute-start(bf16[448,896]{1,0:T(8,128)(2,1)} %shard_map.128.refs_0_), channel_id=1, source_target_pairs={{0,1},{1,0},{2,3},{3,2},{4,5},{5,4},{6,7},{7,6},{8,9},{9,8},{10,11... | collective-permute-start | bytes 2408456 | tf_op jit(solution)/shard_map/ppermute | solution.py:50
  128.5 24.6 %collective-permute-start.22 = (bf16[448,896]{1,0:T(8,128)(2,1)}, bf16[448,896]{1,0:T(8,128)(2,1)}, u32[]{:S(2)}, u32[]{:S(2)}) collective-permute-start(bf16[448,896]{1,0:T(8,128)(2,1)} %collective-permute-done.18.refs_3_), channel_id=1, source_target_pairs={{0,1},{1,0},{2,3},{3,2},{4,5},{5,4},{6,7},{7,6},{8,9},{9,8},{10,11... | collective-permute-start | bytes 2408456 | tf_op jit(solution)/shard_map/ppermute | solution.py:50
  130.4 25.1 %collective-permute-start.21 = (bf16[448,896]{1,0:T(8,128)(2,1)}, bf16[448,896]{1,0:T(8,128)(2,1)}, u32[]{:S(2)}, u32[]{:S(2)}) collective-permute-start(bf16[448,896]{1,0:T(8,128)(2,1)} %collective-permute-done.17.refs_2_), channel_id=1, source_target_pairs={{0,1},{1,0},{2,3},{3,2},{4,5},{5,4},{6,7},{7,6},{8,9},{9,8},{10,11... | collective-permute-start | bytes 2408456 | tf_op jit(solution)/shard_map/ppermute | solution.py:50
  133.0 44.6 %copy-start.4 = (bf16[128,2048]{1,0:T(8,128)(2,1)}, bf16[128,2048]{1,0:T(8,128)(2,1)S(1)}, u32[]{:S(2)}) copy-start(bf16[128,2048]{1,0:T(8,128)(2,1)S(1)} %collective-permute-done.4.refs_6_) | copy-start | bytes 1572868
  133.0 12.7 %collective-permute-start.3 = (bf16[128,2048]{1,0:T(8,128)(2,1)S(1)}, bf16[128,2048]{1,0:T(8,128)(2,1)S(1)}, u32[]{:S(2)}, u32[]{:S(2)}) collective-permute-start(bf16[128,2048]{1,0:T(8,128)(2,1)S(1)} %bitcast.25), channel_id=1, source_target_pairs={{0,6},{2,0},{4,2},{6,4},{1,7},{3,1},{5,3},{7,5},{8,14},{10,8},{12,... | collective-permute-start | bytes 1572872 | tf_op jit(solution)/shard_map/ppermute | solution.py:46
  135.2 29.3 %collective-permute-start.20 = (bf16[448,896]{1,0:T(8,128)(2,1)}, bf16[448,896]{1,0:T(8,128)(2,1)}, u32[]{:S(2)}, u32[]{:S(2)}) collective-permute-start(bf16[448,896]{1,0:T(8,128)(2,1)} %collective-permute-done.16.refs_1_), channel_id=1, source_target_pairs={{0,1},{1,0},{2,3},{3,2},{4,5},{5,4},{6,7},{7,6},{8,9},{9,8},{10,11... | collective-permute-start | bytes 2408456 | tf_op jit(solution)/shard_map/ppermute | solution.py:50
  145.8 31.8 %copy-start.5 = (bf16[128,2048]{1,0:T(8,128)(2,1)}, bf16[128,2048]{1,0:T(8,128)(2,1)S(1)}, u32[]{:S(2)}) copy-start(bf16[128,2048]{1,0:T(8,128)(2,1)S(1)} %collective-permute-done.3.refs_5_) | copy-start | bytes 1572868
  145.8 31.8 %collective-permute-start.6 = (bf16[128,2048]{1,0:T(8,128)(2,1)S(1)}, bf16[128,2048]{1,0:T(8,128)(2,1)}, u32[]{:S(2)}, u32[]{:S(2)}) collective-permute-start(bf16[128,2048]{1,0:T(8,128)(2,1)S(1)} %bitcast.26), channel_id=1, source_target_pairs={{0,1},{1,0},{2,3},{3,2},{4,5},{5,4},{6,7},{7,6},{8,9},{9,8},{10,11... | collective-permute-start | bytes 1572872 | tf_op jit(solution)/shard_map/ppermute | solution.py:50
  151.2 28.4 %collective-permute-start.9 = (bf16[128,2048]{1,0:T(8,128)(2,1)S(1)}, bf16[128,2048]{1,0:T(8,128)(2,1)}, u32[]{:S(2)}, u32[]{:S(2)}) collective-permute-start(bf16[128,2048]{1,0:T(8,128)(2,1)S(1)} %collective-permute-done.5.refs_7_), channel_id=1, source_target_pairs={{0,1},{1,0},{2,3},{3,2},{4,5},{5,4},{6,7},{7,6},{8,9},{9,8},{10,11... | collective-permute-start | bytes 1572872 | tf_op jit(solution)/shard_map/ppermute | solution.py:50
  153.1 30.8 %collective-permute-start.8 = (bf16[128,2048]{1,0:T(8,128)(2,1)S(1)}, bf16[128,2048]{1,0:T(8,128)(2,1)}, u32[]{:S(2)}, u32[]{:S(2)}) collective-permute-start(bf16[128,2048]{1,0:T(8,128)(2,1)S(1)} %collective-permute-done.4.refs_6_), channel_id=1, source_target_pairs={{0,1},{1,0},{2,3},{3,2},{4,5},{5,4},{6,7},{7,6},{8,9},{9,8},{10,11... | collective-permute-start | bytes 1572872 | tf_op jit(solution)/shard_map/ppermute | solution.py:50
  155.5 30.5 %collective-permute-start.7 = (bf16[128,2048]{1,0:T(8,128)(2,1)S(1)}, bf16[128,2048]{1,0:T(8,128)(2,1)}, u32[]{:S(2)}, u32[]{:S(2)}) collective-permute-start(bf16[128,2048]{1,0:T(8,128)(2,1)S(1)} %collective-permute-done.3.refs_5_), channel_id=1, source_target_pairs={{0,1},{1,0},{2,3},{3,2},{4,5},{5,4},{6,7},{7,6},{8,9},{9,8},{10,11... | collective-permute-start | bytes 1572872 | tf_op jit(solution)/shard_map/ppermute | solution.py:50
  164.5 50.5 %copy-start.21 = (bf16[32,256]{1,0:T(8,128)(2,1)S(1)}, bf16[32,256]{1,0:T(8,128)(2,1)}, u32[]{:S(2)}) copy-start(bf16[32,256]{1,0:T(8,128)(2,1)} %param.22) | copy-start | bytes 49156
  164.5 25.6 %copy-start = (bf16[16,32,512]{2,1,0:T(8,128)(2,1)}, bf16[16,32,512]{2,1,0:T(8,128)(2,1)S(1)}, u32[]{:S(2)}) copy-start(bf16[16,32,512]{2,1,0:T(8,128)(2,1)S(1)} %all-to-all-done.refs_0_) | copy-start | bytes 1572868
  164.5 25.6 %collective-permute-start.2 = (bf16[16,32,512]{2,1,0:T(8,128)(2,1)S(1)}, bf16[16,32,512]{2,1,0:T(8,128)(2,1)S(1)}, u32[]{:S(2)}, u32[]{:S(2)}) collective-permute-start(bf16[16,32,512]{2,1,0:T(8,128)(2,1)S(1)} %all-to-all-done.refs_0_), channel_id=1, source_target_pairs={{0,8},{8,16},{16,24},{24,0},{1,9},{9,17},{17,25},{25,1},{2,10},{10... | collective-permute-start | bytes 1572872 | tf_op jit(solution)/shard_map/ppermute | solution.py:56
  177.6 28.1 %collective-permute-start.25 = (bf16[320,896]{1,0:T(8,128)(2,1)}, bf16[320,896]{1,0:T(8,128)(2,1)}, u32[]{:S(2)}, u32[]{:S(2)}) collective-permute-start(bf16[320,896]{1,0:T(8,128)(2,1)} %shard_map.129.refs_0_), channel_id=1, source_target_pairs={{0,2},{2,4},{4,6},{6,0},{1,3},{3,5},{5,7},{7,1},{8,10},{10,12},{12... | collective-permute-start | bytes 1720328 | tf_op jit(solution)/shard_map/ppermute | solution.py:47
  179.6 31.1 %collective-permute-start.24 = (bf16[320,896]{1,0:T(8,128)(2,1)}, bf16[320,896]{1,0:T(8,128)(2,1)}, u32[]{:S(2)}, u32[]{:S(2)}) collective-permute-start(bf16[320,896]{1,0:T(8,128)(2,1)} %shard_map.129.refs_0_), channel_id=1, source_target_pairs={{0,4},{2,6},{4,0},{6,2},{1,5},{3,7},{5,1},{7,3},{8,12},{10,14},{12... | collective-permute-start | bytes 1720328 | tf_op jit(solution)/shard_map/ppermute | solution.py:48
  183.9 28.7 %collective-permute-start.23 = (bf16[320,896]{1,0:T(8,128)(2,1)}, bf16[320,896]{1,0:T(8,128)(2,1)S(1)}, u32[]{:S(2)}, u32[]{:S(2)}) collective-permute-start(bf16[320,896]{1,0:T(8,128)(2,1)} %shard_map.129.refs_0_), channel_id=1, source_target_pairs={{0,6},{2,0},{4,2},{6,4},{1,7},{3,1},{5,3},{7,5},{8,14},{10,8},{12,... | collective-permute-start | bytes 1720328 | tf_op jit(solution)/shard_map/ppermute | solution.py:46
  186.1 15.6 %collective-permute-start.1 = (bf16[16,32,512]{2,1,0:T(8,128)(2,1)S(1)}, bf16[16,32,512]{2,1,0:T(8,128)(2,1)S(1)}, u32[]{:S(2)}, u32[]{:S(2)}) collective-permute-start(bf16[16,32,512]{2,1,0:T(8,128)(2,1)S(1)} %all-to-all-done.refs_0_), channel_id=1, source_target_pairs={{0,16},{8,24},{16,0},{24,8},{1,17},{9,25},{17,1},{25,9},{2,18},{10... | collective-permute-start | bytes 1572872 | tf_op jit(solution)/shard_map/ppermute | solution.py:56
  190.1 38.4 %copy-start.6 = (bf16[16,32,512]{2,1,0:T(8,128)(2,1)}, bf16[16,32,512]{2,1,0:T(8,128)(2,1)S(1)}, u32[]{:S(2)}) copy-start(bf16[16,32,512]{2,1,0:T(8,128)(2,1)S(1)} %collective-permute-done.2.refs_3_) | copy-start | bytes 1572868
  190.1 38.4 %collective-permute-start = (bf16[16,32,512]{2,1,0:T(8,128)(2,1)S(1)}, bf16[16,32,512]{2,1,0:T(8,128)(2,1)S(1)}, u32[]{:S(2)}, u32[]{:S(2)}) collective-permute-start(bf16[16,32,512]{2,1,0:T(8,128)(2,1)S(1)} %all-to-all-done.refs_0_), channel_id=1, source_target_pairs={{0,24},{8,0},{16,8},{24,16},{1,25},{9,1},{17,9},{25,17},{2,26},{10... | collective-permute-start | bytes 1572872 | tf_op jit(solution)/shard_map/ppermute | solution.py:56
  201.7 26.8 %copy-start.10 = (bf16[16,32,512]{2,1,0:T(8,128)(2,1)}, bf16[16,32,512]{2,1,0:T(8,128)(2,1)S(1)}, u32[]{:S(2)}) copy-start(bf16[16,32,512]{2,1,0:T(8,128)(2,1)S(1)} %collective-permute-done.1.refs_2_) | copy-start | bytes 1572868
  201.7 34.6 %collective-permute-start.26 = (bf16[320,896]{1,0:T(8,128)(2,1)}, bf16[320,896]{1,0:T(8,128)(2,1)S(1)}, u32[]{:S(2)}, u32[]{:S(2)}) collective-permute-start(bf16[320,896]{1,0:T(8,128)(2,1)} %shard_map.129.refs_0_), channel_id=1, source_target_pairs={{0,1},{1,0},{2,3},{3,2},{4,5},{5,4},{6,7},{7,6},{8,9},{9,8},{10,11... | collective-permute-start | bytes 1720328 | tf_op jit(solution)/shard_map/ppermute | solution.py:50
  205.7 30.6 %collective-permute-start.29 = (bf16[320,896]{1,0:T(8,128)(2,1)}, bf16[320,896]{1,0:T(8,128)(2,1)}, u32[]{:S(2)}, u32[]{:S(2)}) collective-permute-start(bf16[320,896]{1,0:T(8,128)(2,1)} %collective-permute-done.25.refs_3_), channel_id=1, source_target_pairs={{0,1},{1,0},{2,3},{3,2},{4,5},{5,4},{6,7},{7,6},{8,9},{9,8},{10,11... | collective-permute-start | bytes 1720328 | tf_op jit(solution)/shard_map/ppermute | solution.py:50
  210.6 25.7 %collective-permute-start.28 = (bf16[320,896]{1,0:T(8,128)(2,1)}, bf16[320,896]{1,0:T(8,128)(2,1)}, u32[]{:S(2)}, u32[]{:S(2)}) collective-permute-start(bf16[320,896]{1,0:T(8,128)(2,1)} %collective-permute-done.24.refs_2_), channel_id=1, source_target_pairs={{0,1},{1,0},{2,3},{3,2},{4,5},{5,4},{6,7},{7,6},{8,9},{9,8},{10,11... | collective-permute-start | bytes 1720328 | tf_op jit(solution)/shard_map/ppermute | solution.py:50
  212.6 23.7 %copy-start.28 = (bf16[320,896]{1,0:T(8,128)(2,1)}, bf16[320,896]{1,0:T(8,128)(2,1)S(1)}, u32[]{:S(2)}) copy-start(bf16[320,896]{1,0:T(8,128)(2,1)S(1)} %collective-permute-done.23.refs_1_) | copy-start | bytes 1720324
  212.6 23.8 %collective-permute-start.27 = (bf16[320,896]{1,0:T(8,128)(2,1)S(1)}, bf16[320,896]{1,0:T(8,128)(2,1)}, u32[]{:S(2)}, u32[]{:S(2)}) collective-permute-start(bf16[320,896]{1,0:T(8,128)(2,1)S(1)} %collective-permute-done.23.refs_1_), channel_id=1, source_target_pairs={{0,1},{1,0},{2,3},{3,2},{4,5},{5,4},{6,7},{7,6},{8,9},{9,8},{10,11... | collective-permute-start | bytes 1720328 | tf_op jit(solution)/shard_map/ppermute | solution.py:50
  215.7 42.9 %all-to-all-start.1 = ((bf16[16,32,256]{2,1,0:T(8,128)(2,1)}), bf16[16,32,256]{2,1,0:T(8,128)(2,1)S(1)}, u32[]{:S(2)}, u32[]{:S(2)}) async-start(bf16[16,32,256]{2,1,0:T(8,128)(2,1)} %broadcast_in_dim.9), calls=%async_computation.1 | async-start | bytes 524288 | tf_op jit(solution)/shard_map/all_to_all | solution.py:33
  250.2 27.8 %collective-permute-start.32 = (bf16[1024,256]{1,0:T(8,128)(2,1)}, bf16[1024,256]{1,0:T(8,128)(2,1)S(1)}, u32[]{:S(2)}, u32[]{:S(2)}) collective-permute-start(bf16[1024,256]{1,0:T(8,128)(2,1)} %shard_map.130.refs_4_), channel_id=1, source_target_pairs={{0,2},{2,4},{4,6},{6,0},{1,3},{3,5},{5,7},{7,1},{8,10},{10,12},{12... | collective-permute-start | bytes 1572872 | tf_op jit(solution)/shard_map/ppermute | solution.py:47
  252.2 28.9 %collective-permute-start.31 = (bf16[1024,256]{1,0:T(8,128)(2,1)}, bf16[1024,256]{1,0:T(8,128)(2,1)S(1)}, u32[]{:S(2)}, u32[]{:S(2)}) collective-permute-start(bf16[1024,256]{1,0:T(8,128)(2,1)} %shard_map.130.refs_4_), channel_id=1, source_target_pairs={{0,4},{2,6},{4,0},{6,2},{1,5},{3,7},{5,1},{7,3},{8,12},{10,14},{12... | collective-permute-start | bytes 1572872 | tf_op jit(solution)/shard_map/ppermute | solution.py:48
  255.7 27.3 %collective-permute-start.30 = (bf16[1024,256]{1,0:T(8,128)(2,1)}, bf16[1024,256]{1,0:T(8,128)(2,1)S(1)}, u32[]{:S(2)}, u32[]{:S(2)}) collective-permute-start(bf16[1024,256]{1,0:T(8,128)(2,1)} %shard_map.130.refs_4_), channel_id=1, source_target_pairs={{0,6},{2,0},{4,2},{6,4},{1,7},{3,1},{5,3},{7,5},{8,14},{10,8},{12,... | collective-permute-start | bytes 1572872 | tf_op jit(solution)/shard_map/ppermute | solution.py:46
  258.7 38.0 %copy-start.1 = (bf16[16,32,256]{2,1,0:T(8,128)(2,1)}, bf16[16,32,256]{2,1,0:T(8,128)(2,1)S(1)}, u32[]{:S(2)}) copy-start(bf16[16,32,256]{2,1,0:T(8,128)(2,1)S(1)} %all-to-all-done.1.refs_0_) | copy-start | bytes 786436
  258.7 11.1 %collective-permute-start.12 = (bf16[16,32,256]{2,1,0:T(8,128)(2,1)S(1)}, bf16[16,32,256]{2,1,0:T(8,128)(2,1)S(1)}, u32[]{:S(2)}, u32[]{:S(2)}) collective-permute-start(bf16[16,32,256]{2,1,0:T(8,128)(2,1)S(1)} %all-to-all-done.1.refs_0_), channel_id=1, source_target_pairs={{0,8},{8,16},{16,24},{24,0},{1,9},{9,17},{17,25},{25,1},{2,10},{10... | collective-permute-start | bytes 786440 | tf_op jit(solution)/shard_map/ppermute | solution.py:56
  261.2 24.2 %collective-permute-start.11 = (bf16[16,32,256]{2,1,0:T(8,128)(2,1)S(1)}, bf16[16,32,256]{2,1,0:T(8,128)(2,1)S(1)}, u32[]{:S(2)}, u32[]{:S(2)}) collective-permute-start(bf16[16,32,256]{2,1,0:T(8,128)(2,1)S(1)} %all-to-all-done.1.refs_0_), channel_id=1, source_target_pairs={{0,16},{8,24},{16,0},{24,8},{1,17},{9,25},{17,1},{25,9},{2,18},{10... | collective-permute-start | bytes 786440 | tf_op jit(solution)/shard_map/ppermute | solution.py:56
  269.8 13.2 %copy-start.18 = (bf16[16,32,256]{2,1,0:T(8,128)(2,1)}, bf16[16,32,256]{2,1,0:T(8,128)(2,1)S(1)}, u32[]{:S(2)}) copy-start(bf16[16,32,256]{2,1,0:T(8,128)(2,1)S(1)} %collective-permute-done.12.refs_3_) | copy-start | bytes 786436
  269.8 25.4 %collective-permute-start.33 = (bf16[1024,256]{1,0:T(8,128)(2,1)}, bf16[1024,256]{1,0:T(8,128)(2,1)S(1)}, u32[]{:S(2)}, u32[]{:S(2)}) collective-permute-start(bf16[1024,256]{1,0:T(8,128)(2,1)} %shard_map.130.refs_4_), channel_id=1, source_target_pairs={{0,1},{1,0},{2,3},{3,2},{4,5},{5,4},{6,7},{7,6},{8,9},{9,8},{10,11... | collective-permute-start | bytes 1572872 | tf_op jit(solution)/shard_map/ppermute | solution.py:50
  278.1 18.6 %copy-start.7 = (bf16[1024,256]{1,0:T(8,128)(2,1)}, bf16[1024,256]{1,0:T(8,128)(2,1)S(1)}, u32[]{:S(2)}) copy-start(bf16[1024,256]{1,0:T(8,128)(2,1)S(1)} %collective-permute-done.32.refs_7_) | copy-start | bytes 1572868
  278.1 17.1 %collective-permute-start.36 = (bf16[1024,256]{1,0:T(8,128)(2,1)S(1)}, bf16[1024,256]{1,0:T(8,128)(2,1)S(1)}, u32[]{:S(2)}, u32[]{:S(2)}) collective-permute-start(bf16[1024,256]{1,0:T(8,128)(2,1)S(1)} %collective-permute-done.32.refs_7_), channel_id=1, source_target_pairs={{0,1},{1,0},{2,3},{3,2},{4,5},{5,4},{6,7},{7,6},{8,9},{9,8},{10,11... | collective-permute-start | bytes 1572872 | tf_op jit(solution)/shard_map/ppermute | solution.py:50
  281.0 15.6 %copy-start.8 = (bf16[1024,256]{1,0:T(8,128)(2,1)}, bf16[1024,256]{1,0:T(8,128)(2,1)S(1)}, u32[]{:S(2)}) copy-start(bf16[1024,256]{1,0:T(8,128)(2,1)S(1)} %collective-permute-done.31.refs_6_) | copy-start | bytes 1572868
  281.1 14.2 %collective-permute-start.35 = (bf16[1024,256]{1,0:T(8,128)(2,1)S(1)}, bf16[1024,256]{1,0:T(8,128)(2,1)S(1)}, u32[]{:S(2)}, u32[]{:S(2)}) collective-permute-start(bf16[1024,256]{1,0:T(8,128)(2,1)S(1)} %collective-permute-done.31.refs_6_), channel_id=1, source_target_pairs={{0,1},{1,0},{2,3},{3,2},{4,5},{5,4},{6,7},{7,6},{8,9},{9,8},{10,11... | collective-permute-start | bytes 1572872 | tf_op jit(solution)/shard_map/ppermute | solution.py:50
  283.0 13.7 %copy-start.9 = (bf16[1024,256]{1,0:T(8,128)(2,1)}, bf16[1024,256]{1,0:T(8,128)(2,1)S(1)}, u32[]{:S(2)}) copy-start(bf16[1024,256]{1,0:T(8,128)(2,1)S(1)} %collective-permute-done.30.refs_5_) | copy-start | bytes 1572868
  283.0 12.2 %collective-permute-start.34 = (bf16[1024,256]{1,0:T(8,128)(2,1)S(1)}, bf16[1024,256]{1,0:T(8,128)(2,1)S(1)}, u32[]{:S(2)}, u32[]{:S(2)}) collective-permute-start(bf16[1024,256]{1,0:T(8,128)(2,1)S(1)} %collective-permute-done.30.refs_5_), channel_id=1, source_target_pairs={{0,1},{1,0},{2,3},{3,2},{4,5},{5,4},{6,7},{7,6},{8,9},{9,8},{10,11... | collective-permute-start | bytes 1572872 | tf_op jit(solution)/shard_map/ppermute | solution.py:50
  285.4 9.7 %collective-permute-start.10 = (bf16[16,32,256]{2,1,0:T(8,128)(2,1)S(1)}, bf16[16,32,256]{2,1,0:T(8,128)(2,1)S(1)}, u32[]{:S(2)}, u32[]{:S(2)}) collective-permute-start(bf16[16,32,256]{2,1,0:T(8,128)(2,1)S(1)} %all-to-all-done.1.refs_0_), channel_id=1, source_target_pairs={{0,24},{8,0},{16,8},{24,16},{1,25},{9,1},{17,9},{25,17},{2,26},{10... | collective-permute-start | bytes 786440 | tf_op jit(solution)/shard_map/ppermute | solution.py:56
  (10 other events, 20.6 us)

commit v3 on v2

--- a/solution.py
+++ b/solution.py
@@ -1,3 +1,5 @@
+import functools
+
 import jax
 import jax.numpy as jnp
 from jax import lax
@@ -67,6 +69,17 @@
     c = lax.axis_index("c")
     ahead = (y + jnp.arange(NY, dtype=jnp.int32)) % NY * NC
     return jnp.concatenate([ahead + c, ahead + 1 - c]).astype(jnp.int32)
+
+
+def fixed_places():
+    c = lax.axis_index("c")
+    even = jnp.arange(NY, dtype=jnp.int32) * NC
+    return jnp.concatenate([even + c, even + 1 - c]).astype(jnp.int32)
+
+
+def gather_mine(part):
+    mine = spread(part, "y", NY)
+    return mine, lax.ppermute(mine, "c", [(0, 1), (1, 0)])
 
 
 def call(kernel, out_shape, operands, scalars, flops, scratch=()):
@@ -84,9 +97,10 @@
 NT = (((1,), (1,)), ((), ()))
 
 
-def feed_forward_kernel(rows_ref, gain_ref, *refs):
-    pieces, out_ref = refs[:-1], refs[-1]
+def feed_forward_kernel(packing_ref, arrived_ref, gain_ref, *refs):
+    pieces, (out_ref, rows_ref) = refs[:-2], refs[-2:]
     each = pieces[0].shape[0] // 2
+    rows_ref[...] = dot(packing_ref[...], arrived_ref[...]).astype(jnp.bfloat16)
     rows = rows_ref[...]
     normed = rms_scale(rows, gain_ref[...]).astype(jnp.bfloat16)
     total = rows.astype(jnp.float32)
@@ -108,7 +122,8 @@
     pieces, out_ref = refs[:-1], refs[-1]
     features = out_ref.shape[1]
     slots = NZ * 16
-    total = jnp.zeros(out_ref.shape, jnp.float32)
+    lanes = pieces[0].shape[2]
+    total = jnp.zeros((lanes, features), jnp.float32)
     for j, piece in enumerate(pieces):
         held = feature_slots(column_ref[j], features // (NZ * NX), slots, 0)
         place = lax.broadcasted_iota(jnp.int32, (slots, features), 1) == held
@@ -118,7 +133,10 @@
             (((0,), (0,)), ((), ())),
             preferred_element_type=jnp.float32,
         )
-    out_ref[...] = total.astype(jnp.bfloat16)
+    total = total.astype(jnp.bfloat16)
+    each = out_ref.shape[0] // 2
+    out_ref[:each] = total[:each]
+    out_ref[each:] = total[lanes // 2 : lanes // 2 + each]
 
 
 def query_kernel(place_ref, column_ref, gain_ref, *refs):
@@ -136,7 +154,7 @@
             w_ref[pl.ds(pl.multiple_of(at + 16, 16), 16)] = piece[z, :16, width:]
         held = feature_slots(column, features // (NZ * NX), slots, 1)
         place = lax.broadcasted_iota(jnp.int32, (features, slots), 0) == held
-        total = total + dot(place.astype(jnp.bfloat16), piece[:, 16:].reshape(slots, -1))
+        total = total + dot(place.astype(jnp.bfloat16), piece[:, 16:32].reshape(slots, -1))
     pairs_ref[...] = total.astype(jnp.bfloat16)
     count = pieces[0].shape[0]
     own = pl.multiple_of(place_ref[0] * width, width)
@@ -147,16 +165,20 @@
         residual_ref[at, :] = piece[:, pl.ds(own, width)]
 
 
-def attention_kernel(place_ref, live_ref, query_ref, w_ref, *refs):
-    pieces, out_ref, pair_ref = refs[:-2], refs[-2], refs[-1]
+def attention_kernel(first_piece, place_ref, live_ref, query_ref, w_ref, *refs):
+    before, (piece_ref, out_ref, pair_ref) = refs[:-3], refs[-3:]
     width = query_ref.shape[1]
     total_rows = query_ref.shape[0]
-    for i, piece in enumerate(pieces):
-        pair_ref[i] = dot(piece[...], w_ref[...]).astype(jnp.bfloat16)
-    out_ref[:SPAN] = jnp.zeros((SPAN, width), jnp.bfloat16)
+    count = piece_ref.shape[0]
+    for i in range(count):
+        pair_ref[i] = dot(piece_ref[i], w_ref[...]).astype(jnp.bfloat16)
+    if before:
+        out_ref[...] = before[0][...]
+    else:
+        out_ref[:SPAN] = jnp.zeros((SPAN, width), jnp.bfloat16)
 
     def one(i, carry):
-        place = place_ref[i]
+        place = place_ref[first_piece + i]
         first = pl.multiple_of(place * 2 * SPAN + SPAN, SPAN)
         second = pl.multiple_of(jnp.minimum(first + SPAN, total_rows - SPAN), SPAN)
         query = jnp.concatenate([query_ref[pl.ds(first, SPAN)], query_ref[pl.ds(second, SPAN)]])
@@ -184,25 +206,25 @@
 
         return carry
 
-    lax.fori_loop(0, len(pieces), one, 0)
+    lax.fori_loop(0, count, one, 0, unroll=2)
 
 
 def output_kernel(place_ref, column_ref, residual_ref, *refs):
-    head_pieces, pieces = refs[:NX], refs[NX : NX + NY * NC]
-    out_ref, w_ref = refs[NX + NY * NC :]
-    width = pieces[0].shape[1]
+    head_pieces, sides, (out_ref, w_ref) = refs[:NX], refs[NX:-2], refs[-2:]
+    width = w_ref.shape[1]
     chunk = 256
     for j, piece in enumerate(head_pieces):
         for z in range(NZ):
             at = pl.multiple_of((z * NX + column_ref[j]) * 32, 32)
-            w_ref[pl.ds(at, 32)] = piece[z]
+            w_ref[pl.ds(at, 16)] = piece[z, 32:, :width]
+            w_ref[pl.ds(pl.multiple_of(at + 16, 16), 16)] = piece[z, 32:, width:]
 
     def one(step, carry):
         at = pl.ds(pl.multiple_of(step * chunk, chunk), chunk)
         total = residual_ref[at].astype(jnp.float32)
-        for i, piece in enumerate(pieces):
+        for i in range(NY * NC):
             depth = pl.ds(pl.multiple_of(place_ref[i] * width, width), width)
-            total = total + dot(piece[at], w_ref[depth])
+            total = total + dot(sides[i // NY][i % NY, at], w_ref[depth])
         out_ref[at] = total.astype(jnp.bfloat16)
         return carry
 
@@ -242,11 +264,20 @@
     arrived = exchange(outgoing, DB)
     arrived = arrived.reshape(shards * per_row * stripe, features)
 
+    rows_each = w_expand.shape[0]
     padded = 16
-    ff_part = pad_rows(jnp.concatenate([w_expand, w_reduce.T], axis=1), padded)
+    _, width = w_query.shape
+    hidden_each = w_expand.shape[1]
+    gap = ((0, padded - rows_each), (0, width - hidden_each))
+    ff_part = jnp.concatenate([jnp.pad(w_expand, gap), jnp.pad(w_reduce.T, gap)], axis=1)
+    pair_part = pad_rows(jnp.concatenate([w_key, w_value], axis=1), padded)
+    query_part = jnp.concatenate([w_query[:padded], w_query[padded:]], axis=1)
+    out_part = jnp.concatenate([w_output[:padded], w_output[padded:]], axis=1)
+    part = jnp.concatenate([ff_part, query_part, pair_part, out_part], axis=0)
+    weights = spread(part, "z", NZ)
     columns = natural_columns()
-    ff_x = gather_x(spread(ff_part, "z", NZ))
-    hidden_each = w_expand.shape[1]
+    ff_x = gather_x(weights[:, :padded])
+    head_x = gather_x(weights[:, padded:])
     ff_t = call(
         arrange_kernel,
         jax.ShapeDtypeStruct((2 * hidden_each, features), bf16),
@@ -255,13 +286,6 @@
         4 * shards * padded * features * hidden_each,
     )
     ff_pieces = gather_seq(ff_t)
-
-    _, width = w_query.shape
-    key_value = pad_rows(jnp.concatenate([w_key, w_value], axis=1), padded)
-    halves = jnp.concatenate([w_query[:padded], w_query[padded:]], axis=1)
-    head_part = jnp.concatenate([halves, key_value], axis=0)
-    head_x = gather_x(spread(head_part, "z", NZ))
-    out_x = gather_x(spread(w_output, "z", NZ))
 
     row_pieces = gather_seq(reader[0])
     places = natural_places()
@@ -279,8 +303,8 @@
 
     own_len = lax.dynamic_index_in_dim(lengths[0], seq_index, 0, keepdims=False)
     own_owner = lax.dynamic_index_in_dim(owners[0], seq_index, 0, keepdims=False)
+    start = jnp.int32(0)
     position = jnp.arange(PACK, dtype=jnp.int32)
-    start = jnp.int32(0)
     source_row = jnp.zeros((PACK,), jnp.int32)
     for j in range(per_row):
         token = position - start
@@ -291,30 +315,34 @@
         start = start + own_len[j]
     slots = jnp.arange(arrived.shape[0], dtype=jnp.int32)
     packing = (source_row[:, None] == slots[None]).astype(bf16)
-    live_rows = dot(packing, arrived).astype(bf16)
-
     encoded = call(
         feed_forward_kernel,
         jax.ShapeDtypeStruct((PACK, features), bf16),
-        [live_rows, encoder_gain.reshape(1, -1)] + ff_pieces,
+        [packing, arrived, encoder_gain.reshape(1, -1)] + ff_pieces,
         0,
         4 * PACK * features * hidden_each * NY * NC,
-    )
-    encoded_pieces = gather_seq(encoded)
+        [pltpu.VMEM((PACK, features), bf16)],
+    )
+    encoded_mine, encoded_other = gather_mine(encoded)
+    fixed = fixed_places()
     first_live = lengths[0, :, 0] + lengths[0, :, 1]
-    attended = call(
-        attention_kernel,
-        half_shape,
-        [places, first_live, queries, w_pairs] + encoded_pieces,
-        2,
-        2 * PACK * NY * NC * features * 2 * width,
-        [pltpu.VMEM((NY * NC, PACK, 2 * width), bf16)],
-    )
-    attended_pieces = gather_seq(attended)
+    attended = []
+    for first_piece, side in ((0, encoded_mine), (NY, encoded_other)):
+        attended = [
+            call(
+                functools.partial(attention_kernel, first_piece),
+                half_shape,
+                [fixed, first_live, queries, w_pairs] + attended + [side],
+                2,
+                PACK * NY * NC * features * 2 * width,
+                [pltpu.VMEM((NY, PACK, 2 * width), bf16)],
+            )
+        ]
+    attended_sides = gather_mine(attended[0])
     result = call(
         output_kernel,
         half_shape,
-        [places, columns, residual] + out_x + attended_pieces,
+        [fixed, columns, residual] + head_x + list(attended_sides),
         2,
         2 * seq_len * model * width,
         [pltpu.VMEM((model, width), bf16)],

time: 304 us -> 352 us (1.16)
  starting transfers between devices: 168 us -> 107 us
  blocking collectives: 0 us -> 59.3 us
  waiting for transfers between devices: 75.7 us -> 120 us
  Pallas kernels: 35.9 us -> 40.3 us
    all_to_all x0 -> x2, blocking collectives: none -> 59.3 us  [exchange(): return lax.all_to_all(blocks, axis, split_axis=0, concat_axis=0, tiled=True)]
    ppermute x16 -> x8, starting transfers between devices: 53.1 us -> 26.6 us  [gather_seq(): return mine + [lax.ppermute(piece, 'c', swap) for piece in mine]]
    all_to_all x4 -> x2, waiting for transfers between devices: 23.2 us -> 42.3 us  [exchange(): return lax.all_to_all(blocks, axis, split_axis=0, concat_axis=0, tiled=True)]
    all_to_all x4 -> x2, starting transfers between devices: 46.7 us -> 32.1 us  [exchange(): return lax.all_to_all(blocks, axis, split_axis=0, concat_axis=0, tiled=True)]
    ppermute x4 -> x2, waiting for transfers between devices: 0.18 us -> 13 us  [gather_seq(): far = lax.ppermute(part, 'y', ring(2))]
    ppermute x9 -> x6, starting transfers between devices: 31.2 us -> 21.1 us  [gather_x(): lax.ppermute(part, 'x', [(i, (i + step) % NX) for i in range(NX)])]
    ppermute x0 -> x2, starting transfers between devices: none -> 7.73 us  [gather_mine(): return (mine, lax.ppermute(mine, 'c', [(0, 1), (1, 0)]))]
    ppermute x4 -> x2, starting transfers between devices: 15.9 us -> 8.22 us  [gather_seq(): far = lax.ppermute(part, 'y', ring(2))]
  transfers between devices with their start and end apart: 41 -> 24, of which waited for: 10 -> 11; matrix products, arithmetic and copies ran while one was open for 5% -> 4% of each run, Pallas kernels for 10% -> 5%
where the time goes in v3:
time: 352 us; the launch traced here: 351 us
  waiting for transfers between devices  120 us (34%)
  starting transfers between devices  107 us (30%)
  blocking collectives  59.3 us (17%)
  Pallas kernels  40.3 us (11%)
  local copies, waits for them, and re-layouts  10.6 us (3%)
  other arithmetic  10.6 us (3%)
    all_to_all x2, blocking collectives, exchange(): return lax.all_to_all(blocks, axis, split_axis=0, concat_axis=0, tiled=True)  59.3 us
    all_to_all x2, waiting for transfers between devices, exchange(): return lax.all_to_all(blocks, axis, split_axis=0, concat_axis=0, tiled=True)  42.3 us
    pallas_call x6, Pallas kernels, call(): pl.pallas_call(kernel, out_shape=out_shape, in_specs=[pl.BlockSpec(memory...  40.3 us
    ppermute x6, waiting for transfers between devices, gather_x(): lax.ppermute(part, 'x', [(i, (i + step) % NX) for i in range(NX)])  37.8 us
    all_to_all x2, starting transfers between devices, exchange(): return lax.all_to_all(blocks, axis, split_axis=0, concat_axis=0, tiled=True)  32.1 us
    ppermute x8, starting transfers between devices, gather_seq(): return mine + [lax.ppermute(piece, 'c', swap) for piece in mine]  26.6 us
    ppermute x2, waiting for transfers between devices, gather_seq(): last = lax.ppermute(part, 'y', ring(1))  22.7 us
    ppermute x6, starting transfers between devices, gather_x(): lax.ppermute(part, 'x', [(i, (i + step) % NX) for i in range(NX)])  21.1 us
  transfers between devices with their start and end apart: 24, of which 11 were waited for; matrix products, arithmetic and copies ran while one was open for 4% of the time, Pallas kernels for 5%

profile of v3, /device:TPU:1, one launch (start us, length us, event | category | flops | bytes accessed | tf_op | source)
XLA Modules:
  0.0 350.8 jit_solution(249768246602893714)
XLA Ops:
  0.0 0.8 fusion.15
  0.8 0.7 fusion.68
  1.5 0.7 fusion.12
  2.3 1.1 broadcast_in_dim.8
  3.4 15.7 %all-to-all-start = ((bf16[16,64,512]{2,1,0:T(8,128)(2,1)}), bf16[16,64,512]{2,1,0:T(8,128)(2,1)S(1)}, u32[]{:S(2)}, u32[]{:S(2)}) async-start(bf16[16,64,512]{2,1,0:T(8,128)(2,1)} %broadcast_in_dim.8), calls=%async_computation | async-start | bytes 2097152 | tf_op jit(solution)/shard_map/all_to_all | solution.py:35
  19.1 0.7 multiply_bitcast_fusion
  20.4 1.5 fusion
  21.8 42.3 %all-to-all-done = bf16[16,64,512]{2,1,0:T(8,128)(2,1)S(1)} async-done(((bf16[16,64,512]{2,1,0:T(8,128)(2,1)}), bf16[16,64,512]{2,1,0:T(8,128)(2,1)S(1)}, u32[]{:S(2)}, u32[]{:S(2)}) %all-to-all-start) | async-done | bytes 1048608 | tf_op jit(solution)/shard_map/all_to_all | solution.py:35
  64.1 16.4 %all-to-all-start.1 = ((bf16[64,8,896]{2,1,0:T(8,128)(2,1)}), bf16[64,8,896]{2,1,0:T(8,128)(2,1)S(1)}, u32[]{:S(2)}, u32[]{:S(2)}) async-start(bf16[64,8,896]{2,1,0:T(8,128)(2,1)} %fusion), calls=%async_computation.1 | async-start | bytes 1835008 | tf_op jit(solution)/shard_map/all_to_all | solution.py:35
  80.6 2.9 collective-permute-start.12
  83.5 4.3 %collective-permute-start.11 = (bf16[16,16,512]{2,1,0:T(8,128)(2,1)S(1)}, bf16[16,16,512]{2,1,0:T(8,128)(2,1)S(1)}, u32[]{:S(2)}, u32[]{:S(2)}) collective-permute-start(bf16[16,16,512]{2,1,0:T(8,128)(2,1)S(1)} %slice.76.refs_0_), channel_id=1, source_target_pairs={{0,16},{8,24},{16,0},{24,8},{1,17},{9,25},{17,1},{25,9},{2,18},{10... | collective-permute-start | bytes 786440 | tf_op jit(solution)/shard_map/ppermute | solution.py:58
  87.8 3.1 collective-permute-start.10
  90.9 0.5 and_select_fusion.1.column_ref
  91.5 0.5 collective-permute-done.12.refs_3_
  92.0 8.4 %collective-permute-done.11.refs_2_ = bf16[16,16,512]{2,1,0:T(8,128)(2,1)S(1)} collective-permute-done((bf16[16,16,512]{2,1,0:T(8,128)(2,1)S(1)}, bf16[16,16,512]{2,1,0:T(8,128)(2,1)S(1)}, u32[]{:S(2)}, u32[]{:S(2)}) %collective-permute-start.11) | collective-permute-done | bytes 262176 | tf_op jit(solution)/shard_map/ppermute | solution.py:58
  100.4 2.5 collective-permute-done.10.refs_1_
  102.9 0.7 copy-done.23
  103.6 3.4 shard_map.128.refs_0_
  107.0 3.2 collective-permute-start.15
  110.2 4.5 %collective-permute-start.14 = (bf16[448,896]{1,0:T(8,128)(2,1)}, bf16[448,896]{1,0:T(8,128)(2,1)}, u32[]{:S(2)}, u32[]{:S(2)}) collective-permute-start(bf16[448,896]{1,0:T(8,128)(2,1)} %shard_map.128.refs_0_), channel_id=1, source_target_pairs={{0,4},{2,6},{4,0},{6,2},{1,5},{3,7},{5,1},{7,3},{8,12},{10,14},{12... | collective-permute-start | bytes 2408456 | tf_op jit(solution)/shard_map/ppermute | solution.py:50
  114.8 3.0 collective-permute-start.13
  117.7 4.5 %collective-permute-start.16 = (bf16[448,896]{1,0:T(8,128)(2,1)}, bf16[448,896]{1,0:T(8,128)(2,1)}, u32[]{:S(2)}, u32[]{:S(2)}) collective-permute-start(bf16[448,896]{1,0:T(8,128)(2,1)} %shard_map.128.refs_0_), channel_id=1, source_target_pairs={{0,1},{1,0},{2,3},{3,2},{4,5},{5,4},{6,7},{7,6},{8,9},{9,8},{10,11... | collective-permute-start | bytes 2408456 | tf_op jit(solution)/shard_map/ppermute | solution.py:52
  122.2 6.0 %collective-permute-done.15.refs_3_ = bf16[448,896]{1,0:T(8,128)(2,1)S(1)} collective-permute-done((bf16[448,896]{1,0:T(8,128)(2,1)}, bf16[448,896]{1,0:T(8,128)(2,1)S(1)}, u32[]{:S(2)}, u32[]{:S(2)}) %collective-permute-start.15) | collective-permute-done | bytes 802848 | tf_op jit(solution)/shard_map/ppermute | solution.py:49
  128.2 5.4 %collective-permute-start.19 = (bf16[448,896]{1,0:T(8,128)(2,1)S(1)}, bf16[448,896]{1,0:T(8,128)(2,1)}, u32[]{:S(2)}, u32[]{:S(2)}) collective-permute-start(bf16[448,896]{1,0:T(8,128)(2,1)S(1)} %collective-permute-done.15.refs_3_), channel_id=1, source_target_pairs={{0,1},{1,0},{2,3},{3,2},{4,5},{5,4},{6,7},{7,6},{8,9},{9,8},{10,11... | collective-permute-start | bytes 2408456 | tf_op jit(solution)/shard_map/ppermute | solution.py:52
  133.6 13.0 %collective-permute-done.14.refs_2_ = bf16[448,896]{1,0:T(8,128)(2,1)} collective-permute-done((bf16[448,896]{1,0:T(8,128)(2,1)}, bf16[448,896]{1,0:T(8,128)(2,1)}, u32[]{:S(2)}, u32[]{:S(2)}) %collective-permute-start.14) | collective-permute-done | bytes 802848 | tf_op jit(solution)/shard_map/ppermute | solution.py:50
  146.6 4.5 %collective-permute-start.18 = (bf16[448,896]{1,0:T(8,128)(2,1)}, bf16[448,896]{1,0:T(8,128)(2,1)}, u32[]{:S(2)}, u32[]{:S(2)}) collective-permute-start(bf16[448,896]{1,0:T(8,128)(2,1)} %collective-permute-done.14.refs_2_), channel_id=1, source_target_pairs={{0,1},{1,0},{2,3},{3,2},{4,5},{5,4},{6,7},{7,6},{8,9},{9,8},{10,11... | collective-permute-start | bytes 2408456 | tf_op jit(solution)/shard_map/ppermute | solution.py:52
  151.1 1.9 collective-permute-start.17
  153.0 0.6 reshape.248.gain_ref
  153.7 0.6 fusion.70
  156.1 0.6 fusion.71
  156.7 5.1 %fusion.26 = s32[320]{0:T(512)S(1)} fusion(s32[]{:T(128)} %bitcast.11, s32[]{:T(128)} %bitcast.10, s32[]{:T(128)} %bitcast.5, s32[]{:T(128)} %bitcast.4, s32[]{:T(128)} %bitcast.9, s32[]{:T(128)} %bitcast.6, s32[]{:T(128)S(6)} %add.279, s32[]{:T(128)} %bitcast.8, s32[]{:T(128)} %bitcast.7, s32[]{:T(128)S(6)} %add.280), kind=kLoop, calls=%fused_computation.69 | loop fusion | flops 47360 | bytes 1320 | tf_op jit(solution)/shard_map/jit(_where)/select_n | solution.py:314
  161.8 0.8 fusion.1.packing_ref
  162.7 0.9 copy-done.2
  163.6 7.8 %shard_map.129 = bf16[320,896]{1,0:T(8,128)(2,1)} custom-call(bf16[320,512]{1,0:T(8,128)(2,1)} %fusion.1.packing_ref, bf16[512,896]{1,0:T(8,128)(2,1)} %bitcast.20, f32[1,896]{1,0:T(1,128)} %reshape.248.gain_ref, bf16[448,896]{1,0:T(8,128)(2,1)} %shard_map.128.refs_0_, bf16[448,896]{1,0:T(8,128)(2,1)} %collective-permute-done.13.refs_1_, ...), custom_call_target="tpu_custom_call" | custom-call | flops 2055208960 | bytes 7671296 | tf_op jit(solution)/shard_map/pallas_call | solution.py:87
  171.4 1.2 broadcast_in_dim.9
  172.6 32.0 %all_to_all.20.refs_0_ = bf16[4,320,896]{2,1,0:T(8,128)(2,1)} all-to-all(bf16[4,320,896]{2,1,0:T(8,128)(2,1)S(1)} %broadcast_in_dim.9), channel_id=1, replica_groups=mesh['z'=16,'x'=4,'y'=4,'c'=2] {'y'}, dimensions={0} | all-to-all | bytes 4587520 | tf_op jit(solution)/shard_map/all_to_all | solution.py:35
  204.7 3.3 collective-permute-start.20
  208.1 2.2 collective-permute-start.5
  210.3 3.7 %collective-permute-start.4 = (bf16[128,2048]{1,0:T(8,128)(2,1)S(1)}, bf16[128,2048]{1,0:T(8,128)(2,1)S(1)}, u32[]{:S(2)}, u32[]{:S(2)}) collective-permute-start(bf16[128,2048]{1,0:T(8,128)(2,1)S(1)} %bitcast.23), channel_id=1, source_target_pairs={{0,4},{2,6},{4,0},{6,2},{1,5},{3,7},{5,1},{7,3},{8,12},{10,14},{12... | collective-permute-start | bytes 1572872 | tf_op jit(solution)/shard_map/ppermute | solution.py:50
  214.0 2.5 collective-permute-start.6
  216.4 2.6 collective-permute-start.3
  219.1 16.8 %collective-permute-done.5.refs_7_ = bf16[128,2048]{1,0:T(8,128)(2,1)S(1)} collective-permute-done((bf16[128,2048]{1,0:T(8,128)(2,1)S(1)}, bf16[128,2048]{1,0:T(8,128)(2,1)S(1)}, u32[]{:S(2)}, u32[]{:S(2)}) %collective-permute-start.5) | collective-permute-done | bytes 524320 | tf_op jit(solution)/shard_map/ppermute | solution.py:49
  235.9 2.8 collective-permute-start.9
  238.7 1.9 collective-permute-start.8
  240.7 4.6 %collective-permute-start.2 = (bf16[16,48,512]{2,1,0:T(8,128)(2,1)S(1)}, bf16[16,48,512]{2,1,0:T(8,128)(2,1)S(1)}, u32[]{:S(2)}, u32[]{:S(2)}) collective-permute-start(bf16[16,48,512]{2,1,0:T(8,128)(2,1)S(1)} %slice.75.refs_0_), channel_id=1, source_target_pairs={{0,8},{8,16},{16,24},{24,0},{1,9},{9,17},{17,25},{25,1},{2,10},{10... | collective-permute-start | bytes 2359304 | tf_op jit(solution)/shard_map/ppermute | solution.py:58
  245.3 4.1 %collective-permute-start.1 = (bf16[16,48,512]{2,1,0:T(8,128)(2,1)S(1)}, bf16[16,48,512]{2,1,0:T(8,128)(2,1)S(1)}, u32[]{:S(2)}, u32[]{:S(2)}) collective-permute-start(bf16[16,48,512]{2,1,0:T(8,128)(2,1)S(1)} %slice.75.refs_0_), channel_id=1, source_target_pairs={{0,16},{8,24},{16,0},{24,8},{1,17},{9,25},{17,1},{25,9},{2,18},{10... | collective-permute-start | bytes 2359304 | tf_op jit(solution)/shard_map/ppermute | solution.py:58
  249.5 2.1 collective-permute-start
  251.6 3.1 collective-permute-start.7
  254.8 0.6 pad_add_fusion.1.place_ref
  255.4 0.7 pad_add_fusion.place_ref
  256.0 0.5 add_bitcast_fusion.live_ref
  256.6 7.2 %collective-permute-done.2.refs_3_ = bf16[16,48,512]{2,1,0:T(8,128)(2,1)S(1)} collective-permute-done((bf16[16,48,512]{2,1,0:T(8,128)(2,1)S(1)}, bf16[16,48,512]{2,1,0:T(8,128)(2,1)S(1)}, u32[]{:S(2)}, u32[]{:S(2)}) %collective-permute-start.2) | collective-permute-done | bytes 786464 | tf_op jit(solution)/shard_map/ppermute | solution.py:58
  263.7 17.7 %collective-permute-done.1.refs_2_ = bf16[16,48,512]{2,1,0:T(8,128)(2,1)S(1)} collective-permute-done((bf16[16,48,512]{2,1,0:T(8,128)(2,1)S(1)}, bf16[16,48,512]{2,1,0:T(8,128)(2,1)S(1)}, u32[]{:S(2)}, u32[]{:S(2)}) %collective-permute-start.1) | collective-permute-done | bytes 786464 | tf_op jit(solution)/shard_map/ppermute | solution.py:58
  281.5 1.4 collective-permute-done.refs_1_
  282.9 0.9 copy-done.5
  283.8 7.4 %shard_map.127 = (bf16[1024,256]{1,0:T(8,128)(2,1)}, bf16[1024,256]{1,0:T(8,128)(2,1)}, bf16[896,512]{1,0:T(8,128)(2,1)}) custom-call(s32[8]{0:T(128)} %pad_add_fusion.1.place_ref, s32[4]{0:T(128)} %and_select_fusion.1.column_ref, f32[1,2048]{1,0:T(1,128)} %bitcast.26, bf16[16,48,512]{2,1,0:T(8,128)(2,1)} %copy-done.1, bf16[16,48,512]{2,1,0:T(8,128)(2,1)} %copy-done.5, ...), custom_call_target="tpu_custom_call" | custom-call | flops 1073741824 | bytes 7348272 | tf_op jit(solution)/shard_map/pallas_call | solution.py:87
  291.2 7.7 %shard_map.130.refs_0_ = bf16[1024,256]{1,0:T(8,128)(2,1)} custom-call(s32[8]{0:T(128)} %pad_add_fusion.place_ref, s32[8]{0:T(128)} %add_bitcast_fusion.live_ref, bf16[1024,256]{1,0:T(8,128)(2,1)} %get-tuple-element.9.query_ref, bf16[896,512]{1,0:T(8,128)(2,1)} %get-tuple-element.10.w_ref, bf16[4,320,896]{2,1,0:T(8,128)(2,1)} %all_to_all.20.refs_0_), custom_call_target="tpu_custom_call" | custom-call | flops 1174405120 | bytes 3735616 | tf_op jit(solution)/shard_map/pallas_call | solution.py:87
  298.9 7.9 %shard_map.131 = bf16[1024,256]{1,0:T(8,128)(2,1)} custom-call(s32[8]{0:T(128)} %pad_add_fusion.place_ref, s32[8]{0:T(128)} %add_bitcast_fusion.live_ref, bf16[1024,256]{1,0:T(8,128)(2,1)} %get-tuple-element.9.query_ref, bf16[896,512]{1,0:T(8,128)(2,1)} %get-tuple-element.10.w_ref, bf16[1024,256]{1,0:T(8,128)(2,1)} %shard_map.130.refs_0_, ...), custom_call_target="tpu_custom_call" | custom-call | flops 1174405120 | bytes 4259904 | tf_op jit(solution)/shard_map/pallas_call | solution.py:87
  306.8 1.2 broadcast_in_dim.10
  308.0 27.3 %all_to_all.21.refs_4_ = bf16[4,1024,256]{2,1,0:T(8,128)(2,1)S(1)} all-to-all(bf16[4,1024,256]{2,1,0:T(8,128)(2,1)S(1)} %broadcast_in_dim.10), channel_id=1, replica_groups=mesh['z'=16,'x'=4,'y'=4,'c'=2] {'y'}, dimensions={0} | all-to-all | bytes 4194304 | tf_op jit(solution)/shard_map/all_to_all | solution.py:35
  335.3 4.4 %collective-permute-start.21 = (bf16[4,1024,256]{2,1,0:T(8,128)(2,1)S(1)}, bf16[4,1024,256]{2,1,0:T(8,128)(2,1)S(1)}, u32[]{:S(2)}, u32[]{:S(2)}) collective-permute-start(bf16[4,1024,256]{2,1,0:T(8,128)(2,1)S(1)} %all_to_all.21.refs_4_), channel_id=1, source_target_pairs={{0,1},{1,0},{2,3},{3,2},{4,5},{5,4},{6,7},{7,6},{8,9},{9,8},{10,11... | collective-permute-start | bytes 6291464 | tf_op jit(solution)/shard_map/ppermute | solution.py:82
  339.7 3.8 %collective-permute-done.21.refs_5_ = bf16[4,1024,256]{2,1,0:T(8,128)(2,1)S(1)} collective-permute-done((bf16[4,1024,256]{2,1,0:T(8,128)(2,1)S(1)}, bf16[4,1024,256]{2,1,0:T(8,128)(2,1)S(1)}, u32[]{:S(2)}, u32[]{:S(2)}) %collective-permute-start.21) | collective-permute-done | bytes 2097184 | tf_op jit(solution)/shard_map/ppermute | solution.py:82
  343.4 1.4 copy-done.6
  344.8 6.1 %shard_map.132 = bf16[1024,256]{1,0:T(8,128)(2,1)} custom-call(s32[8]{0:T(128)} %pad_add_fusion.place_ref, s32[4]{0:T(128)} %and_select_fusion.1.column_ref, bf16[1024,256]{1,0:T(8,128)(2,1)} %get-tuple-element.8.residual_ref, bf16[16,48,512]{2,1,0:T(8,128)(2,1)} %copy-done.1, bf16[16,48,512]{2,1,0:T(8,128)(2,1)} %copy-done.5, ...), custom_call_target="tpu_custom_call" | custom-call | flops 1073741824 | bytes 7864368 | tf_op jit(solution)/shard_map/pallas_call | solution.py:87
  (66 shorter events, 0.9 us)
Async XLA Ops:
  0.0 20.2 %copy-start.16 = (bf16[128,2,896]{2,1,0:T(2,128)(2,1)S(1)}, bf16[128,2,896]{2,1,0:T(2,128)(2,1)}, u32[]{:S(2)}) copy-start(bf16[128,2,896]{2,1,0:T(2,128)(2,1)} %param.15) | copy-start | bytes 1376260
  3.4 60.7 %all-to-all-start = ((bf16[16,64,512]{2,1,0:T(8,128)(2,1)}), bf16[16,64,512]{2,1,0:T(8,128)(2,1)S(1)}, u32[]{:S(2)}, u32[]{:S(2)}) async-start(bf16[16,64,512]{2,1,0:T(8,128)(2,1)} %broadcast_in_dim.8), calls=%async_computation | async-start | bytes 2097152 | tf_op jit(solution)/shard_map/all_to_all | solution.py:35
  64.1 98.5 %all-to-all-start.1 = ((bf16[64,8,896]{2,1,0:T(8,128)(2,1)}), bf16[64,8,896]{2,1,0:T(8,128)(2,1)S(1)}, u32[]{:S(2)}, u32[]{:S(2)}) async-start(bf16[64,8,896]{2,1,0:T(8,128)(2,1)} %fusion), calls=%async_computation.1 | async-start | bytes 1835008 | tf_op jit(solution)/shard_map/all_to_all | solution.py:35
  80.5 72.5 %copy-start.18 = (f32[896]{0:T(1024)S(1)}, f32[896]{0:T(1024)}, u32[]{:S(2)}) copy-start(f32[896]{0:T(1024)} %param.16) | copy-start | bytes 10756
  80.5 73.1 %copy-start.19 = (s32[1,8,4]{1,2,0:T(4,128)S(1)}, s32[1,8,4]{1,2,0:T(4,128)}, u32[]{:S(2)}) copy-start(s32[1,8,4]{1,2,0:T(4,128)} %param.25) | copy-start | bytes 388
  80.5 73.1 %copy-start.20 = (s32[1,8,4]{1,2,0:T(4,128)S(1)}, s32[1,8,4]{1,2,0:T(4,128)}, u32[]{:S(2)}) copy-start(s32[1,8,4]{1,2,0:T(4,128)} %param.24) | copy-start | bytes 388
  80.6 22.4 %copy-start.17 = (bf16[16,16,512]{2,1,0:T(8,128)(2,1)}, bf16[16,16,512]{2,1,0:T(8,128)(2,1)S(1)}, u32[]{:S(2)}) copy-start(bf16[16,16,512]{2,1,0:T(8,128)(2,1)S(1)} %slice.76.refs_0_) | copy-start | bytes 786436
  80.6 11.4 %collective-permute-start.12 = (bf16[16,16,512]{2,1,0:T(8,128)(2,1)S(1)}, bf16[16,16,512]{2,1,0:T(8,128)(2,1)S(1)}, u32[]{:S(2)}, u32[]{:S(2)}) collective-permute-start(bf16[16,16,512]{2,1,0:T(8,128)(2,1)S(1)} %slice.76.refs_0_), channel_id=1, source_target_pairs={{0,8},{8,16},{16,24},{24,0},{1,9},{9,17},{17,25},{25,1},{2,10},{10... | collective-permute-start | bytes 786440 | tf_op jit(solution)/shard_map/ppermute | solution.py:58
  83.5 16.9 %collective-permute-start.11 = (bf16[16,16,512]{2,1,0:T(8,128)(2,1)S(1)}, bf16[16,16,512]{2,1,0:T(8,128)(2,1)S(1)}, u32[]{:S(2)}, u32[]{:S(2)}) collective-permute-start(bf16[16,16,512]{2,1,0:T(8,128)(2,1)S(1)} %slice.76.refs_0_), channel_id=1, source_target_pairs={{0,16},{8,24},{16,0},{24,8},{1,17},{9,25},{17,1},{25,9},{2,18},{10... | collective-permute-start | bytes 786440 | tf_op jit(solution)/shard_map/ppermute | solution.py:58
  87.8 15.1 %collective-permute-start.10 = (bf16[16,16,512]{2,1,0:T(8,128)(2,1)S(1)}, bf16[16,16,512]{2,1,0:T(8,128)(2,1)S(1)}, u32[]{:S(2)}, u32[]{:S(2)}) collective-permute-start(bf16[16,16,512]{2,1,0:T(8,128)(2,1)S(1)} %slice.76.refs_0_), channel_id=1, source_target_pairs={{0,24},{8,0},{16,8},{24,16},{1,25},{9,1},{17,9},{25,17},{2,26},{10... | collective-permute-start | bytes 786440 | tf_op jit(solution)/shard_map/ppermute | solution.py:58
  92.0 10.9 %copy-start.21 = (bf16[16,16,512]{2,1,0:T(8,128)(2,1)}, bf16[16,16,512]{2,1,0:T(8,128)(2,1)S(1)}, u32[]{:S(2)}) copy-start(bf16[16,16,512]{2,1,0:T(8,128)(2,1)S(1)} %collective-permute-done.12.refs_3_) | copy-start | bytes 786436
  100.4 2.5 copy-start.22
  102.9 0.7 copy-start.23
  107.0 21.2 %collective-permute-start.15 = (bf16[448,896]{1,0:T(8,128)(2,1)}, bf16[448,896]{1,0:T(8,128)(2,1)S(1)}, u32[]{:S(2)}, u32[]{:S(2)}) collective-permute-start(bf16[448,896]{1,0:T(8,128)(2,1)} %shard_map.128.refs_0_), channel_id=1, source_target_pairs={{0,2},{2,4},{4,6},{6,0},{1,3},{3,5},{5,7},{7,1},{8,10},{10,12},{12... | collective-permute-start | bytes 2408456 | tf_op jit(solution)/shard_map/ppermute | solution.py:49
  110.2 36.4 %collective-permute-start.14 = (bf16[448,896]{1,0:T(8,128)(2,1)}, bf16[448,896]{1,0:T(8,128)(2,1)}, u32[]{:S(2)}, u32[]{:S(2)}) collective-permute-start(bf16[448,896]{1,0:T(8,128)(2,1)} %shard_map.128.refs_0_), channel_id=1, source_target_pairs={{0,4},{2,6},{4,0},{6,2},{1,5},{3,7},{5,1},{7,3},{8,12},{10,14},{12... | collective-permute-start | bytes 2408456 | tf_op jit(solution)/shard_map/ppermute | solution.py:50
  114.8 36.3 %collective-permute-start.13 = (bf16[448,896]{1,0:T(8,128)(2,1)}, bf16[448,896]{1,0:T(8,128)(2,1)}, u32[]{:S(2)}, u32[]{:S(2)}) collective-permute-start(bf16[448,896]{1,0:T(8,128)(2,1)} %shard_map.128.refs_0_), channel_id=1, source_target_pairs={{0,6},{2,0},{4,2},{6,4},{1,7},{3,1},{5,3},{7,5},{8,14},{10,8},{12,... | collective-permute-start | bytes 2408456 | tf_op jit(solution)/shard_map/ppermute | solution.py:48
  117.7 44.9 %collective-permute-start.16 = (bf16[448,896]{1,0:T(8,128)(2,1)}, bf16[448,896]{1,0:T(8,128)(2,1)}, u32[]{:S(2)}, u32[]{:S(2)}) collective-permute-start(bf16[448,896]{1,0:T(8,128)(2,1)} %shard_map.128.refs_0_), channel_id=1, source_target_pairs={{0,1},{1,0},{2,3},{3,2},{4,5},{5,4},{6,7},{7,6},{8,9},{9,8},{10,11... | collective-permute-start | bytes 2408456 | tf_op jit(solution)/shard_map/ppermute | solution.py:52
  128.2 34.5 %copy-start.7 = (bf16[448,896]{1,0:T(8,128)(2,1)}, bf16[448,896]{1,0:T(8,128)(2,1)S(1)}, u32[]{:S(2)}) copy-start(bf16[448,896]{1,0:T(8,128)(2,1)S(1)} %collective-permute-done.15.refs_3_) | copy-start | bytes 2408452
  128.2 34.5 %collective-permute-start.19 = (bf16[448,896]{1,0:T(8,128)(2,1)S(1)}, bf16[448,896]{1,0:T(8,128)(2,1)}, u32[]{:S(2)}, u32[]{:S(2)}) collective-permute-start(bf16[448,896]{1,0:T(8,128)(2,1)S(1)} %collective-permute-done.15.refs_3_), channel_id=1, source_target_pairs={{0,1},{1,0},{2,3},{3,2},{4,5},{5,4},{6,7},{7,6},{8,9},{9,8},{10,11... | collective-permute-start | bytes 2408456 | tf_op jit(solution)/shard_map/ppermute | solution.py:52
  146.6 16.1 %collective-permute-start.18 = (bf16[448,896]{1,0:T(8,128)(2,1)}, bf16[448,896]{1,0:T(8,128)(2,1)}, u32[]{:S(2)}, u32[]{:S(2)}) collective-permute-start(bf16[448,896]{1,0:T(8,128)(2,1)} %collective-permute-done.14.refs_2_), channel_id=1, source_target_pairs={{0,1},{1,0},{2,3},{3,2},{4,5},{5,4},{6,7},{7,6},{8,9},{9,8},{10,11... | collective-permute-start | bytes 2408456 | tf_op jit(solution)/shard_map/ppermute | solution.py:52
  151.1 11.6 %collective-permute-start.17 = (bf16[448,896]{1,0:T(8,128)(2,1)}, bf16[448,896]{1,0:T(8,128)(2,1)}, u32[]{:S(2)}, u32[]{:S(2)}) collective-permute-start(bf16[448,896]{1,0:T(8,128)(2,1)} %collective-permute-done.13.refs_1_), channel_id=1, source_target_pairs={{0,1},{1,0},{2,3},{3,2},{4,5},{5,4},{6,7},{7,6},{8,9},{9,8},{10,11... | collective-permute-start | bytes 2408456 | tf_op jit(solution)/shard_map/ppermute | solution.py:52
  162.6 1.0 copy-start.2
  172.6 35.4 %copy-start.8 = (bf16[1,128,2048]{2,1,0:T(8,128)(2,1)S(1)}, bf16[1,128,2048]{2,1,0:T(8,128)(2,1)}, u32[]{:S(2)}) copy-start(bf16[1,128,2048]{2,1,0:T(8,128)(2,1)} %param.13) | copy-start | bytes 1572868
  204.7 94.2 %collective-permute-start.20 = (bf16[4,320,896]{2,1,0:T(8,128)(2,1)}, bf16[4,320,896]{2,1,0:T(8,128)(2,1)}, u32[]{:S(2)}, u32[]{:S(2)}) collective-permute-start(bf16[4,320,896]{2,1,0:T(8,128)(2,1)} %all_to_all.20.refs_0_), channel_id=1, source_target_pairs={{0,1},{1,0},{2,3},{3,2},{4,5},{5,4},{6,7},{7,6},{8,9},{9,8},{10,11... | collective-permute-start | bytes 6881288 | tf_op jit(solution)/shard_map/ppermute | solution.py:82
  208.1 27.8 %collective-permute-start.5 = (bf16[128,2048]{1,0:T(8,128)(2,1)S(1)}, bf16[128,2048]{1,0:T(8,128)(2,1)S(1)}, u32[]{:S(2)}, u32[]{:S(2)}) collective-permute-start(bf16[128,2048]{1,0:T(8,128)(2,1)S(1)} %bitcast.22), channel_id=1, source_target_pairs={{0,2},{2,4},{4,6},{6,0},{1,3},{3,5},{5,7},{7,1},{8,10},{10,12},{12... | collective-permute-start | bytes 1572872 | tf_op jit(solution)/shard_map/ppermute | solution.py:49
  210.3 28.4 %collective-permute-start.4 = (bf16[128,2048]{1,0:T(8,128)(2,1)S(1)}, bf16[128,2048]{1,0:T(8,128)(2,1)S(1)}, u32[]{:S(2)}, u32[]{:S(2)}) collective-permute-start(bf16[128,2048]{1,0:T(8,128)(2,1)S(1)} %bitcast.23), channel_id=1, source_target_pairs={{0,4},{2,6},{4,0},{6,2},{1,5},{3,7},{5,1},{7,3},{8,12},{10,14},{12... | collective-permute-start | bytes 1572872 | tf_op jit(solution)/shard_map/ppermute | solution.py:50
  214.0 26.7 %collective-permute-start.6 = (bf16[128,2048]{1,0:T(8,128)(2,1)S(1)}, bf16[128,2048]{1,0:T(8,128)(2,1)S(1)}, u32[]{:S(2)}, u32[]{:S(2)}) collective-permute-start(bf16[128,2048]{1,0:T(8,128)(2,1)S(1)} %bitcast.24), channel_id=1, source_target_pairs={{0,1},{1,0},{2,3},{3,2},{4,5},{5,4},{6,7},{7,6},{8,9},{9,8},{10,11... | collective-permute-start | bytes 1572872 | tf_op jit(solution)/shard_map/ppermute | solution.py:52
  216.4 28.9 %collective-permute-start.3 = (bf16[128,2048]{1,0:T(8,128)(2,1)S(1)}, bf16[128,2048]{1,0:T(8,128)(2,1)S(1)}, u32[]{:S(2)}, u32[]{:S(2)}) collective-permute-start(bf16[128,2048]{1,0:T(8,128)(2,1)S(1)} %bitcast.25), channel_id=1, source_target_pairs={{0,6},{2,0},{4,2},{6,4},{1,7},{3,1},{5,3},{7,5},{8,14},{10,8},{12,... | collective-permute-start | bytes 1572872 | tf_op jit(solution)/shard_map/ppermute | solution.py:48
  235.9 47.0 %copy-start.9 = (bf16[128,2048]{1,0:T(8,128)(2,1)}, bf16[128,2048]{1,0:T(8,128)(2,1)S(1)}, u32[]{:S(2)}) copy-start(bf16[128,2048]{1,0:T(8,128)(2,1)S(1)} %collective-permute-done.5.refs_7_) | copy-start | bytes 1572868
  235.9 13.6 %collective-permute-start.9 = (bf16[128,2048]{1,0:T(8,128)(2,1)S(1)}, bf16[128,2048]{1,0:T(8,128)(2,1)S(1)}, u32[]{:S(2)}, u32[]{:S(2)}) collective-permute-start(bf16[128,2048]{1,0:T(8,128)(2,1)S(1)} %collective-permute-done.5.refs_7_), channel_id=1, source_target_pairs={{0,1},{1,0},{2,3},{3,2},{4,5},{5,4},{6,7},{7,6},{8,9},{9,8},{10,11... | collective-permute-start | bytes 1572872 | tf_op jit(solution)/shard_map/ppermute | solution.py:52
  238.6 44.2 %copy-start.10 = (bf16[128,2048]{1,0:T(8,128)(2,1)}, bf16[128,2048]{1,0:T(8,128)(2,1)S(1)}, u32[]{:S(2)}) copy-start(bf16[128,2048]{1,0:T(8,128)(2,1)S(1)} %collective-permute-done.4.refs_6_) | copy-start | bytes 1572868
  238.7 12.9 %collective-permute-start.8 = (bf16[128,2048]{1,0:T(8,128)(2,1)S(1)}, bf16[128,2048]{1,0:T(8,128)(2,1)S(1)}, u32[]{:S(2)}, u32[]{:S(2)}) collective-permute-start(bf16[128,2048]{1,0:T(8,128)(2,1)S(1)} %collective-permute-done.4.refs_6_), channel_id=1, source_target_pairs={{0,1},{1,0},{2,3},{3,2},{4,5},{5,4},{6,7},{7,6},{8,9},{9,8},{10,11... | collective-permute-start | bytes 1572872 | tf_op jit(solution)/shard_map/ppermute | solution.py:52
  240.7 43.1 %copy-start.1 = (bf16[16,48,512]{2,1,0:T(8,128)(2,1)}, bf16[16,48,512]{2,1,0:T(8,128)(2,1)S(1)}, u32[]{:S(2)}) copy-start(bf16[16,48,512]{2,1,0:T(8,128)(2,1)S(1)} %slice.75.refs_0_) | copy-start | bytes 2359300
  240.7 4.6 %copy-start.11 = (bf16[128,2048]{1,0:T(8,128)(2,1)}, bf16[128,2048]{1,0:T(8,128)(2,1)S(1)}, u32[]{:S(2)}) copy-start(bf16[128,2048]{1,0:T(8,128)(2,1)S(1)} %collective-permute-done.6.refs_8_) | copy-start | bytes 1572868
  240.7 23.0 %collective-permute-start.2 = (bf16[16,48,512]{2,1,0:T(8,128)(2,1)S(1)}, bf16[16,48,512]{2,1,0:T(8,128)(2,1)S(1)}, u32[]{:S(2)}, u32[]{:S(2)}) collective-permute-start(bf16[16,48,512]{2,1,0:T(8,128)(2,1)S(1)} %slice.75.refs_0_), channel_id=1, source_target_pairs={{0,8},{8,16},{16,24},{24,0},{1,9},{9,17},{17,25},{25,1},{2,10},{10... | collective-permute-start | bytes 2359304 | tf_op jit(solution)/shard_map/ppermute | solution.py:58
  245.3 37.6 %copy-start.12 = (bf16[128,2048]{1,0:T(8,128)(2,1)}, bf16[128,2048]{1,0:T(8,128)(2,1)S(1)}, u32[]{:S(2)}) copy-start(bf16[128,2048]{1,0:T(8,128)(2,1)S(1)} %collective-permute-done.3.refs_5_) | copy-start | bytes 1572868
  245.3 36.2 %collective-permute-start.1 = (bf16[16,48,512]{2,1,0:T(8,128)(2,1)S(1)}, bf16[16,48,512]{2,1,0:T(8,128)(2,1)S(1)}, u32[]{:S(2)}, u32[]{:S(2)}) collective-permute-start(bf16[16,48,512]{2,1,0:T(8,128)(2,1)S(1)} %slice.75.refs_0_), channel_id=1, source_target_pairs={{0,16},{8,24},{16,0},{24,8},{1,17},{9,25},{17,1},{25,9},{2,18},{10... | collective-permute-start | bytes 2359304 | tf_op jit(solution)/shard_map/ppermute | solution.py:58
  249.5 33.4 %copy-start.13 = (bf16[128,2048]{1,0:T(8,128)(2,1)}, bf16[128,2048]{1,0:T(8,128)(2,1)S(1)}, u32[]{:S(2)}) copy-start(bf16[128,2048]{1,0:T(8,128)(2,1)S(1)} %collective-permute-done.9.refs_11_) | copy-start | bytes 1572868
  249.5 33.4 %collective-permute-start = (bf16[16,48,512]{2,1,0:T(8,128)(2,1)S(1)}, bf16[16,48,512]{2,1,0:T(8,128)(2,1)S(1)}, u32[]{:S(2)}, u32[]{:S(2)}) collective-permute-start(bf16[16,48,512]{2,1,0:T(8,128)(2,1)S(1)} %slice.75.refs_0_), channel_id=1, source_target_pairs={{0,24},{8,0},{16,8},{24,16},{1,25},{9,1},{17,9},{25,17},{2,26},{10... | collective-permute-start | bytes 2359304 | tf_op jit(solution)/shard_map/ppermute | solution.py:58
  251.6 31.3 %copy-start.14 = (bf16[128,2048]{1,0:T(8,128)(2,1)}, bf16[128,2048]{1,0:T(8,128)(2,1)S(1)}, u32[]{:S(2)}) copy-start(bf16[128,2048]{1,0:T(8,128)(2,1)S(1)} %collective-permute-done.8.refs_10_) | copy-start | bytes 1572868
  251.6 5.0 %collective-permute-start.7 = (bf16[128,2048]{1,0:T(8,128)(2,1)S(1)}, bf16[128,2048]{1,0:T(8,128)(2,1)S(1)}, u32[]{:S(2)}, u32[]{:S(2)}) collective-permute-start(bf16[128,2048]{1,0:T(8,128)(2,1)S(1)} %collective-permute-done.3.refs_5_), channel_id=1, source_target_pairs={{0,1},{1,0},{2,3},{3,2},{4,5},{5,4},{6,7},{7,6},{8,9},{9,8},{10,11... | collective-permute-start | bytes 1572872 | tf_op jit(solution)/shard_map/ppermute | solution.py:52
  256.6 27.2 %copy-start.15 = (bf16[128,2048]{1,0:T(8,128)(2,1)}, bf16[128,2048]{1,0:T(8,128)(2,1)S(1)}, u32[]{:S(2)}) copy-start(bf16[128,2048]{1,0:T(8,128)(2,1)S(1)} %collective-permute-done.7.refs_9_) | copy-start | bytes 1572868
  263.7 20.1 %copy-start.3 = (bf16[16,48,512]{2,1,0:T(8,128)(2,1)}, bf16[16,48,512]{2,1,0:T(8,128)(2,1)S(1)}, u32[]{:S(2)}) copy-start(bf16[16,48,512]{2,1,0:T(8,128)(2,1)S(1)} %collective-permute-done.2.refs_3_) | copy-start | bytes 2359300
  281.5 2.3 copy-start.4
  282.9 0.9 copy-start.5
  335.3 9.5 %copy-start = (bf16[4,1024,256]{2,1,0:T(8,128)(2,1)}, bf16[4,1024,256]{2,1,0:T(8,128)(2,1)S(1)}, u32[]{:S(2)}) copy-start(bf16[4,1024,256]{2,1,0:T(8,128)(2,1)S(1)} %all_to_all.21.refs_4_) | copy-start | bytes 6291460
  335.3 8.2 %collective-permute-start.21 = (bf16[4,1024,256]{2,1,0:T(8,128)(2,1)S(1)}, bf16[4,1024,256]{2,1,0:T(8,128)(2,1)S(1)}, u32[]{:S(2)}, u32[]{:S(2)}) collective-permute-start(bf16[4,1024,256]{2,1,0:T(8,128)(2,1)S(1)} %all_to_all.21.refs_4_), channel_id=1, source_target_pairs={{0,1},{1,0},{2,3},{3,2},{4,5},{5,4},{6,7},{7,6},{8,9},{9,8},{10,11... | collective-permute-start | bytes 6291464 | tf_op jit(solution)/shard_map/ppermute | solution.py:82
  343.4 1.4 copy-start.6

commit v4 on v3

--- a/solution.py
+++ b/solution.py
@@ -154,7 +154,7 @@
             w_ref[pl.ds(pl.multiple_of(at + 16, 16), 16)] = piece[z, :16, width:]
         held = feature_slots(column, features // (NZ * NX), slots, 1)
         place = lax.broadcasted_iota(jnp.int32, (features, slots), 0) == held
-        total = total + dot(place.astype(jnp.bfloat16), piece[:, 16:32].reshape(slots, -1))
+        total = total + dot(place.astype(jnp.bfloat16), piece[:, 16:].reshape(slots, -1))
     pairs_ref[...] = total.astype(jnp.bfloat16)
     count = pieces[0].shape[0]
     own = pl.multiple_of(place_ref[0] * width, width)
@@ -166,12 +166,12 @@
 
 
 def attention_kernel(first_piece, place_ref, live_ref, query_ref, w_ref, *refs):
-    before, (piece_ref, out_ref, pair_ref) = refs[:-3], refs[-3:]
+    before, pieces, (out_ref, pair_ref) = refs[: -NY - 2], refs[-NY - 2 : -2], refs[-2:]
     width = query_ref.shape[1]
     total_rows = query_ref.shape[0]
-    count = piece_ref.shape[0]
-    for i in range(count):
-        pair_ref[i] = dot(piece_ref[i], w_ref[...]).astype(jnp.bfloat16)
+    count = len(pieces)
+    for i, piece in enumerate(pieces):
+        pair_ref[i] = dot(piece[...], w_ref[...]).astype(jnp.bfloat16)
     if before:
         out_ref[...] = before[0][...]
     else:
@@ -209,26 +209,38 @@
     lax.fori_loop(0, count, one, 0, unroll=2)
 
 
-def output_kernel(place_ref, column_ref, residual_ref, *refs):
-    head_pieces, sides, (out_ref, w_ref) = refs[:NX], refs[NX:-2], refs[-2:]
+def output_rows(place_ref, first_piece, side, w_ref, base_ref, out_ref):
     width = w_ref.shape[1]
     chunk = 256
+
+    def one(step, carry):
+        at = pl.ds(pl.multiple_of(step * chunk, chunk), chunk)
+        total = base_ref[at].astype(jnp.float32)
+        for i in range(NY):
+            depth = pl.multiple_of(place_ref[first_piece + i] * width, width)
+            total = total + dot(side[i, at], w_ref[pl.ds(depth, width)])
+        out_ref[at] = total.astype(out_ref.dtype)
+        return carry
+
+    lax.fori_loop(0, out_ref.shape[0] // chunk, one, 0)
+
+
+def out_weight_kernel(column_ref, *refs):
+    head_pieces, w_ref = refs[:-1], refs[-1]
+    width = w_ref.shape[1]
     for j, piece in enumerate(head_pieces):
         for z in range(NZ):
             at = pl.multiple_of((z * NX + column_ref[j]) * 32, 32)
-            w_ref[pl.ds(at, 16)] = piece[z, 32:, :width]
-            w_ref[pl.ds(pl.multiple_of(at + 16, 16), 16)] = piece[z, 32:, width:]
-
-    def one(step, carry):
-        at = pl.ds(pl.multiple_of(step * chunk, chunk), chunk)
-        total = residual_ref[at].astype(jnp.float32)
-        for i in range(NY * NC):
-            depth = pl.ds(pl.multiple_of(place_ref[i] * width, width), width)
-            total = total + dot(sides[i // NY][i % NY, at], w_ref[depth])
-        out_ref[at] = total.astype(jnp.bfloat16)
-        return carry
-
-    lax.fori_loop(0, out_ref.shape[0] // chunk, one, 0)
+            w_ref[pl.ds(at, 16)] = piece[z, :, :width]
+            w_ref[pl.ds(pl.multiple_of(at + 16, 16), 16)] = piece[z, :, width:]
+
+
+def first_output_kernel(place_ref, residual_ref, w_ref, side, out_ref):
+    output_rows(place_ref, 0, side, w_ref, residual_ref, out_ref)
+
+
+def second_output_kernel(place_ref, partial_ref, w_ref, side, out_ref):
+    output_rows(place_ref, NY, side, w_ref, partial_ref, out_ref)
 
 
 def pad_rows(a, rows):
@@ -273,11 +285,11 @@
     pair_part = pad_rows(jnp.concatenate([w_key, w_value], axis=1), padded)
     query_part = jnp.concatenate([w_query[:padded], w_query[padded:]], axis=1)
     out_part = jnp.concatenate([w_output[:padded], w_output[padded:]], axis=1)
-    part = jnp.concatenate([ff_part, query_part, pair_part, out_part], axis=0)
-    weights = spread(part, "z", NZ)
     columns = natural_columns()
-    ff_x = gather_x(weights[:, :padded])
-    head_x = gather_x(weights[:, padded:])
+    ff_x = gather_x(spread(ff_part, "z", NZ))
+    head_part = jnp.concatenate([query_part, pair_part], axis=0)
+    head_x = gather_x(spread(head_part, "z", NZ))
+    out_x = gather_x(spread(out_part, "z", NZ))
     ff_t = call(
         arrange_kernel,
         jax.ShapeDtypeStruct((2 * hidden_each, features), bf16),
@@ -323,29 +335,44 @@
         4 * PACK * features * hidden_each * NY * NC,
         [pltpu.VMEM((PACK, features), bf16)],
     )
-    encoded_mine, encoded_other = gather_mine(encoded)
+    encoded_pieces = gather_seq(encoded)
     fixed = fixed_places()
     first_live = lengths[0, :, 0] + lengths[0, :, 1]
     attended = []
-    for first_piece, side in ((0, encoded_mine), (NY, encoded_other)):
+    for first_piece in (0, NY):
         attended = [
             call(
                 functools.partial(attention_kernel, first_piece),
                 half_shape,
-                [fixed, first_live, queries, w_pairs] + attended + [side],
+                [places, first_live, queries, w_pairs]
+                + attended
+                + encoded_pieces[first_piece : first_piece + NY],
                 2,
                 PACK * NY * NC * features * 2 * width,
                 [pltpu.VMEM((NY, PACK, 2 * width), bf16)],
             )
         ]
-    attended_sides = gather_mine(attended[0])
+    attended_mine, attended_other = gather_mine(attended[0])
+    w_o = call(
+        out_weight_kernel,
+        jax.ShapeDtypeStruct((model, width), bf16),
+        [columns] + out_x,
+        1,
+        model * width,
+    )
+    partial = call(
+        first_output_kernel,
+        jax.ShapeDtypeStruct((seq_len, width), jnp.float32),
+        [fixed, residual, w_o, attended_mine],
+        1,
+        seq_len * model * width,
+    )
     result = call(
-        output_kernel,
+        second_output_kernel,
         half_shape,
-        [fixed, columns, residual] + head_x + list(attended_sides),
-        2,
-        2 * seq_len * model * width,
-        [pltpu.VMEM((model, width), bf16)],
+        [fixed, partial, w_o, attended_other],
+        1,
+        seq_len * model * width,
     )
     return result[None]
 

time: 352 us -> 382 us (1.085); the launches traced: 351 us -> 376 us
  starting transfers between devices: 107 us -> 128 us
  blocking collectives: 59.3 us -> 54.6 us
  Pallas kernels: 40.3 us -> 44.7 us
    ppermute x2 -> x3, waiting for transfers between devices: 0.01 us -> 44.5 us  [gather_seq(): near = lax.ppermute(part, 'y', ring(-1))]
    ppermute x2 -> x3, waiting for transfers between devices: 13 us -> 0.01 us  [gather_seq(): far = lax.ppermute(part, 'y', ring(2))]
    ppermute x2 -> x3, waiting for transfers between devices: 22.7 us -> 11.7 us  [gather_seq(): last = lax.ppermute(part, 'y', ring(1))]
    all_to_all x2 -> x3, waiting for transfers between devices: 42.3 us -> 32.6 us  [exchange(): return lax.all_to_all(blocks, axis, split_axis=0, concat_axis=0, tiled=True)]
    all_to_all x2 -> x3, starting transfers between devices: 32.1 us -> 41.7 us  [exchange(): return lax.all_to_all(blocks, axis, split_axis=0, concat_axis=0, tiled=True)]
    ppermute x2 -> x3, starting transfers between devices: 5.6 us -> 10.7 us  [gather_seq(): near = lax.ppermute(part, 'y', ring(-1))]
    all_to_all x2, blocking collectives: 59.3 us -> 54.6 us  [exchange(): return lax.all_to_all(blocks, axis, split_axis=0, concat_axis=0, tiled=True)]
    ppermute x6 -> x9, starting transfers between devices: 21.1 us -> 25.7 us  [gather_x(): lax.ppermute(part, 'x', [(i, (i + step) % NX) for i in range(NX)])]
  transfers between devices with their start and end apart: 24 -> 34, of which waited for: 11 -> 11; matrix products, arithmetic and copies ran while one was open for 4% -> 4% of each run, Pallas kernels for 5% -> 9%
where the time goes in v4:
time: 382 us; the launch traced here: 376 us
  starting transfers between devices  128 us (34%)
  waiting for transfers between devices  123 us (32%)
  blocking collectives  54.6 us (14%)
  Pallas kernels  44.7 us (12%)
  local copies, waits for them, and re-layouts  11 us (3%)
  other arithmetic  10.7 us (3%)
    all_to_all x2, blocking collectives, exchange(): return lax.all_to_all(blocks, axis, split_axis=0, concat_axis=0, tiled=True)  54.6 us
    pallas_call x8, Pallas kernels, call(): pl.pallas_call(kernel, out_shape=out_shape, in_specs=[pl.BlockSpec(memory...  44.7 us
    ppermute x3, waiting for transfers between devices, gather_seq(): near = lax.ppermute(part, 'y', ring(-1))  44.5 us
    all_to_all x3, starting transfers between devices, exchange(): return lax.all_to_all(blocks, axis, split_axis=0, concat_axis=0, tiled=True)  41.7 us
    ppermute x9, waiting for transfers between devices, gather_x(): lax.ppermute(part, 'x', [(i, (i + step) % NX) for i in range(NX)])  34.2 us
    all_to_all x3, waiting for transfers between devices, exchange(): return lax.all_to_all(blocks, axis, split_axis=0, concat_axis=0, tiled=True)  32.6 us
    ppermute x12, starting transfers between devices, gather_seq(): return mine + [lax.ppermute(piece, 'c', swap) for piece in mine]  30.6 us
    ppermute x9, starting transfers between devices, gather_x(): lax.ppermute(part, 'x', [(i, (i + step) % NX) for i in range(NX)])  25.7 us
  transfers between devices with their start and end apart: 34, of which 11 were waited for; matrix products, arithmetic and copies ran while one was open for 4% of the time, Pallas kernels for 9%

profile of v4, /device:TPU:1, one launch (start us, length us, event | category | flops | bytes accessed | tf_op | source)
XLA Modules:
  0.0 375.8 jit_solution(5752375831055071743)
XLA Ops:
  0.0 0.8 fusion.7
  1.5 15.7 %all-to-all-start.3 = ((bf16[16,16,512]{2,1,0:T(8,128)(2,1)}), bf16[16,16,512]{2,1,0:T(8,128)(2,1)S(1)}, u32[]{:S(2)}, u32[]{:S(2)}) async-start(bf16[16,16,512]{2,1,0:T(8,128)(2,1)} %broadcast_in_dim.12), calls=%async_computation.3 | async-start | bytes 524288 | tf_op jit(solution)/shard_map/all_to_all | solution.py:35
  18.7 12.3 %all-to-all-done.3.refs_0_ = bf16[16,16,512]{2,1,0:T(8,128)(2,1)S(1)} async-done(((bf16[16,16,512]{2,1,0:T(8,128)(2,1)}), bf16[16,16,512]{2,1,0:T(8,128)(2,1)S(1)}, u32[]{:S(2)}, u32[]{:S(2)}) %all-to-all-start.3) | async-done | bytes 262176 | tf_op jit(solution)/shard_map/all_to_all | solution.py:35
  31.0 0.9 broadcast_in_dim.10
  31.9 10.3 %all-to-all-start = ((bf16[16,32,512]{2,1,0:T(8,128)(2,1)}), bf16[16,32,512]{2,1,0:T(8,128)(2,1)S(1)}, u32[]{:S(2)}, u32[]{:S(2)}) async-start(bf16[16,32,512]{2,1,0:T(8,128)(2,1)} %broadcast_in_dim.10), calls=%async_computation | async-start | bytes 1048576 | tf_op jit(solution)/shard_map/all_to_all | solution.py:35
  43.5 1.5 fusion
  45.0 20.3 %all-to-all-done.refs_0_ = bf16[16,32,512]{2,1,0:T(8,128)(2,1)S(1)} async-done(((bf16[16,32,512]{2,1,0:T(8,128)(2,1)}), bf16[16,32,512]{2,1,0:T(8,128)(2,1)S(1)}, u32[]{:S(2)}, u32[]{:S(2)}) %all-to-all-start) | async-done | bytes 524320 | tf_op jit(solution)/shard_map/all_to_all | solution.py:35
  65.3 15.7 %all-to-all-start.2 = ((bf16[64,8,896]{2,1,0:T(8,128)(2,1)}), bf16[64,8,896]{2,1,0:T(8,128)(2,1)S(1)}, u32[]{:S(2)}, u32[]{:S(2)}) async-start(bf16[64,8,896]{2,1,0:T(8,128)(2,1)} %fusion), calls=%async_computation.2 | async-start | bytes 1835008 | tf_op jit(solution)/shard_map/all_to_all | solution.py:35
  80.9 4.1 %collective-permute-start.13 = (bf16[16,16,512]{2,1,0:T(8,128)(2,1)S(1)}, bf16[16,16,512]{2,1,0:T(8,128)(2,1)S(1)}, u32[]{:S(2)}, u32[]{:S(2)}) collective-permute-start(bf16[16,16,512]{2,1,0:T(8,128)(2,1)S(1)} %all-to-all-done.3.refs_0_), channel_id=1, source_target_pairs={{0,24},{8,0},{16,8},{24,16},{1,25},{9,1},{17,9},{25,17},{2,26},{10... | collective-permute-start | bytes 786440 | tf_op jit(solution)/shard_map/ppermute | solution.py:58
  85.1 2.5 collective-permute-start.14
  87.6 2.5 collective-permute-start.15
  91.3 6.6 %collective-permute-done.14.refs_2_ = bf16[16,16,512]{2,1,0:T(8,128)(2,1)S(1)} collective-permute-done((bf16[16,16,512]{2,1,0:T(8,128)(2,1)S(1)}, bf16[16,16,512]{2,1,0:T(8,128)(2,1)S(1)}, u32[]{:S(2)}, u32[]{:S(2)}) %collective-permute-start.14) | collective-permute-done | bytes 262176 | tf_op jit(solution)/shard_map/ppermute | solution.py:58
  98.0 8.2 %collective-permute-done.15.refs_3_ = bf16[16,16,512]{2,1,0:T(8,128)(2,1)S(1)} collective-permute-done((bf16[16,16,512]{2,1,0:T(8,128)(2,1)S(1)}, bf16[16,16,512]{2,1,0:T(8,128)(2,1)S(1)}, u32[]{:S(2)}, u32[]{:S(2)}) %collective-permute-start.15) | collective-permute-done | bytes 262176 | tf_op jit(solution)/shard_map/ppermute | solution.py:58
  106.9 3.4 shard_map.129.refs_0_
  110.3 4.6 %collective-permute-start.16 = (bf16[448,896]{1,0:T(8,128)(2,1)}, bf16[448,896]{1,0:T(8,128)(2,1)S(1)}, u32[]{:S(2)}, u32[]{:S(2)}) collective-permute-start(bf16[448,896]{1,0:T(8,128)(2,1)} %shard_map.129.refs_0_), channel_id=1, source_target_pairs={{0,6},{2,0},{4,2},{6,4},{1,7},{3,1},{5,3},{7,5},{8,14},{10,8},{12,... | collective-permute-start | bytes 2408456 | tf_op jit(solution)/shard_map/ppermute | solution.py:48
  114.9 2.3 collective-permute-start.17
  117.2 2.7 collective-permute-start.3
  119.9 2.6 collective-permute-start.18
  122.5 4.5 %collective-permute-start.4 = (bf16[128,2048]{1,0:T(8,128)(2,1)}, bf16[128,2048]{1,0:T(8,128)(2,1)}, u32[]{:S(2)}, u32[]{:S(2)}) collective-permute-start(bf16[128,2048]{1,0:T(8,128)(2,1)} %bitcast.22), channel_id=1, source_target_pairs={{0,4},{2,6},{4,0},{6,2},{1,5},{3,7},{5,1},{7,3},{8,12},{10,14},{12... | collective-permute-start | bytes 1572872 | tf_op jit(solution)/shard_map/ppermute | solution.py:50
  127.1 44.5 %collective-permute-done.3.refs_5_ = bf16[128,2048]{1,0:T(8,128)(2,1)S(1)} collective-permute-done((bf16[128,2048]{1,0:T(8,128)(2,1)}, bf16[128,2048]{1,0:T(8,128)(2,1)S(1)}, u32[]{:S(2)}, u32[]{:S(2)}) %collective-permute-start.3) | collective-permute-done | bytes 524320 | tf_op jit(solution)/shard_map/ppermute | solution.py:48
  171.5 3.4 collective-permute-start.19
  175.0 1.9 collective-permute-start.20
  176.9 2.4 collective-permute-start.21
  179.3 1.9 collective-permute-start.5
  181.3 1.9 collective-permute-start.22
  186.4 10.8 %collective-permute-done.5.refs_7_ = bf16[128,2048]{1,0:T(8,128)(2,1)} collective-permute-done((bf16[128,2048]{1,0:T(8,128)(2,1)}, bf16[128,2048]{1,0:T(8,128)(2,1)}, u32[]{:S(2)}, u32[]{:S(2)}) %collective-permute-start.5) | collective-permute-done | bytes 524320 | tf_op jit(solution)/shard_map/ppermute | solution.py:49
  197.1 2.5 collective-permute-start.6
  199.7 1.9 collective-permute-start.7
  201.6 2.4 collective-permute-start.8
  204.0 1.9 collective-permute-start.9
  206.0 5.1 %fusion.19 = s32[320]{0:T(512)S(1)} fusion(s32[]{:T(128)} %bitcast.10, s32[]{:T(128)} %bitcast.9, s32[]{:T(128)} %bitcast.4, s32[]{:T(128)} %bitcast.3, s32[]{:T(128)} %bitcast.8, s32[]{:T(128)} %bitcast.5, s32[]{:T(128)S(6)} %add.279, s32[]{:T(128)} %bitcast.7, s32[]{:T(128)} %bitcast.6, s32[]{:T(128)S(6)} %add.280), kind=kLoop, calls=%fused_computation.63 | loop fusion | flops 47360 | bytes 1320 | tf_op jit(solution)/shard_map/jit(_where)/select_n | solution.py:326
  211.7 0.9 fusion.1.packing_ref
  212.6 1.9 collective-permute-start
  214.5 1.0 copy-done.1
  215.5 7.8 %shard_map.130.refs_0_ = bf16[320,896]{1,0:T(8,128)(2,1)} custom-call(bf16[320,512]{1,0:T(8,128)(2,1)} %fusion.1.packing_ref, bf16[512,896]{1,0:T(8,128)(2,1)} %bitcast.20, f32[1,896]{1,0:T(1,128)} %reshape.249.gain_ref, bf16[448,896]{1,0:T(8,128)(2,1)} %shard_map.129.refs_0_, bf16[448,896]{1,0:T(8,128)(2,1)} %copy-done.4, bf16[448,896]{1,0:T(8,128)(2,1)} %copy-done.5, ...), custom_call_target="tpu_custom_call" | custom-call | flops 2055208960 | bytes 7671296 | tf_op jit(solution)/shard_map/pallas_call | solution.py:87
  223.3 3.4 collective-permute-start.23
  226.7 1.9 collective-permute-start.24
  228.6 2.5 collective-permute-start.25
  231.1 3.0 collective-permute-start.1
  234.2 2.8 collective-permute-start.2
  236.9 10.1 %collective-permute-done.1.refs_2_ = bf16[16,32,512]{2,1,0:T(8,128)(2,1)S(1)} collective-permute-done((bf16[16,32,512]{2,1,0:T(8,128)(2,1)S(1)}, bf16[16,32,512]{2,1,0:T(8,128)(2,1)S(1)}, u32[]{:S(2)}, u32[]{:S(2)}) %collective-permute-start.1) | collective-permute-done | bytes 524320 | tf_op jit(solution)/shard_map/ppermute | solution.py:58
  247.0 5.3 %collective-permute-start.26 = (bf16[320,896]{1,0:T(8,128)(2,1)}, bf16[320,896]{1,0:T(8,128)(2,1)S(1)}, u32[]{:S(2)}, u32[]{:S(2)}) collective-permute-start(bf16[320,896]{1,0:T(8,128)(2,1)} %shard_map.130.refs_0_), channel_id=1, source_target_pairs={{0,1},{1,0},{2,3},{3,2},{4,5},{5,4},{6,7},{7,6},{8,9},{9,8},{10,11... | collective-permute-start | bytes 1720328 | tf_op jit(solution)/shard_map/ppermute | solution.py:52
  252.3 1.9 collective-permute-start.27
  254.3 2.4 collective-permute-start.28
  256.7 0.9 collective-permute-done.25.refs_3_
  257.6 2.6 collective-permute-start.29
  261.3 0.8 copy-done.12
  262.1 7.1 %shard_map.127 = (bf16[1024,256]{1,0:T(8,128)(2,1)}, bf16[1024,256]{1,0:T(8,128)(2,1)}, bf16[896,512]{1,0:T(8,128)(2,1)}) custom-call(s32[8]{0:T(128)} %pad_add_fusion.1.place_ref, s32[4]{0:T(128)} %and_select_fusion.column_ref, f32[1,2048]{1,0:T(1,128)} %bitcast.26, bf16[16,32,512]{2,1,0:T(8,128)(2,1)} %copy-done.2, ...), custom_call_target="tpu_custom_call" | custom-call | flops 1073741824 | bytes 6299696 | tf_op jit(solution)/shard_map/pallas_call | solution.py:87
  269.3 7.7 %shard_map.131.refs_0_ = bf16[1024,256]{1,0:T(8,128)(2,1)} custom-call(s32[8]{0:T(128)} %pad_add_fusion.1.place_ref, s32[8]{0:T(128)} %add_bitcast_fusion.live_ref, bf16[1024,256]{1,0:T(8,128)(2,1)} %get-tuple-element.9.query_ref, bf16[896,512]{1,0:T(8,128)(2,1)} %get-tuple-element.10.w_ref, bf16[320,896]{1,0:T(8,128)(2,1)} %shard_map.130.refs_0_, ...), custom_call_target="tpu_custom_call" | custom-call | flops 1174405120 | bytes 3735616 | tf_op jit(solution)/shard_map/pallas_call | solution.py:87
  277.0 0.8 copy-done.6
  278.1 0.8 copy-done.9
  278.9 7.8 %shard_map.132 = bf16[1024,256]{1,0:T(8,128)(2,1)} custom-call(s32[8]{0:T(128)} %pad_add_fusion.1.place_ref, s32[8]{0:T(128)} %add_bitcast_fusion.live_ref, bf16[1024,256]{1,0:T(8,128)(2,1)} %get-tuple-element.9.query_ref, bf16[896,512]{1,0:T(8,128)(2,1)} %get-tuple-element.10.w_ref, bf16[1024,256]{1,0:T(8,128)(2,1)} %shard_map.131.refs_0_, ...), custom_call_target="tpu_custom_call" | custom-call | flops 1174405120 | bytes 4259904 | tf_op jit(solution)/shard_map/pallas_call | solution.py:87
  286.8 1.2 broadcast_in_dim.13
  288.0 29.1 %all_to_all.25.side = bf16[4,1024,256]{2,1,0:T(8,128)(2,1)S(1)} all-to-all(bf16[4,1024,256]{2,1,0:T(8,128)(2,1)S(1)} %broadcast_in_dim.13), channel_id=1, replica_groups=mesh['z'=16,'x'=4,'y'=4,'c'=2] {'y'}, dimensions={0} | all-to-all | bytes 4194304 | tf_op jit(solution)/shard_map/all_to_all | solution.py:35
  317.0 3.3 collective-permute-start.30
  320.4 25.5 %all_to_all.26.refs_0_ = bf16[16,16,512]{2,1,0:T(8,128)(2,1)S(1)} all-to-all(bf16[16,16,512]{2,1,0:T(8,128)(2,1)S(1)} %broadcast_in_dim.11), channel_id=1, replica_groups=mesh['z'=16,'x'=4,'y'=4,'c'=2] {'z'}, dimensions={0} | all-to-all | bytes 524288 | tf_op jit(solution)/shard_map/all_to_all | solution.py:35
  345.9 2.5 collective-permute-start.10
  348.4 4.5 %collective-permute-start.11 = (bf16[16,16,512]{2,1,0:T(8,128)(2,1)S(1)}, bf16[16,16,512]{2,1,0:T(8,128)(2,1)S(1)}, u32[]{:S(2)}, u32[]{:S(2)}) collective-permute-start(bf16[16,16,512]{2,1,0:T(8,128)(2,1)S(1)} %all_to_all.26.refs_0_), channel_id=1, source_target_pairs={{0,16},{8,24},{16,0},{24,8},{1,17},{9,25},{17,1},{25,9},{2,18},{10... | collective-permute-start | bytes 786440 | tf_op jit(solution)/shard_map/ppermute | solution.py:58
  353.0 1.9 collective-permute-start.12
  355.6 1.5 collective-permute-done.11.refs_2_
  357.1 7.0 %collective-permute-done.12.refs_3_ = bf16[16,16,512]{2,1,0:T(8,128)(2,1)S(1)} collective-permute-done((bf16[16,16,512]{2,1,0:T(8,128)(2,1)S(1)}, bf16[16,16,512]{2,1,0:T(8,128)(2,1)S(1)}, u32[]{:S(2)}, u32[]{:S(2)}) %collective-permute-start.12) | collective-permute-done | bytes 262176 | tf_op jit(solution)/shard_map/ppermute | solution.py:58
  364.8 2.3 shard_map.128.w_ref
  367.2 4.3 %shard_map.133.partial_ref = f32[1024,256]{1,0:T(8,128)} custom-call(s32[8]{0:T(128)} %pad_add_fusion.place_ref, bf16[1024,256]{1,0:T(8,128)(2,1)} %get-tuple-element.8.residual_ref, bf16[2048,256]{1,0:T(8,128)(2,1)} %shard_map.128.w_ref, bf16[4,1024,256]{2,1,0:T(8,128)(2,1)} %copy-done), custom_call_target="tpu_custom_call" | custom-call | flops 536870912 | bytes 3670048 | tf_op jit(solution)/shard_map/pallas_call | solution.py:87
  371.5 4.3 %shard_map.134 = bf16[1024,256]{1,0:T(8,128)(2,1)} custom-call(s32[8]{0:T(128)} %pad_add_fusion.place_ref, f32[1024,256]{1,0:T(8,128)} %shard_map.133.partial_ref, bf16[2048,256]{1,0:T(8,128)(2,1)} %shard_map.128.w_ref, bf16[4,1024,256]{2,1,0:T(8,128)(2,1)} %collective-permute-done.30.side), custom_call_target="tpu_custom_call" | custom-call | flops 536870912 | bytes 4194336 | tf_op jit(solution)/shard_map/pallas_call | solution.py:87
  (92 shorter events, 10.4 us)
Async XLA Ops:
  0.0 43.3 %copy-start.13 = (bf16[128,2,896]{2,1,0:T(2,128)(2,1)S(1)}, bf16[128,2,896]{2,1,0:T(2,128)(2,1)}, u32[]{:S(2)}) copy-start(bf16[128,2,896]{2,1,0:T(2,128)(2,1)} %param.15) | copy-start | bytes 1376260
  1.5 29.5 %all-to-all-start.3 = ((bf16[16,16,512]{2,1,0:T(8,128)(2,1)}), bf16[16,16,512]{2,1,0:T(8,128)(2,1)S(1)}, u32[]{:S(2)}, u32[]{:S(2)}) async-start(bf16[16,16,512]{2,1,0:T(8,128)(2,1)} %broadcast_in_dim.12), calls=%async_computation.3 | async-start | bytes 524288 | tf_op jit(solution)/shard_map/all_to_all | solution.py:35
  31.0 56.5 %copy-start.17 = (bf16[16,16,512]{2,1,0:T(8,128)(2,1)}, bf16[16,16,512]{2,1,0:T(8,128)(2,1)S(1)}, u32[]{:S(2)}) copy-start(bf16[16,16,512]{2,1,0:T(8,128)(2,1)S(1)} %all-to-all-done.3.refs_0_) | copy-start | bytes 786436
  31.9 33.4 %all-to-all-start = ((bf16[16,32,512]{2,1,0:T(8,128)(2,1)}), bf16[16,32,512]{2,1,0:T(8,128)(2,1)S(1)}, u32[]{:S(2)}, u32[]{:S(2)}) async-start(bf16[16,32,512]{2,1,0:T(8,128)(2,1)} %broadcast_in_dim.10), calls=%async_computation | async-start | bytes 1048576 | tf_op jit(solution)/shard_map/all_to_all | solution.py:35
  45.0 138.2 %copy-start.20 = (s32[1,8,4]{1,2,0:T(4,128)S(1)}, s32[1,8,4]{1,2,0:T(4,128)}, u32[]{:S(2)}) copy-start(s32[1,8,4]{1,2,0:T(4,128)} %param.25) | copy-start | bytes 388
  45.0 138.2 %copy-start.21 = (s32[1,8,4]{1,2,0:T(4,128)S(1)}, s32[1,8,4]{1,2,0:T(4,128)}, u32[]{:S(2)}) copy-start(s32[1,8,4]{1,2,0:T(4,128)} %param.24) | copy-start | bytes 388
  45.0 166.1 %copy-start.19 = (f32[896]{0:T(1024)S(1)}, f32[896]{0:T(1024)}, u32[]{:S(2)}) copy-start(f32[896]{0:T(1024)} %param.16) | copy-start | bytes 10756
  65.3 168.9 %copy-start.2 = (bf16[16,32,512]{2,1,0:T(8,128)(2,1)}, bf16[16,32,512]{2,1,0:T(8,128)(2,1)S(1)}, u32[]{:S(2)}) copy-start(bf16[16,32,512]{2,1,0:T(8,128)(2,1)S(1)} %all-to-all-done.refs_0_) | copy-start | bytes 1572868
  65.3 149.2 %all-to-all-start.2 = ((bf16[64,8,896]{2,1,0:T(8,128)(2,1)}), bf16[64,8,896]{2,1,0:T(8,128)(2,1)S(1)}, u32[]{:S(2)}, u32[]{:S(2)}) async-start(bf16[64,8,896]{2,1,0:T(8,128)(2,1)} %fusion), calls=%async_computation.2 | async-start | bytes 1835008 | tf_op jit(solution)/shard_map/all_to_all | solution.py:35
  80.9 10.4 %collective-permute-start.13 = (bf16[16,16,512]{2,1,0:T(8,128)(2,1)S(1)}, bf16[16,16,512]{2,1,0:T(8,128)(2,1)S(1)}, u32[]{:S(2)}, u32[]{:S(2)}) collective-permute-start(bf16[16,16,512]{2,1,0:T(8,128)(2,1)S(1)} %all-to-all-done.3.refs_0_), channel_id=1, source_target_pairs={{0,24},{8,0},{16,8},{24,16},{1,25},{9,1},{17,9},{25,17},{2,26},{10... | collective-permute-start | bytes 786440 | tf_op jit(solution)/shard_map/ppermute | solution.py:58
  85.1 12.9 %collective-permute-start.14 = (bf16[16,16,512]{2,1,0:T(8,128)(2,1)S(1)}, bf16[16,16,512]{2,1,0:T(8,128)(2,1)S(1)}, u32[]{:S(2)}, u32[]{:S(2)}) collective-permute-start(bf16[16,16,512]{2,1,0:T(8,128)(2,1)S(1)} %all-to-all-done.3.refs_0_), channel_id=1, source_target_pairs={{0,16},{8,24},{16,0},{24,8},{1,17},{9,25},{17,1},{25,9},{2,18},{10... | collective-permute-start | bytes 786440 | tf_op jit(solution)/shard_map/ppermute | solution.py:58
  87.6 18.6 %collective-permute-start.15 = (bf16[16,16,512]{2,1,0:T(8,128)(2,1)S(1)}, bf16[16,16,512]{2,1,0:T(8,128)(2,1)S(1)}, u32[]{:S(2)}, u32[]{:S(2)}) collective-permute-start(bf16[16,16,512]{2,1,0:T(8,128)(2,1)S(1)} %all-to-all-done.3.refs_0_), channel_id=1, source_target_pairs={{0,8},{8,16},{16,24},{24,0},{1,9},{9,17},{17,25},{25,1},{2,10},{10... | collective-permute-start | bytes 786440 | tf_op jit(solution)/shard_map/ppermute | solution.py:58
  91.3 14.8 %copy-start.22 = (bf16[16,16,512]{2,1,0:T(8,128)(2,1)}, bf16[16,16,512]{2,1,0:T(8,128)(2,1)S(1)}, u32[]{:S(2)}) copy-start(bf16[16,16,512]{2,1,0:T(8,128)(2,1)S(1)} %collective-permute-done.13.refs_1_) | copy-start | bytes 786436
  98.0 8.2 %copy-start.23 = (bf16[16,16,512]{2,1,0:T(8,128)(2,1)}, bf16[16,16,512]{2,1,0:T(8,128)(2,1)S(1)}, u32[]{:S(2)}) copy-start(bf16[16,16,512]{2,1,0:T(8,128)(2,1)S(1)} %collective-permute-done.14.refs_2_) | copy-start | bytes 786436
  106.2 0.7 copy-start.24
  110.3 64.6 %collective-permute-start.16 = (bf16[448,896]{1,0:T(8,128)(2,1)}, bf16[448,896]{1,0:T(8,128)(2,1)S(1)}, u32[]{:S(2)}, u32[]{:S(2)}) collective-permute-start(bf16[448,896]{1,0:T(8,128)(2,1)} %shard_map.129.refs_0_), channel_id=1, source_target_pairs={{0,6},{2,0},{4,2},{6,4},{1,7},{3,1},{5,3},{7,5},{8,14},{10,8},{12,... | collective-permute-start | bytes 2408456 | tf_op jit(solution)/shard_map/ppermute | solution.py:48
  114.9 61.9 %collective-permute-start.17 = (bf16[448,896]{1,0:T(8,128)(2,1)}, bf16[448,896]{1,0:T(8,128)(2,1)S(1)}, u32[]{:S(2)}, u32[]{:S(2)}) collective-permute-start(bf16[448,896]{1,0:T(8,128)(2,1)} %shard_map.129.refs_0_), channel_id=1, source_target_pairs={{0,4},{2,6},{4,0},{6,2},{1,5},{3,7},{5,1},{7,3},{8,12},{10,14},{12... | collective-permute-start | bytes 2408456 | tf_op jit(solution)/shard_map/ppermute | solution.py:50
  117.2 54.3 %collective-permute-start.3 = (bf16[128,2048]{1,0:T(8,128)(2,1)}, bf16[128,2048]{1,0:T(8,128)(2,1)S(1)}, u32[]{:S(2)}, u32[]{:S(2)}) collective-permute-start(bf16[128,2048]{1,0:T(8,128)(2,1)} %bitcast.21), channel_id=1, source_target_pairs={{0,6},{2,0},{4,2},{6,4},{1,7},{3,1},{5,3},{7,5},{8,14},{10,8},{12,... | collective-permute-start | bytes 1572872 | tf_op jit(solution)/shard_map/ppermute | solution.py:48
  119.9 61.4 %collective-permute-start.18 = (bf16[448,896]{1,0:T(8,128)(2,1)}, bf16[448,896]{1,0:T(8,128)(2,1)}, u32[]{:S(2)}, u32[]{:S(2)}) collective-permute-start(bf16[448,896]{1,0:T(8,128)(2,1)} %shard_map.129.refs_0_), channel_id=1, source_target_pairs={{0,2},{2,4},{4,6},{6,0},{1,3},{3,5},{5,7},{7,1},{8,10},{10,12},{12... | collective-permute-start | bytes 2408456 | tf_op jit(solution)/shard_map/ppermute | solution.py:49
  122.5 56.8 %collective-permute-start.4 = (bf16[128,2048]{1,0:T(8,128)(2,1)}, bf16[128,2048]{1,0:T(8,128)(2,1)}, u32[]{:S(2)}, u32[]{:S(2)}) collective-permute-start(bf16[128,2048]{1,0:T(8,128)(2,1)} %bitcast.22), channel_id=1, source_target_pairs={{0,4},{2,6},{4,0},{6,2},{1,5},{3,7},{5,1},{7,3},{8,12},{10,14},{12... | collective-permute-start | bytes 1572872 | tf_op jit(solution)/shard_map/ppermute | solution.py:50
  171.5 5.4 %copy-start.10 = (bf16[128,2048]{1,0:T(8,128)(2,1)}, bf16[128,2048]{1,0:T(8,128)(2,1)S(1)}, u32[]{:S(2)}) copy-start(bf16[128,2048]{1,0:T(8,128)(2,1)S(1)} %collective-permute-done.3.refs_5_) | copy-start | bytes 1572868
  171.5 28.1 %collective-permute-start.19 = (bf16[448,896]{1,0:T(8,128)(2,1)}, bf16[448,896]{1,0:T(8,128)(2,1)}, u32[]{:S(2)}, u32[]{:S(2)}) collective-permute-start(bf16[448,896]{1,0:T(8,128)(2,1)} %shard_map.129.refs_0_), channel_id=1, source_target_pairs={{0,1},{1,0},{2,3},{3,2},{4,5},{5,4},{6,7},{7,6},{8,9},{9,8},{10,11... | collective-permute-start | bytes 2408456 | tf_op jit(solution)/shard_map/ppermute | solution.py:52
  174.9 39.6 %copy-start.4 = (bf16[448,896]{1,0:T(8,128)(2,1)}, bf16[448,896]{1,0:T(8,128)(2,1)S(1)}, u32[]{:S(2)}) copy-start(bf16[448,896]{1,0:T(8,128)(2,1)S(1)} %collective-permute-done.16.refs_1_) | copy-start | bytes 2408452
  175.0 26.6 %collective-permute-start.20 = (bf16[448,896]{1,0:T(8,128)(2,1)S(1)}, bf16[448,896]{1,0:T(8,128)(2,1)}, u32[]{:S(2)}, u32[]{:S(2)}) collective-permute-start(bf16[448,896]{1,0:T(8,128)(2,1)S(1)} %collective-permute-done.16.refs_1_), channel_id=1, source_target_pairs={{0,1},{1,0},{2,3},{3,2},{4,5},{5,4},{6,7},{7,6},{8,9},{9,8},{10,11... | collective-permute-start | bytes 2408456 | tf_op jit(solution)/shard_map/ppermute | solution.py:52
  176.9 37.6 %copy-start.5 = (bf16[448,896]{1,0:T(8,128)(2,1)}, bf16[448,896]{1,0:T(8,128)(2,1)S(1)}, u32[]{:S(2)}) copy-start(bf16[448,896]{1,0:T(8,128)(2,1)S(1)} %collective-permute-done.17.refs_2_) | copy-start | bytes 2408452
  176.9 27.1 %collective-permute-start.21 = (bf16[448,896]{1,0:T(8,128)(2,1)S(1)}, bf16[448,896]{1,0:T(8,128)(2,1)}, u32[]{:S(2)}, u32[]{:S(2)}) collective-permute-start(bf16[448,896]{1,0:T(8,128)(2,1)S(1)} %collective-permute-done.17.refs_2_), channel_id=1, source_target_pairs={{0,1},{1,0},{2,3},{3,2},{4,5},{5,4},{6,7},{7,6},{8,9},{9,8},{10,11... | collective-permute-start | bytes 2408456 | tf_op jit(solution)/shard_map/ppermute | solution.py:52
  179.3 17.8 %collective-permute-start.5 = (bf16[128,2048]{1,0:T(8,128)(2,1)}, bf16[128,2048]{1,0:T(8,128)(2,1)}, u32[]{:S(2)}, u32[]{:S(2)}) collective-permute-start(bf16[128,2048]{1,0:T(8,128)(2,1)} %bitcast.23), channel_id=1, source_target_pairs={{0,2},{2,4},{4,6},{6,0},{1,3},{3,5},{5,7},{7,1},{8,10},{10,12},{12... | collective-permute-start | bytes 1572872 | tf_op jit(solution)/shard_map/ppermute | solution.py:49
  181.3 31.3 %collective-permute-start.22 = (bf16[448,896]{1,0:T(8,128)(2,1)}, bf16[448,896]{1,0:T(8,128)(2,1)}, u32[]{:S(2)}, u32[]{:S(2)}) collective-permute-start(bf16[448,896]{1,0:T(8,128)(2,1)} %collective-permute-done.18.refs_3_), channel_id=1, source_target_pairs={{0,1},{1,0},{2,3},{3,2},{4,5},{5,4},{6,7},{7,6},{8,9},{9,8},{10,11... | collective-permute-start | bytes 2408456 | tf_op jit(solution)/shard_map/ppermute | solution.py:52
  197.1 26.2 %collective-permute-start.6 = (bf16[128,2048]{1,0:T(8,128)(2,1)}, bf16[128,2048]{1,0:T(8,128)(2,1)}, u32[]{:S(2)}, u32[]{:S(2)}) collective-permute-start(bf16[128,2048]{1,0:T(8,128)(2,1)} %bitcast.24), channel_id=1, source_target_pairs={{0,1},{1,0},{2,3},{3,2},{4,5},{5,4},{6,7},{7,6},{8,9},{9,8},{10,11... | collective-permute-start | bytes 1572872 | tf_op jit(solution)/shard_map/ppermute | solution.py:52
  199.7 27.0 %collective-permute-start.7 = (bf16[128,2048]{1,0:T(8,128)(2,1)}, bf16[128,2048]{1,0:T(8,128)(2,1)}, u32[]{:S(2)}, u32[]{:S(2)}) collective-permute-start(bf16[128,2048]{1,0:T(8,128)(2,1)} %copy-done.10), channel_id=1, source_target_pairs={{0,1},{1,0},{2,3},{3,2},{4,5},{5,4},{6,7},{7,6},{8,9},{9,8},{10,11... | collective-permute-start | bytes 1572872 | tf_op jit(solution)/shard_map/ppermute | solution.py:52
  201.6 27.0 %collective-permute-start.8 = (bf16[128,2048]{1,0:T(8,128)(2,1)}, bf16[128,2048]{1,0:T(8,128)(2,1)}, u32[]{:S(2)}, u32[]{:S(2)}) collective-permute-start(bf16[128,2048]{1,0:T(8,128)(2,1)} %collective-permute-done.4.refs_6_), channel_id=1, source_target_pairs={{0,1},{1,0},{2,3},{3,2},{4,5},{5,4},{6,7},{7,6},{8,9},{9,8},{10,11... | collective-permute-start | bytes 1572872 | tf_op jit(solution)/shard_map/ppermute | solution.py:52
  204.0 27.1 %collective-permute-start.9 = (bf16[128,2048]{1,0:T(8,128)(2,1)}, bf16[128,2048]{1,0:T(8,128)(2,1)}, u32[]{:S(2)}, u32[]{:S(2)}) collective-permute-start(bf16[128,2048]{1,0:T(8,128)(2,1)} %collective-permute-done.5.refs_7_), channel_id=1, source_target_pairs={{0,1},{1,0},{2,3},{3,2},{4,5},{5,4},{6,7},{7,6},{8,9},{9,8},{10,11... | collective-permute-start | bytes 1572872 | tf_op jit(solution)/shard_map/ppermute | solution.py:52
  212.6 21.6 %collective-permute-start = (bf16[16,32,512]{2,1,0:T(8,128)(2,1)S(1)}, bf16[16,32,512]{2,1,0:T(8,128)(2,1)}, u32[]{:S(2)}, u32[]{:S(2)}) collective-permute-start(bf16[16,32,512]{2,1,0:T(8,128)(2,1)S(1)} %all-to-all-done.refs_0_), channel_id=1, source_target_pairs={{0,24},{8,0},{16,8},{24,16},{1,25},{9,1},{17,9},{25,17},{2,26},{10... | collective-permute-start | bytes 1572872 | tf_op jit(solution)/shard_map/ppermute | solution.py:58
  214.5 1.0 copy-start.1
  223.3 29.0 %collective-permute-start.23 = (bf16[320,896]{1,0:T(8,128)(2,1)}, bf16[320,896]{1,0:T(8,128)(2,1)}, u32[]{:S(2)}, u32[]{:S(2)}) collective-permute-start(bf16[320,896]{1,0:T(8,128)(2,1)} %shard_map.130.refs_0_), channel_id=1, source_target_pairs={{0,6},{2,0},{4,2},{6,4},{1,7},{3,1},{5,3},{7,5},{8,14},{10,8},{12,... | collective-permute-start | bytes 1720328 | tf_op jit(solution)/shard_map/ppermute | solution.py:48
  226.7 27.6 %collective-permute-start.24 = (bf16[320,896]{1,0:T(8,128)(2,1)}, bf16[320,896]{1,0:T(8,128)(2,1)}, u32[]{:S(2)}, u32[]{:S(2)}) collective-permute-start(bf16[320,896]{1,0:T(8,128)(2,1)} %shard_map.130.refs_0_), channel_id=1, source_target_pairs={{0,4},{2,6},{4,0},{6,2},{1,5},{3,7},{5,1},{7,3},{8,12},{10,14},{12... | collective-permute-start | bytes 1720328 | tf_op jit(solution)/shard_map/ppermute | solution.py:50
  228.6 29.0 %collective-permute-start.25 = (bf16[320,896]{1,0:T(8,128)(2,1)}, bf16[320,896]{1,0:T(8,128)(2,1)}, u32[]{:S(2)}, u32[]{:S(2)}) collective-permute-start(bf16[320,896]{1,0:T(8,128)(2,1)} %shard_map.130.refs_0_), channel_id=1, source_target_pairs={{0,2},{2,4},{4,6},{6,0},{1,3},{3,5},{5,7},{7,1},{8,10},{10,12},{12... | collective-permute-start | bytes 1720328 | tf_op jit(solution)/shard_map/ppermute | solution.py:49
  231.1 15.9 %collective-permute-start.1 = (bf16[16,32,512]{2,1,0:T(8,128)(2,1)S(1)}, bf16[16,32,512]{2,1,0:T(8,128)(2,1)S(1)}, u32[]{:S(2)}, u32[]{:S(2)}) collective-permute-start(bf16[16,32,512]{2,1,0:T(8,128)(2,1)S(1)} %all-to-all-done.refs_0_), channel_id=1, source_target_pairs={{0,16},{8,24},{16,0},{24,8},{1,17},{9,25},{17,1},{25,9},{2,18},{10... | collective-permute-start | bytes 1572872 | tf_op jit(solution)/shard_map/ppermute | solution.py:58
  234.2 27.2 %collective-permute-start.2 = (bf16[16,32,512]{2,1,0:T(8,128)(2,1)S(1)}, bf16[16,32,512]{2,1,0:T(8,128)(2,1)S(1)}, u32[]{:S(2)}, u32[]{:S(2)}) collective-permute-start(bf16[16,32,512]{2,1,0:T(8,128)(2,1)S(1)} %all-to-all-done.refs_0_), channel_id=1, source_target_pairs={{0,8},{8,16},{16,24},{24,0},{1,9},{9,17},{17,25},{25,1},{2,10},{10... | collective-permute-start | bytes 1572872 | tf_op jit(solution)/shard_map/ppermute | solution.py:58
  247.0 15.1 %copy-start.11 = (bf16[16,32,512]{2,1,0:T(8,128)(2,1)}, bf16[16,32,512]{2,1,0:T(8,128)(2,1)S(1)}, u32[]{:S(2)}) copy-start(bf16[16,32,512]{2,1,0:T(8,128)(2,1)S(1)} %collective-permute-done.1.refs_2_) | copy-start | bytes 1572868
  247.0 29.9 %collective-permute-start.26 = (bf16[320,896]{1,0:T(8,128)(2,1)}, bf16[320,896]{1,0:T(8,128)(2,1)S(1)}, u32[]{:S(2)}, u32[]{:S(2)}) collective-permute-start(bf16[320,896]{1,0:T(8,128)(2,1)} %shard_map.130.refs_0_), channel_id=1, source_target_pairs={{0,1},{1,0},{2,3},{3,2},{4,5},{5,4},{6,7},{7,6},{8,9},{9,8},{10,11... | collective-permute-start | bytes 1720328 | tf_op jit(solution)/shard_map/ppermute | solution.py:52
  252.3 24.6 %collective-permute-start.27 = (bf16[320,896]{1,0:T(8,128)(2,1)}, bf16[320,896]{1,0:T(8,128)(2,1)S(1)}, u32[]{:S(2)}, u32[]{:S(2)}) collective-permute-start(bf16[320,896]{1,0:T(8,128)(2,1)} %collective-permute-done.23.refs_1_), channel_id=1, source_target_pairs={{0,1},{1,0},{2,3},{3,2},{4,5},{5,4},{6,7},{7,6},{8,9},{9,8},{10,11... | collective-permute-start | bytes 1720328 | tf_op jit(solution)/shard_map/ppermute | solution.py:52
  254.3 22.7 %collective-permute-start.28 = (bf16[320,896]{1,0:T(8,128)(2,1)}, bf16[320,896]{1,0:T(8,128)(2,1)S(1)}, u32[]{:S(2)}, u32[]{:S(2)}) collective-permute-start(bf16[320,896]{1,0:T(8,128)(2,1)} %collective-permute-done.24.refs_2_), channel_id=1, source_target_pairs={{0,1},{1,0},{2,3},{3,2},{4,5},{5,4},{6,7},{7,6},{8,9},{9,8},{10,11... | collective-permute-start | bytes 1720328 | tf_op jit(solution)/shard_map/ppermute | solution.py:52
  257.6 19.4 %collective-permute-start.29 = (bf16[320,896]{1,0:T(8,128)(2,1)}, bf16[320,896]{1,0:T(8,128)(2,1)S(1)}, u32[]{:S(2)}, u32[]{:S(2)}) collective-permute-start(bf16[320,896]{1,0:T(8,128)(2,1)} %collective-permute-done.25.refs_3_), channel_id=1, source_target_pairs={{0,1},{1,0},{2,3},{3,2},{4,5},{5,4},{6,7},{7,6},{8,9},{9,8},{10,11... | collective-permute-start | bytes 1720328 | tf_op jit(solution)/shard_map/ppermute | solution.py:52
  261.3 0.8 copy-start.12
  276.9 0.8 copy-start.6
  276.9 1.0 copy-start.7
  277.0 1.2 copy-start.8
  278.1 0.8 copy-start.9
  288.0 32.4 %copy-start.18 = (bf16[32,256]{1,0:T(8,128)(2,1)S(1)}, bf16[32,256]{1,0:T(8,128)(2,1)}, u32[]{:S(2)}) copy-start(bf16[32,256]{1,0:T(8,128)(2,1)} %param.22) | copy-start | bytes 49156
  317.0 50.1 %copy-start = (bf16[4,1024,256]{2,1,0:T(8,128)(2,1)}, bf16[4,1024,256]{2,1,0:T(8,128)(2,1)S(1)}, u32[]{:S(2)}) copy-start(bf16[4,1024,256]{2,1,0:T(8,128)(2,1)S(1)} %all_to_all.25.side) | copy-start | bytes 6291460
  317.0 54.4 %collective-permute-start.30 = (bf16[4,1024,256]{2,1,0:T(8,128)(2,1)S(1)}, bf16[4,1024,256]{2,1,0:T(8,128)(2,1)}, u32[]{:S(2)}, u32[]{:S(2)}) collective-permute-start(bf16[4,1024,256]{2,1,0:T(8,128)(2,1)S(1)} %all_to_all.25.side), channel_id=1, source_target_pairs={{0,1},{1,0},{2,3},{3,2},{4,5},{5,4},{6,7},{7,6},{8,9},{9,8},{10,11... | collective-permute-start | bytes 6291464 | tf_op jit(solution)/shard_map/ppermute | solution.py:82
  345.9 18.2 %copy-start.3 = (bf16[16,16,512]{2,1,0:T(8,128)(2,1)}, bf16[16,16,512]{2,1,0:T(8,128)(2,1)S(1)}, u32[]{:S(2)}) copy-start(bf16[16,16,512]{2,1,0:T(8,128)(2,1)S(1)} %all_to_all.26.refs_0_) | copy-start | bytes 786436
  345.9 9.7 %collective-permute-start.10 = (bf16[16,16,512]{2,1,0:T(8,128)(2,1)S(1)}, bf16[16,16,512]{2,1,0:T(8,128)(2,1)S(1)}, u32[]{:S(2)}, u32[]{:S(2)}) collective-permute-start(bf16[16,16,512]{2,1,0:T(8,128)(2,1)S(1)} %all_to_all.26.refs_0_), channel_id=1, source_target_pairs={{0,24},{8,0},{16,8},{24,16},{1,25},{9,1},{17,9},{25,17},{2,26},{10... | collective-permute-start | bytes 786440 | tf_op jit(solution)/shard_map/ppermute | solution.py:58
  348.4 8.6 %collective-permute-start.11 = (bf16[16,16,512]{2,1,0:T(8,128)(2,1)S(1)}, bf16[16,16,512]{2,1,0:T(8,128)(2,1)S(1)}, u32[]{:S(2)}, u32[]{:S(2)}) collective-permute-start(bf16[16,16,512]{2,1,0:T(8,128)(2,1)S(1)} %all_to_all.26.refs_0_), channel_id=1, source_target_pairs={{0,16},{8,24},{16,0},{24,8},{1,17},{9,25},{17,1},{25,9},{2,18},{10... | collective-permute-start | bytes 786440 | tf_op jit(solution)/shard_map/ppermute | solution.py:58
  353.0 11.1 %collective-permute-start.12 = (bf16[16,16,512]{2,1,0:T(8,128)(2,1)S(1)}, bf16[16,16,512]{2,1,0:T(8,128)(2,1)S(1)}, u32[]{:S(2)}, u32[]{:S(2)}) collective-permute-start(bf16[16,16,512]{2,1,0:T(8,128)(2,1)S(1)} %all_to_all.26.refs_0_), channel_id=1, source_target_pairs={{0,8},{8,16},{16,24},{24,0},{1,9},{9,17},{17,25},{25,1},{2,10},{10... | collective-permute-start | bytes 786440 | tf_op jit(solution)/shard_map/ppermute | solution.py:58
  355.6 8.5 %copy-start.14 = (bf16[16,16,512]{2,1,0:T(8,128)(2,1)}, bf16[16,16,512]{2,1,0:T(8,128)(2,1)S(1)}, u32[]{:S(2)}) copy-start(bf16[16,16,512]{2,1,0:T(8,128)(2,1)S(1)} %collective-permute-done.10.refs_1_) | copy-start | bytes 786436
  357.1 7.1 %copy-start.15 = (bf16[16,16,512]{2,1,0:T(8,128)(2,1)}, bf16[16,16,512]{2,1,0:T(8,128)(2,1)S(1)}, u32[]{:S(2)}) copy-start(bf16[16,16,512]{2,1,0:T(8,128)(2,1)S(1)} %collective-permute-done.11.refs_2_) | copy-start | bytes 786436
  364.1 0.7 copy-start.16
